TPU v7x, 32 devices: a whole 2x2x4 slice. The times are simulated.
32 devices in a mesh: cells: 16 (over z, x, core), src: 2 (over y).
Axes of the slice: x: 2, y: 2, z: 4, core: 2. Of those that a mesh axis runs over, the one named last changes fastest.
Arguments:
- conductivity: float32 [64, 1024], P('cells'), may hold values from 0.2 to 5
- prev_fields: bfloat16 [1024, 64, 1024], P('src', 'cells'), may hold values from -6 to 6
- electrodes: int32 [1024, 2], P('src'), may hold values from 0 to 65535, as said below
- data_weight: bfloat16 [1024, 1024], replicated, may hold values from -3 to 4
Outputs:
- potentials: bfloat16 [1024, 64, 1024], P('src', 'cells')
- gradient: float32 [64, 1024], P('cells', 'src')
Inputs may be any that keep to these rules, and one draw needn't show every extreme that they name: `electrodes`: in each row the two cells differ.
All inputs are finite; a program needn't handle non-finite values.
Results may differ from a plain program's by a relative error of at most 0.0034.
Values may be sent and summed in bfloat16 or wider, within the bound.
No kernel may reach another device: no remote copies, remote signals or barrier semaphores. Data moves between devices by JAX's collectives and lax.ppermute only.
A program may use at most 128 MiB of HBM per device.

v0:
```python
import functools

import jax
import jax.numpy as jnp
from jax import lax
from jax.experimental import pallas as pl
from jax.experimental.pallas import tpu as pltpu
from jax.sharding import PartitionSpec as P


NY = 32
current = 4.0
LANES = 128
GROUP = 16
ROWS = 32
UNIT = 128
LOW = 2
HIGH = 3


def neighbours(axis, step):
    count = lax.axis_size(axis)
    return [(i, i + step) for i in range(count) if 0 <= i + step < count]


def shift_last(values, offset):
    if offset > 0:
        padding = jnp.zeros(values.shape[:-1] + (offset,), values.dtype)
        return jnp.concatenate([values[..., offset:], padding], axis=-1)
    padding = jnp.zeros(values.shape[:-1] + (-offset,), values.dtype)
    return jnp.concatenate([padding, values[..., :offset]], axis=-1)


def split(values):
    parts = []
    for _ in range(3):
        parts.append(lax.reduce_precision(values, 8, 7))
        values = values - parts[-1]
    rows = jnp.stack(parts, axis=1).astype(jnp.bfloat16)
    return jnp.pad(rows, ((0, 0), (0, GROUP - 3), (0, 0)))


def joined(rows):
    rows = rows[:, :3].astype(jnp.float32)
    return (rows[:, 2] + rows[:, 1]) + rows[:, 0]


def stencil_coefficients(conductivity, low, high, first_plane, planes_total):
    _, cells = conductivity.shape
    padded = jnp.concatenate([low, conductivity, high], axis=0)
    sigma = padded[1:-1]
    column = jnp.arange(cells, dtype=jnp.int32)
    upper = (column % NY != NY - 1).astype(jnp.float32)
    lower = (column % NY != 0).astype(jnp.float32)
    plane = first_plane - 1 + jnp.arange(sigma.shape[0], dtype=jnp.int32)
    inside = ((plane >= 0) & (plane < planes_total))[:, None]
    z_plus = 0.5 * (sigma + padded[2:])
    z_minus = 0.5 * (sigma + padded[:-2])
    y_plus = 0.5 * (sigma + shift_last(sigma, 1) * upper)
    y_minus = 0.5 * (sigma + shift_last(sigma, -1) * lower)
    x_plus = 0.5 * (sigma + shift_last(sigma, NY))
    x_minus = 0.5 * (sigma + shift_last(sigma, -NY))
    diagonal = z_plus + z_minus + y_plus + y_minus + x_plus + x_minus
    scale = jnp.where(inside, 2.0 / jnp.where(inside, diagonal, 1.0), 0.0)
    rows = [
        z_plus * scale,
        z_minus * scale,
        y_plus * scale * upper,
        y_minus * scale * lower,
        x_plus * scale * (column < cells - NY),
        x_minus * scale * (column >= NY),
        current * scale,
        -current * scale,
    ]
    return jnp.stack(rows, axis=1)


def lane_index(shape):
    return lax.broadcasted_iota(jnp.int32, shape, 1)


def sweep_kernel(depth, count, band, place_ref, own_ref, low_ref, high_ref, coef_ref, elec_ref, *refs):
    refs = refs[-(count + 6) :]
    pot_ref, outs, (first, second, extra, final) = refs[0], refs[1 : count + 1], refs[count + 1 : count + 5]
    elec_b = refs[count + 5]
    rows, _, cells = own_ref.shape
    tiles = cells // LANES
    first[0:LOW] = low_ref[...]
    first[LOW : LOW + depth] = jnp.swapaxes(own_ref[...].astype(jnp.float32), 0, 1).astype(jnp.bfloat16)
    first[LOW + depth :] = high_ref[...]
    elec_b[0] = jnp.broadcast_to(elec_ref[:, 0:1], (rows, LANES))
    elec_b[1] = jnp.broadcast_to(elec_ref[:, 1:2], (rows, LANES))
    lane = lane_index((GROUP, LANES))
    left = lane < LANES - NY
    right = lane >= NY
    groups = rows // GROUP

    def spread(row):
        return jnp.broadcast_to(row, (GROUP, LANES))

    def stencil(source, plane, coef_plane, at):
        centre = [source[plane, at, pl.ds(v * LANES, LANES)].astype(jnp.float32) for v in range(tiles)]
        ahead = [pltpu.roll(c, LANES - NY, 1) for c in centre]
        behind = [pltpu.roll(c, NY, 1) for c in centre]

        def tile(v):
            lanes = pl.ds(v * LANES, LANES)

            def coef(kind):
                return spread(coef_ref[coef_plane, kind : kind + 1, lanes])

            x_plus = ahead[v] if v == tiles - 1 else jnp.where(left, ahead[v], ahead[v + 1])
            x_minus = behind[v] if v == 0 else jnp.where(right, behind[v], behind[v - 1])
            total = centre[v] + coef(0) * source[plane + 1, at, lanes].astype(jnp.float32)
            side = coef(1) * source[plane - 1, at, lanes].astype(jnp.float32)
            total = total + coef(2) * pltpu.roll(centre[v], LANES - 1, 1)
            side = side + coef(3) * pltpu.roll(centre[v], 1, 1)
            total = total + coef(4) * x_plus
            side = side + coef(5) * x_minus
            return total + side

        return tile

    def relax_first(plane, at):
        sums = stencil(first, plane + 1, plane, at)
        base = place_ref[1] + (plane - 1) * cells
        plus = elec_b[0, at, :] - base
        minus = elec_b[1, at, :] - base

        def tile(v):
            lanes = pl.ds(v * LANES, LANES)
            strength = spread(coef_ref[plane, 6:7, lanes])
            negative = spread(coef_ref[plane, 7:8, lanes])
            here = lane + v * LANES
            added = jnp.where(plus == here, strength, jnp.where(minus == here, negative, 0.0))
            extra[plane, at, lanes] = added
            second[plane, at, lanes] = sums(v) + added

        return tile

    def relax_second(plane, at):
        sums = stencil(second, plane + 1, plane + 1, at)

        def tile(v):
            lanes = pl.ds(v * LANES, LANES)
            value = sums(v) * (1.0 / 9.0) + extra[plane + 1, at, lanes] * (1.0 / 3.0)
            final[plane, at, lanes] = value.astype(jnp.bfloat16)

        return tile

    spans = [pl.ds(group * GROUP, GROUP) for group in range(groups)]

    def run(makers):
        works = [make() for make in makers]
        for v in range(tiles):
            for work in works:
                work(v)

    def only_first(plane, carry):
        for at in spans:
            run([lambda: relax_first(plane, at)])
        return carry

    def both(plane, carry):
        for at in spans:
            run([lambda: relax_second(plane - 3, at), lambda: relax_first(plane, at)])
        return carry

    lax.fori_loop(0, 3, only_first, 0)
    lax.fori_loop(3, depth + HIGH, both, 0)
    for plane in range(depth + HIGH - 3, depth + 1):
        for at in spans:
            run([lambda: relax_second(plane, at)])
    pot_ref[...] = jnp.swapaxes(final[0:depth].astype(jnp.float32), 0, 1).astype(jnp.bfloat16)

    wide = lane_index((rows, LANES))
    for r in range(count):
        out = outs[r]
        target = lax.rem(place_ref[0] + r, count)
        start = pl.multiple_of(target * band, LANES)
        for plane in range(depth + 1):
            out[:, plane * band : (plane + 1) * band] = final[plane, :, pl.ds(start, band)]
        after = jnp.minimum(target + 1, count - 1)
        after_start = pl.multiple_of(after * band, LANES)
        kept = (target < count - 1).astype(jnp.float32)
        for piece in range(beside_width(depth) // LANES):
            packed = jnp.zeros((rows, LANES), jnp.float32)
            for slot in range(LANES // NY):
                plane = piece * (LANES // NY) + slot
                if plane < depth:
                    row = final[plane, :, pl.ds(after_start, LANES)].astype(jnp.float32)
                    row = pltpu.roll(row, slot * NY, 1) if slot else row
                    mine = (wide >= slot * NY) & (wide < (slot + 1) * NY)
                    packed = jnp.where(mine, row, packed)
            begin = (depth + 1) * band + piece * LANES
            out[:, begin : begin + LANES] = (packed * kept).astype(jnp.bfloat16)


def beside_width(depth):
    return -(-depth * NY // LANES) * LANES


def sweep(place, own, low, high, coefs, electrodes, before, begin, size, count, band):
    _, depth, cells = own.shape
    width = (depth + 1) * band + beside_width(depth)
    block = begin // ROWS
    in_specs = [
        pl.BlockSpec((ROWS, depth, cells), lambda i, place: (i + block, 0, 0)),
        pl.BlockSpec((LOW, ROWS, cells), lambda i, place: (0, i, 0)),
        pl.BlockSpec((HIGH, ROWS, cells), lambda i, place: (0, i, 0)),
        pl.BlockSpec(coefs.shape, lambda i, place: (0, 0, 0)),
        pl.BlockSpec((ROWS, 2), lambda i, place: (i + block, 0)),
    ]
    args = [place, own, low, high, coefs, electrodes]
    aliases = {}
    if before is not None:
        in_specs.append(pl.BlockSpec(memory_space=pl.ANY))
        args.append(before)
        aliases = {6: 0}
    planes = depth + HIGH
    flops = size * cells * planes * 40
    return pl.pallas_call(
        functools.partial(sweep_kernel, depth, count, band),
        grid_spec=pltpu.PrefetchScalarGridSpec(
            num_scalar_prefetch=1,
            grid=(size // ROWS,),
            in_specs=in_specs,
            out_specs=[pl.BlockSpec((ROWS, depth, cells), lambda i, place: (i + block, 0, 0))]
            + [pl.BlockSpec((ROWS, width), lambda i, place: (i, 0))] * count,
            scratch_shapes=[
                pltpu.VMEM((LOW + depth + HIGH, ROWS, cells), jnp.bfloat16),
                pltpu.VMEM((planes, ROWS, cells), jnp.float32),
                pltpu.VMEM((planes, ROWS, cells), jnp.float32),
                pltpu.VMEM((depth + 1, ROWS, cells), jnp.bfloat16),
                pltpu.VMEM((2, ROWS, LANES), jnp.int32),
            ],
        ),
        out_shape=[jax.ShapeDtypeStruct(own.shape, jnp.bfloat16)]
        + [jax.ShapeDtypeStruct((size, width), jnp.bfloat16)] * count,
        input_output_aliases=aliases,
        compiler_params=pltpu.CompilerParams(vmem_limit_bytes=24 * 2**20),
        cost_estimate=pl.CostEstimate(
            flops=flops, bytes_accessed=size * cells * 2 * (3 * depth + LOW + HIGH), transcendentals=0
        ),
        name="sweep",
    )(*args)


def fold_kernel(count, per, place_ref, weight_ref, out_ref):
    total = count * per

    def where_is(block):
        holder = lax.rem(place_ref[0] + count - lax.rem(block, count), count)
        return pl.multiple_of((holder * per + lax.div(block, count)) * UNIT, UNIT)

    for q in range(total):
        here = where_is(q)
        chunk = q // count
        rows = pl.ds(q * UNIT, UNIT)

        def folded(other, carry):
            there = where_is(other)
            straight = weight_ref[pl.ds(here, UNIT), pl.ds(there, UNIT)].astype(jnp.float32)
            turned = weight_ref[pl.ds(there, UNIT), pl.ds(here, UNIT)].astype(jnp.float32)
            columns = pl.ds(pl.multiple_of(other * UNIT, UNIT), UNIT)
            out_ref[rows, columns] = (straight + turned.T).astype(jnp.bfloat16)
            return carry

        if chunk:
            lax.fori_loop(0, chunk * count, folded, 0)
        for other in range(chunk * count, (chunk + 1) * count):
            there = where_is(other)
            out_ref[rows, other * UNIT : (other + 1) * UNIT] = weight_ref[
                pl.ds(here, UNIT), pl.ds(there, UNIT)
            ]
        if chunk + 1 < per:
            out_ref[rows, (chunk + 1) * count * UNIT :] = jnp.zeros(
                (UNIT, (per - chunk - 1) * count * UNIT), jnp.bfloat16
            )


def fold(place, weight, count, per):
    return pl.pallas_call(
        functools.partial(fold_kernel, count, per),
        grid_spec=pltpu.PrefetchScalarGridSpec(
            num_scalar_prefetch=1,
            grid=(1,),
            in_specs=[pl.BlockSpec(weight.shape, lambda i, place: (0, 0))],
            out_specs=pl.BlockSpec(weight.shape, lambda i, place: (0, 0)),
        ),
        out_shape=jax.ShapeDtypeStruct(weight.shape, jnp.bfloat16),
        compiler_params=pltpu.CompilerParams(vmem_limit_bytes=24 * 2**20),
        cost_estimate=pl.CostEstimate(
            flops=weight.size, bytes_accessed=weight.size * 4, transcendentals=0
        ),
        name="fold",
    )(place, weight)


def weigh_kernel(depth, band, pieces, row_start, block_rows, chunk_rows, scale, weight_ref, *refs):
    piece_refs = refs[:pieces]
    before_ref, out_ref, held, mixed, partial, sems = refs[pieces:]
    step = pl.program_id(0)
    tiles = band // LANES

    @pl.when(step == 0)
    def _():
        at = 0
        copies = []
        for i, piece in enumerate(piece_refs):
            size = piece.shape[0]
            copies.append(pltpu.make_async_copy(piece, held.at[pl.ds(at, size)], sems.at[i]))
            copies[-1].start()
            at += size
        for copy in copies:
            copy.wait()
        partial[...] = before_ref[...]

    chunk = (row_start + step * block_rows) // chunk_rows
    for c in range(row_start // chunk_rows, held.shape[0] // chunk_rows):
        reach = (c + 1) * chunk_rows

        @pl.when(chunk == c)
        def _():
            mixed[...] = jnp.dot(
                weight_ref[:, :reach], held[:reach], preferred_element_type=jnp.float32
            )

    lane = lane_index((GROUP, LANES))
    left = lane < LANES - NY
    inner = jnp.where(lax.rem(lane, NY) != NY - 1, 1.0, 0.0)
    base = row_start + step * block_rows

    for plane in range(depth):
        beside_tile = (depth + 1) * band + (plane * NY // LANES) * LANES
        turn = (LANES - NY - plane * NY) % LANES

        def rows_of(group, totals):
            at = pl.ds(pl.multiple_of(group * GROUP, GROUP), GROUP)
            at_held = pl.ds(pl.multiple_of(base + group * GROUP, GROUP), GROUP)

            def read(column):
                lanes = pl.ds(column, LANES)
                return held[at_held, lanes].astype(jnp.float32), mixed[at, lanes]

            centre = [read(plane * band + t * LANES) for t in range(tiles)]
            above = [read((plane + 1) * band + t * LANES) for t in range(tiles)]
            ahead = [tuple(pltpu.roll(c, LANES - NY, 1) for c in pair) for pair in centre]
            ahead.append(tuple(pltpu.roll(c, turn, 1) if turn else c for c in read(beside_tile)))
            result = []
            for t in range(tiles):
                value, product = centre[t]
                total = (above[t][0] - value) * (above[t][1] - product)
                total = total + (jnp.where(left, ahead[t][0], ahead[t + 1][0]) - value) * (
                    jnp.where(left, ahead[t][1], ahead[t + 1][1]) - product
                )
                total = total + (pltpu.roll(value, LANES - 1, 1) * inner - value) * (
                    pltpu.roll(product, LANES - 1, 1) * inner - product
                )
                result.append(totals[t] + (total[:8] + total[8:]))
            return tuple(result)

        rows = pl.ds(plane * 8, 8)
        start = tuple(partial[rows, t * LANES : (t + 1) * LANES] for t in range(tiles))
        sums = lax.fori_loop(0, block_rows // GROUP, rows_of, start, unroll=4)
        for t in range(tiles):
            partial[rows, t * LANES : (t + 1) * LANES] = sums[t]

    @pl.when(step == pl.num_programs(0) - 1)
    def _():
        if scale is None:
            out_ref[...] = partial[...]
        else:
            for plane in range(depth):
                total = jnp.sum(partial[plane * 8 : plane * 8 + 8, :], axis=0, keepdims=True)
                out_ref[plane : plane + 1, :] = total * scale


def weigh(weight, pieces, before, row_start, rows, chunk_rows, depth, band, scale):
    width = pieces[0].shape[1]
    held = sum(piece.shape[0] for piece in pieces)
    block_rows = UNIT
    first = row_start // block_rows
    out = (depth, band) if scale is not None else (depth * 8, band)
    return pl.pallas_call(
        functools.partial(
            weigh_kernel, depth, band, len(pieces), row_start, block_rows, chunk_rows, scale
        ),
        grid=(rows // block_rows,),
        in_specs=[pl.BlockSpec((block_rows, weight.shape[1]), lambda i: (i + first, 0))]
        + [pl.BlockSpec(memory_space=pl.ANY)] * len(pieces)
        + [pl.BlockSpec((depth * 8, band), lambda i: (0, 0))],
        out_specs=pl.BlockSpec(out, lambda i: (0, 0)),
        out_shape=jax.ShapeDtypeStruct(out, jnp.float32),
        scratch_shapes=[
            pltpu.VMEM((held, width), jnp.bfloat16),
            pltpu.VMEM((block_rows, width), jnp.float32),
            pltpu.VMEM((depth * 8, band), jnp.float32),
            pltpu.SemaphoreType.DMA((len(pieces),)),
        ],
        compiler_params=pltpu.CompilerParams(vmem_limit_bytes=32 * 2**20),
        cost_estimate=pl.CostEstimate(
            flops=2 * rows * held * width, bytes_accessed=2 * held * width, transcendentals=0
        ),
        name="weigh",
    )(weight, *pieces, before)


def body(conductivity, prev_fields, electrodes, data_weight):
    local, depth, cells = prev_fields.shape
    count = lax.axis_size("src")
    band = cells // count
    sources = data_weight.shape[0]
    per = local // UNIT
    slab = lax.axis_index("cells")
    halos = []
    fields = prev_fields
    for k in range(per):
        chunk = fields[k * UNIT : (k + 1) * UNIT]
        up = jnp.swapaxes(chunk[:, depth - LOW :], 0, 1)
        down = jnp.swapaxes(chunk[:, :HIGH], 0, 1)
        if k == 0:
            up = jnp.concatenate([up, split(conductivity[depth - LOW :])], axis=1)
            down = jnp.concatenate([down, split(conductivity[:HIGH])], axis=1)
        fields, up, down = lax.optimization_barrier((fields, up, down))
        low = lax.ppermute(up, "cells", neighbours("cells", 1))
        high = lax.ppermute(down, "cells", neighbours("cells", -1))
        halos.append((low, high))
    low, high = (joined(halo[:, UNIT:]) for halo in halos[0])
    coefs = stencil_coefficients(conductivity, low, high, slab * depth, depth * lax.axis_size("cells"))
    place = jnp.stack([lax.axis_index("src"), slab * (depth * cells)]).astype(jnp.int32)
    weight = fold(place, data_weight, count, per)
    potentials = None
    pieces = []
    for k in range(per):
        low, high = halos[k]
        potentials, kept, *sent = sweep(
            place, prev_fields, low, high, coefs, electrodes, potentials, k * UNIT, UNIT, count, band
        )
        pieces.append(kept)
        for r in range(1, count):
            pairs = [(i, (i + r) % count) for i in range(count)]
            pieces.append(lax.ppermute(sent[r - 1], "src", pairs))
    partial = jnp.zeros((depth * 8, band), jnp.float32)
    done = 0
    for stop in sorted({max(per - 1, 1), per}):
        rows = (stop - done) * UNIT * count
        last = stop == per
        partial = weigh(
            weight,
            pieces[: stop * count],
            partial,
            done * UNIT * count,
            rows,
            UNIT * count,
            depth,
            band,
            1.0 / sources if last else None,
        )
        done = stop
    return (potentials, partial)


def solution(mesh):
    placed = (P("cells", None), P("src", "cells", None), P("src", None), P())
    return jax.shard_map(
        body,
        mesh=mesh,
        in_specs=placed,
        out_specs=(P("src", "cells", None), P("cells", "src")),
        check_vma=False,
    )
```

profile of v0, /device:TPU:1, one launch (start us, length us, event | category | flops | bytes accessed | tf_op | source)
XLA Modules:
  0.0 166.7 jit_solution(7626693430780590850)
XLA Ops:
  2.5 1.8 %slice_bitcast_fusion.6 = bf16[2,128,1024]{2,0,1:T(2,128)(2,1)S(1)} fusion(bf16[512,4,1024]{2,1,0:T(4,128)(2,1)} %own_ref.7), kind=kLoop, calls=%fused_computation.11 | loop fusion | bytes 1048576 | tf_op jit(solution)/shard_map/transpose | solution.py:420
  4.3 1.6 slice.96
  6.3 1.6 pad_maximum_fusion
  8.9 4.5 %collective-permute-start.2 = (bf16[2,144,1024]{2,0,1:T(2,128)(2,1)}, bf16[2,144,1024]{2,0,1:T(2,128)(2,1)S(1)}, u32[]{:S(2)}, u32[]{:S(2)}) collective-permute-start(bf16[2,144,1024]{2,0,1:T(2,128)(2,1)} %pad_maximum_fusion), channel_id=1, source_target_pairs={{0,2},{2,4},{4,6},{6,8},{8,10},{10,12},{12,14},{14,16},{16,18},{18... | collective-permute-start | bytes 1769480 | tf_op jit(solution)/shard_map/ppermute | solution.py:426
  13.4 1.4 copy.52
  16.6 1.4 copy.54
  23.0 1.9 %collective-permute-start.1 = (bf16[3,128,1024]{2,1,0:T(8,128)(2,1)}, bf16[3,128,1024]{2,1,0:T(8,128)(2,1)S(1)}, u32[]{:S(2)}, u32[]{:S(2)}) collective-permute-start(bf16[3,128,1024]{2,1,0:T(8,128)(2,1)} %slice_bitcast_fusion), channel_id=1, source_target_pairs={{2,0},{4,2},{6,4},{8,6},{10,8},{12,10},{14,12},{16,14},{18,16},{20... | collective-permute-start | bytes 2359304 | tf_op jit(solution)/shard_map/ppermute | solution.py:427
  24.9 1.9 %collective-permute-start.3 = (bf16[3,144,1024]{2,1,0:T(8,128)(2,1)}, bf16[3,144,1024]{2,1,0:T(8,128)(2,1)S(1)}, u32[]{:S(2)}, u32[]{:S(2)}) collective-permute-start(bf16[3,144,1024]{2,1,0:T(8,128)(2,1)} %fusion.1), channel_id=1, source_target_pairs={{2,0},{4,2},{6,4},{8,6},{10,8},{12,10},{14,12},{16,14},{18,16},{20... | collective-permute-start | bytes 2654216 | tf_op jit(solution)/shard_map/ppermute | solution.py:427
  26.8 3.6 %collective-permute-start.4 = (bf16[2,128,1024]{2,1,0:T(8,128)(2,1)}, bf16[2,128,1024]{2,1,0:T(8,128)(2,1)}, u32[]{:S(2)}, u32[]{:S(2)}) collective-permute-start(bf16[2,128,1024]{2,1,0:T(8,128)(2,1)} %slice_bitcast_fusion.4), channel_id=1, source_target_pairs={{0,2},{2,4},{4,6},{6,8},{8,10},{10,12},{12,14},{14,16},{16,18},{18... | collective-permute-start | bytes 1572872 | tf_op jit(solution)/shard_map/ppermute | solution.py:426
  30.5 1.9 %collective-permute-start.5 = (bf16[3,128,1024]{2,1,0:T(8,128)(2,1)}, bf16[3,128,1024]{2,1,0:T(8,128)(2,1)S(1)}, u32[]{:S(2)}, u32[]{:S(2)}) collective-permute-start(bf16[3,128,1024]{2,1,0:T(8,128)(2,1)} %slice_bitcast_fusion.1), channel_id=1, source_target_pairs={{2,0},{4,2},{6,4},{8,6},{10,8},{12,10},{14,12},{16,14},{18,16},{20... | collective-permute-start | bytes 2359304 | tf_op jit(solution)/shard_map/ppermute | solution.py:427
  33.5 3.6 %collective-permute-start.6 = (bf16[2,128,1024]{2,1,0:T(8,128)(2,1)}, bf16[2,128,1024]{2,1,0:T(8,128)(2,1)S(1)}, u32[]{:S(2)}, u32[]{:S(2)}) collective-permute-start(bf16[2,128,1024]{2,1,0:T(8,128)(2,1)} %slice_bitcast_fusion.5), channel_id=1, source_target_pairs={{0,2},{2,4},{4,6},{6,8},{8,10},{10,12},{12,14},{14,16},{16,18},{18... | collective-permute-start | bytes 1572872 | tf_op jit(solution)/shard_map/ppermute | solution.py:426
  39.1 6.9 %collective-permute-done.3.high_ref = bf16[3,144,1024]{2,1,0:T(8,128)(2,1)S(1)} collective-permute-done((bf16[3,144,1024]{2,1,0:T(8,128)(2,1)}, bf16[3,144,1024]{2,1,0:T(8,128)(2,1)S(1)}, u32[]{:S(2)}, u32[]{:S(2)}) %collective-permute-start.3) | collective-permute-done | bytes 884768 | tf_op jit(solution)/shard_map/ppermute | solution.py:427
  46.0 1.9 %collective-permute-start.7 = (bf16[3,128,1024]{2,1,0:T(8,128)(2,1)}, bf16[3,128,1024]{2,1,0:T(8,128)(2,1)}, u32[]{:S(2)}, u32[]{:S(2)}) collective-permute-start(bf16[3,128,1024]{2,1,0:T(8,128)(2,1)} %slice_bitcast_fusion.2), channel_id=1, source_target_pairs={{2,0},{4,2},{6,4},{8,6},{10,8},{12,10},{14,12},{16,14},{18,16},{20... | collective-permute-start | bytes 2359304 | tf_op jit(solution)/shard_map/ppermute | solution.py:427
  48.3 26.2 %collective-permute-done.6.low_ref = bf16[2,128,1024]{2,1,0:T(8,128)(2,1)S(1)} collective-permute-done((bf16[2,128,1024]{2,1,0:T(8,128)(2,1)}, bf16[2,128,1024]{2,1,0:T(8,128)(2,1)S(1)}, u32[]{:S(2)}, u32[]{:S(2)}) %collective-permute-start.6) | collective-permute-done | bytes 524320 | tf_op jit(solution)/shard_map/ppermute | solution.py:426
  74.4 4.5 %collective-permute-start = (bf16[2,128,1024]{2,1,0:T(8,128)(2,1)}, bf16[2,128,1024]{2,1,0:T(8,128)(2,1)}, u32[]{:S(2)}, u32[]{:S(2)}) collective-permute-start(bf16[2,128,1024]{2,1,0:T(8,128)(2,1)} %slice_bitcast_fusion.3), channel_id=1, source_target_pairs={{0,2},{2,4},{4,6},{6,8},{8,10},{10,12},{12,14},{14,16},{16,18},{18... | collective-permute-start | bytes 1572872 | tf_op jit(solution)/shard_map/ppermute | solution.py:426
  85.2 2.2 %copy-done.1 = bf16[512,4,1024]{2,1,0:T(4,128)(2,1)S(1)} copy-done((bf16[512,4,1024]{2,1,0:T(4,128)(2,1)S(1)}, bf16[512,4,1024]{2,1,0:T(4,128)(2,1)}, u32[]{:S(2)}) %copy-start.1) | copy-done | bytes 4194328
  87.4 10.6 %sweep.4 = (bf16[512,4,1024]{2,1,0:T(4,128)(2,1)}, bf16[128,2688]{1,0:T(8,128)(2,1)S(1)}, bf16[128,2688]{1,0:T(8,128)(2,1)S(1)}) custom-call(s32[2]{0:T(128)S(1)} %pad_add_fusion.place_ref, bf16[512,4,1024]{2,1,0:T(4,128)(2,1)S(1)} %copy-done.1, bf16[2,144,1024]{2,1,0:T(8,128)(2,1)S(1)} %copy.66.low_ref, ...), custom_call_target="tpu_custom_call" | custom-call | flops 36700160 | bytes 4456448 | tf_op jit(solution)/shard_map/sweep/pallas_call | solution.py:222
  99.3 11.5 %sweep.5 = (bf16[512,4,1024]{2,1,0:T(4,128)(2,1)}, bf16[128,2688]{1,0:T(8,128)(2,1)S(1)}, bf16[128,2688]{1,0:T(8,128)(2,1)S(1)}) custom-call(s32[2]{0:T(128)S(1)} %pad_add_fusion.place_ref, bf16[512,4,1024]{2,1,0:T(4,128)(2,1)S(1)} %copy-done.1, bf16[2,128,1024]{2,1,0:T(8,128)(2,1)S(1)} %copy-done.4, ...), custom_call_target="tpu_custom_call", output_to_operand_aliasing={{0}: (6, {})} | custom-call | flops 36700160 | bytes 4456448 | tf_op jit(solution)/shard_map/sweep/pallas_call | solution.py:222
  110.9 11.4 %sweep.6 = (bf16[512,4,1024]{2,1,0:T(4,128)(2,1)}, bf16[128,2688]{1,0:T(8,128)(2,1)S(1)}, bf16[128,2688]{1,0:T(8,128)(2,1)S(1)}) custom-call(s32[2]{0:T(128)S(1)} %pad_add_fusion.place_ref, bf16[512,4,1024]{2,1,0:T(4,128)(2,1)S(1)} %copy-done.1, bf16[2,128,1024]{2,1,0:T(8,128)(2,1)} %collective-permute-done.4.low_ref, ...), custom_call_target="tpu_custom_call", output_to_operand_aliasing={{0}: (6, {})} | custom-call | flops 36700160 | bytes 4456448 | tf_op jit(solution)/shard_map/sweep/pallas_call | solution.py:222
  123.6 11.4 %sweep.7 = (bf16[512,4,1024]{2,1,0:T(4,128)(2,1)}, bf16[128,2688]{1,0:T(8,128)(2,1)S(1)}, bf16[128,2688]{1,0:T(8,128)(2,1)S(1)}) custom-call(s32[2]{0:T(128)S(1)} %pad_add_fusion.place_ref, bf16[512,4,1024]{2,1,0:T(4,128)(2,1)S(1)} %copy-done.1, bf16[2,128,1024]{2,1,0:T(8,128)(2,1)} %collective-permute-done.low_ref, ...), custom_call_target="tpu_custom_call", output_to_operand_aliasing={{0}: (6, {})} | custom-call | flops 36700160 | bytes 4456448 | tf_op jit(solution)/shard_map/sweep/pallas_call | solution.py:222
  135.3 3.3 %fold.1.weight_ref = bf16[1024,1024]{1,0:T(8,128)(2,1)S(1)} custom-call(s32[2]{0:T(128)S(1)} %pad_add_fusion.place_ref, bf16[1024,1024]{1,0:T(8,128)(2,1)S(1)} %copy-done.2), custom_call_target="tpu_custom_call" | custom-call | flops 1048576 | bytes 4194304 | tf_op jit(solution)/shard_map/fold/pallas_call | solution.py:283
  138.6 6.4 %collective-permute-done.10.refs_5_ = bf16[128,2688]{1,0:T(8,128)(2,1)S(1)} collective-permute-done((bf16[128,2688]{1,0:T(8,128)(2,1)S(1)}, bf16[128,2688]{1,0:T(8,128)(2,1)S(1)}, u32[]{:S(2)}, u32[]{:S(2)}) %collective-permute-start.10) | collective-permute-done | bytes 688160 | tf_op jit(solution)/shard_map/ppermute | solution.py:443
  145.0 14.0 %weigh.2.refs_8_ = f32[32,512]{1,0:T(8,128)S(1)} custom-call(bf16[1024,1024]{1,0:T(8,128)(2,1)S(1)} %fold.1.weight_ref, bf16[128,2688]{1,0:T(8,128)(2,1)S(1)} %get-tuple-element.40.refs_0_, bf16[128,2688]{1,0:T(8,128)(2,1)S(1)} %collective-permute-done.8.refs_1_, bf16[128,2688]{1,0:T(8,128)(2,1)S(1)} %get-tuple-element.42.refs_2_, ...), custom_call_target="tpu_custom_call" | custom-call | flops 3170893824 | bytes 4128768 | tf_op jit(solution)/shard_map/weigh/pallas_call | solution.py:385
  159.0 7.6 %weigh.3 = f32[4,512]{1,0:T(4,128)} custom-call(bf16[1024,1024]{1,0:T(8,128)(2,1)S(1)} %fold.1.weight_ref, bf16[128,2688]{1,0:T(8,128)(2,1)S(1)} %get-tuple-element.40.refs_0_, bf16[128,2688]{1,0:T(8,128)(2,1)S(1)} %collective-permute-done.8.refs_1_, bf16[128,2688]{1,0:T(8,128)(2,1)S(1)} %get-tuple-element.42.refs_2_, ...), custom_call_target="tpu_custom_call" | custom-call | flops 1409286144 | bytes 5505024 | tf_op jit(solution)/shard_map/weigh/pallas_call | solution.py:385
  (68 shorter events, 22.6 us)
Async XLA Ops:
  0.6 12.7 %copy-start = (bf16[512,4,1024]{2,1,0:T(4,128)(2,1)S(1)}, bf16[512,4,1024]{2,1,0:T(4,128)(2,1)}, u32[]{:S(2)}) copy-start(bf16[512,4,1024]{2,1,0:T(4,128)(2,1)} %own_ref.7) | copy-start | bytes 12582916
  8.9 23.8 %collective-permute-start.2 = (bf16[2,144,1024]{2,0,1:T(2,128)(2,1)}, bf16[2,144,1024]{2,0,1:T(2,128)(2,1)S(1)}, u32[]{:S(2)}, u32[]{:S(2)}) collective-permute-start(bf16[2,144,1024]{2,0,1:T(2,128)(2,1)} %pad_maximum_fusion), channel_id=1, source_target_pairs={{0,2},{2,4},{4,6},{6,8},{8,10},{10,12},{12,14},{14,16},{16,18},{18... | collective-permute-start | bytes 1769480 | tf_op jit(solution)/shard_map/ppermute | solution.py:426
  19.8 12.6 %copy-start.7 = (s32[512,2]{0,1:T(2,128)S(1)}, s32[512,2]{0,1:T(2,128)}, u32[]{:S(2)}) copy-start(s32[512,2]{0,1:T(2,128)} %param.6) | copy-start | bytes 12292
  21.2 26.8 %copy-start.6 = (f32[4,1024]{1,0:T(4,128)S(1)}, f32[4,1024]{1,0:T(4,128)}, u32[]{:S(2)}) copy-start(f32[4,1024]{1,0:T(4,128)} %param.4) | copy-start | bytes 49156
  23.0 100.6 %collective-permute-start.1 = (bf16[3,128,1024]{2,1,0:T(8,128)(2,1)}, bf16[3,128,1024]{2,1,0:T(8,128)(2,1)S(1)}, u32[]{:S(2)}, u32[]{:S(2)}) collective-permute-start(bf16[3,128,1024]{2,1,0:T(8,128)(2,1)} %slice_bitcast_fusion), channel_id=1, source_target_pairs={{2,0},{4,2},{6,4},{8,6},{10,8},{12,10},{14,12},{16,14},{18,16},{20... | collective-permute-start | bytes 2359304 | tf_op jit(solution)/shard_map/ppermute | solution.py:427
  24.9 21.1 %collective-permute-start.3 = (bf16[3,144,1024]{2,1,0:T(8,128)(2,1)}, bf16[3,144,1024]{2,1,0:T(8,128)(2,1)S(1)}, u32[]{:S(2)}, u32[]{:S(2)}) collective-permute-start(bf16[3,144,1024]{2,1,0:T(8,128)(2,1)} %fusion.1), channel_id=1, source_target_pairs={{2,0},{4,2},{6,4},{8,6},{10,8},{12,10},{14,12},{16,14},{18,16},{20... | collective-permute-start | bytes 2654216 | tf_op jit(solution)/shard_map/ppermute | solution.py:427
  26.8 83.9 %collective-permute-start.4 = (bf16[2,128,1024]{2,1,0:T(8,128)(2,1)}, bf16[2,128,1024]{2,1,0:T(8,128)(2,1)}, u32[]{:S(2)}, u32[]{:S(2)}) collective-permute-start(bf16[2,128,1024]{2,1,0:T(8,128)(2,1)} %slice_bitcast_fusion.4), channel_id=1, source_target_pairs={{0,2},{2,4},{4,6},{6,8},{8,10},{10,12},{12,14},{14,16},{16,18},{18... | collective-permute-start | bytes 1572872 | tf_op jit(solution)/shard_map/ppermute | solution.py:426
  30.5 80.5 %collective-permute-start.5 = (bf16[3,128,1024]{2,1,0:T(8,128)(2,1)}, bf16[3,128,1024]{2,1,0:T(8,128)(2,1)S(1)}, u32[]{:S(2)}, u32[]{:S(2)}) collective-permute-start(bf16[3,128,1024]{2,1,0:T(8,128)(2,1)} %slice_bitcast_fusion.1), channel_id=1, source_target_pairs={{2,0},{4,2},{6,4},{8,6},{10,8},{12,10},{14,12},{16,14},{18,16},{20... | collective-permute-start | bytes 2359304 | tf_op jit(solution)/shard_map/ppermute | solution.py:427
  32.7 0.8 copy-start.5
  33.5 40.9 %collective-permute-start.6 = (bf16[2,128,1024]{2,1,0:T(8,128)(2,1)}, bf16[2,128,1024]{2,1,0:T(8,128)(2,1)S(1)}, u32[]{:S(2)}, u32[]{:S(2)}) collective-permute-start(bf16[2,128,1024]{2,1,0:T(8,128)(2,1)} %slice_bitcast_fusion.5), channel_id=1, source_target_pairs={{0,2},{2,4},{4,6},{6,8},{8,10},{10,12},{12,14},{14,16},{16,18},{18... | collective-permute-start | bytes 1572872 | tf_op jit(solution)/shard_map/ppermute | solution.py:426
  46.0 52.0 %collective-permute-start.7 = (bf16[3,128,1024]{2,1,0:T(8,128)(2,1)}, bf16[3,128,1024]{2,1,0:T(8,128)(2,1)}, u32[]{:S(2)}, u32[]{:S(2)}) collective-permute-start(bf16[3,128,1024]{2,1,0:T(8,128)(2,1)} %slice_bitcast_fusion.2), channel_id=1, source_target_pairs={{2,0},{4,2},{6,4},{8,6},{10,8},{12,10},{14,12},{16,14},{18,16},{20... | collective-permute-start | bytes 2359304 | tf_op jit(solution)/shard_map/ppermute | solution.py:427
  74.4 9.0 %copy-start.3 = (bf16[2,128,1024]{2,1,0:T(8,128)(2,1)}, bf16[2,128,1024]{2,1,0:T(8,128)(2,1)S(1)}, u32[]{:S(2)}) copy-start(bf16[2,128,1024]{2,1,0:T(8,128)(2,1)S(1)} %collective-permute-done.6.low_ref) | copy-start | bytes 1572868
  74.4 49.1 %collective-permute-start = (bf16[2,128,1024]{2,1,0:T(8,128)(2,1)}, bf16[2,128,1024]{2,1,0:T(8,128)(2,1)}, u32[]{:S(2)}, u32[]{:S(2)}) collective-permute-start(bf16[2,128,1024]{2,1,0:T(8,128)(2,1)} %slice_bitcast_fusion.3), channel_id=1, source_target_pairs={{0,2},{2,4},{4,6},{6,8},{8,10},{10,12},{12,14},{14,16},{16,18},{18... | collective-permute-start | bytes 1572872 | tf_op jit(solution)/shard_map/ppermute | solution.py:426
  85.2 2.2 %copy-start.1 = (bf16[512,4,1024]{2,1,0:T(4,128)(2,1)S(1)}, bf16[512,4,1024]{2,1,0:T(4,128)(2,1)}, u32[]{:S(2)}) copy-start(bf16[512,4,1024]{2,1,0:T(4,128)(2,1)} %own_ref.7) | copy-start | bytes 12582916
  87.4 11.8 %copy-start.4 = (bf16[2,128,1024]{2,1,0:T(8,128)(2,1)S(1)}, bf16[2,128,1024]{2,1,0:T(8,128)(2,1)}, u32[]{:S(2)}) copy-start(bf16[2,128,1024]{2,1,0:T(8,128)(2,1)} %copy-done.3) | copy-start | bytes 1572868
  98.0 40.5 %collective-permute-start.8 = (bf16[128,2688]{1,0:T(8,128)(2,1)S(1)}, bf16[128,2688]{1,0:T(8,128)(2,1)S(1)}, u32[]{:S(2)}, u32[]{:S(2)}) collective-permute-start(bf16[128,2688]{1,0:T(8,128)(2,1)S(1)} %get-tuple-element.41), channel_id=1, source_target_pairs={{0,1},{1,0},{2,3},{3,2},{4,5},{5,4},{6,7},{7,6},{8,9},{9,8},{10,11... | collective-permute-start | bytes 2064392 | tf_op jit(solution)/shard_map/ppermute | solution.py:443
  110.7 27.8 %collective-permute-start.9 = (bf16[128,2688]{1,0:T(8,128)(2,1)S(1)}, bf16[128,2688]{1,0:T(8,128)(2,1)S(1)}, u32[]{:S(2)}, u32[]{:S(2)}) collective-permute-start(bf16[128,2688]{1,0:T(8,128)(2,1)S(1)} %get-tuple-element.43), channel_id=1, source_target_pairs={{0,1},{1,0},{2,3},{3,2},{4,5},{5,4},{6,7},{7,6},{8,9},{9,8},{10,11... | collective-permute-start | bytes 2064392 | tf_op jit(solution)/shard_map/ppermute | solution.py:443
  122.3 22.6 %collective-permute-start.10 = (bf16[128,2688]{1,0:T(8,128)(2,1)S(1)}, bf16[128,2688]{1,0:T(8,128)(2,1)S(1)}, u32[]{:S(2)}, u32[]{:S(2)}) collective-permute-start(bf16[128,2688]{1,0:T(8,128)(2,1)S(1)} %get-tuple-element.45), channel_id=1, source_target_pairs={{0,1},{1,0},{2,3},{3,2},{4,5},{5,4},{6,7},{7,6},{8,9},{9,8},{10,11... | collective-permute-start | bytes 2064392 | tf_op jit(solution)/shard_map/ppermute | solution.py:443
  123.6 11.7 %copy-start.2 = (bf16[1024,1024]{1,0:T(8,128)(2,1)S(1)}, bf16[1024,1024]{1,0:T(8,128)(2,1)}, u32[]{:S(2)}) copy-start(bf16[1024,1024]{1,0:T(8,128)(2,1)} %weight_ref.1) | copy-start | bytes 6291460
  135.0 23.9 %collective-permute-start.11 = (bf16[128,2688]{1,0:T(8,128)(2,1)S(1)}, bf16[128,2688]{1,0:T(8,128)(2,1)S(1)}, u32[]{:S(2)}, u32[]{:S(2)}) collective-permute-start(bf16[128,2688]{1,0:T(8,128)(2,1)S(1)} %get-tuple-element.47), channel_id=1, source_target_pairs={{0,1},{1,0},{2,3},{3,2},{4,5},{5,4},{6,7},{7,6},{8,9},{9,8},{10,11... | collective-permute-start | bytes 2064392 | tf_op jit(solution)/shard_map/ppermute | solution.py:443
where the time goes:
time: 167 us
  Pallas kernels  69.7 us (42%)
  waiting for transfers between devices  39.5 us (24%)
  starting transfers between devices  26.8 us (16%)
  local copies, waits for them, and re-layouts  24.1 us (14%)
  other arithmetic  5.52 us (3%)
    pallas_call x4, Pallas kernels, sweep(): pl.pallas_call(functools.partial(sweep_kernel, depth, count, band), grid_...  44.9 us
    ppermute x4, waiting for transfers between devices, body(): low = lax.ppermute(up, 'cells', neighbours('cells', 1))  26.2 us
    pallas_call x2, Pallas kernels, weigh(): pl.pallas_call(functools.partial(weigh_kernel, depth, band, len(pieces),...  21.6 us
    ppermute x4, starting transfers between devices, body(): low = lax.ppermute(up, 'cells', neighbours('cells', 1))  16.2 us
    ppermute x4, starting transfers between devices, body(): high = lax.ppermute(down, 'cells', neighbours('cells', -1))  7.66 us
    ppermute x4, waiting for transfers between devices, body(): high = lax.ppermute(down, 'cells', neighbours('cells', -1))  6.9 us
    ppermute x4, waiting for transfers between devices, body(): pieces.append(lax.ppermute(sent[r - 1], 'src', pairs))  6.39 us
    another operation x9, local copies, waits for them, and re-layouts, stencil_coefficients(): return jnp.stack(rows, axis=1)  6.22 us
  transfers between devices with their start and end apart: 12, of which 3 were waited for; matrix products, arithmetic and copies ran while one was open for 11% of the time, Pallas kernels for 37%

commit v1 on v0

--- a/solution.py
+++ b/solution.py
@@ -14,21 +14,14 @@
 GROUP = 16
 ROWS = 32
 UNIT = 128
-LOW = 2
-HIGH = 3
-
-
-def neighbours(axis, step):
+HALO = 2
+PART = 16
+
+
+def pairs_of(axis, first):
     count = lax.axis_size(axis)
-    return [(i, i + step) for i in range(count) if 0 <= i + step < count]
-
-
-def shift_last(values, offset):
-    if offset > 0:
-        padding = jnp.zeros(values.shape[:-1] + (offset,), values.dtype)
-        return jnp.concatenate([values[..., offset:], padding], axis=-1)
-    padding = jnp.zeros(values.shape[:-1] + (-offset,), values.dtype)
-    return jnp.concatenate([padding, values[..., :offset]], axis=-1)
+    pairs = [(i, i + 1) for i in range(first, count - 1, 2)]
+    return pairs + [(b, a) for a, b in pairs]
 
 
 def split(values):
@@ -37,57 +30,104 @@
         parts.append(lax.reduce_precision(values, 8, 7))
         values = values - parts[-1]
     rows = jnp.stack(parts, axis=1).astype(jnp.bfloat16)
-    return jnp.pad(rows, ((0, 0), (0, GROUP - 3), (0, 0)))
-
-
-def joined(rows):
-    rows = rows[:, :3].astype(jnp.float32)
-    return (rows[:, 2] + rows[:, 1]) + rows[:, 0]
-
-
-def stencil_coefficients(conductivity, low, high, first_plane, planes_total):
-    _, cells = conductivity.shape
-    padded = jnp.concatenate([low, conductivity, high], axis=0)
-    sigma = padded[1:-1]
-    column = jnp.arange(cells, dtype=jnp.int32)
-    upper = (column % NY != NY - 1).astype(jnp.float32)
-    lower = (column % NY != 0).astype(jnp.float32)
-    plane = first_plane - 1 + jnp.arange(sigma.shape[0], dtype=jnp.int32)
-    inside = ((plane >= 0) & (plane < planes_total))[:, None]
-    z_plus = 0.5 * (sigma + padded[2:])
-    z_minus = 0.5 * (sigma + padded[:-2])
-    y_plus = 0.5 * (sigma + shift_last(sigma, 1) * upper)
-    y_minus = 0.5 * (sigma + shift_last(sigma, -1) * lower)
-    x_plus = 0.5 * (sigma + shift_last(sigma, NY))
-    x_minus = 0.5 * (sigma + shift_last(sigma, -NY))
+    return jnp.pad(rows, ((0, 0), (0, PART - 3), (0, 0)))
+
+
+def coefficient_kernel(depth, planes_total, place_ref, sigma_ref, inner_ref, outer_ref, out_ref, padded):
+    cells = sigma_ref.shape[1]
+    planes = depth + 2
+    odd = place_ref[2]
+
+    def put(at, ref):
+        for i in range(HALO):
+            part = ref[i].astype(jnp.float32)
+            padded[at + i : at + i + 1, :] = (part[2:3] + part[1:2]) + part[0:1]
+
+    padded[HALO : HALO + depth, :] = sigma_ref[...]
+
+    @pl.when(odd == 0)
+    def _():
+        put(0, outer_ref)
+        put(HALO + depth, inner_ref)
+
+    @pl.when(odd == 1)
+    def _():
+        put(0, inner_ref)
+        put(HALO + depth, outer_ref)
+
+    sigma = padded[1 : planes + 1, :]
+    column = lax.broadcasted_iota(jnp.int32, sigma.shape, 1)
+    row = lax.rem(column, NY)
+    plane = lax.div(place_ref[1], cells) - 1 + lax.broadcasted_iota(jnp.int32, sigma.shape, 0)
+    inside = (plane >= 0) & (plane < planes_total)
+    zero = jnp.zeros_like(sigma)
+    upper, lower = row != NY - 1, row != 0
+    ahead, behind = column < cells - NY, column >= NY
+    z_plus = 0.5 * (sigma + padded[2 : planes + 2, :])
+    z_minus = 0.5 * (sigma + padded[0:planes, :])
+    y_plus = 0.5 * (sigma + jnp.where(upper, pltpu.roll(sigma, cells - 1, 1), zero))
+    y_minus = 0.5 * (sigma + jnp.where(lower, pltpu.roll(sigma, 1, 1), zero))
+    x_plus = 0.5 * (sigma + jnp.where(ahead, pltpu.roll(sigma, cells - NY, 1), zero))
+    x_minus = 0.5 * (sigma + jnp.where(behind, pltpu.roll(sigma, NY, 1), zero))
     diagonal = z_plus + z_minus + y_plus + y_minus + x_plus + x_minus
-    scale = jnp.where(inside, 2.0 / jnp.where(inside, diagonal, 1.0), 0.0)
-    rows = [
+    scale = jnp.where(inside, 2.0 / jnp.where(inside, diagonal, 1.0), zero)
+    kinds = [
         z_plus * scale,
         z_minus * scale,
-        y_plus * scale * upper,
-        y_minus * scale * lower,
-        x_plus * scale * (column < cells - NY),
-        x_minus * scale * (column >= NY),
+        jnp.where(upper, y_plus * scale, zero),
+        jnp.where(lower, y_minus * scale, zero),
+        jnp.where(ahead, x_plus * scale, zero),
+        jnp.where(behind, x_minus * scale, zero),
         current * scale,
         -current * scale,
     ]
-    return jnp.stack(rows, axis=1)
+    for kind, values in enumerate(kinds):
+        for i in range(planes):
+            out_ref[i, kind : kind + 1, :] = values[i : i + 1, :]
+
+
+def stencil_coefficients(place, conductivity, inner, outer, planes_total):
+    depth, cells = conductivity.shape
+    part = inner.shape[1] // PART - 1
+    shape = (depth + 2, 8, cells)
+    return pl.pallas_call(
+        functools.partial(coefficient_kernel, depth, planes_total),
+        grid_spec=pltpu.PrefetchScalarGridSpec(
+            num_scalar_prefetch=1,
+            grid=(1,),
+            in_specs=[pl.BlockSpec((depth, cells), lambda i, place: (0, 0))]
+            + [pl.BlockSpec((HALO, PART, cells), lambda i, place: (0, part, 0))] * 2,
+            out_specs=pl.BlockSpec(shape, lambda i, place: (0, 0, 0)),
+            scratch_shapes=[pltpu.VMEM((2 * HALO + depth, cells), jnp.float32)],
+        ),
+        out_shape=jax.ShapeDtypeStruct(shape, jnp.float32),
+        compiler_params=pltpu.CompilerParams(vmem_limit_bytes=8 * 2**20),
+        name="coefficients",
+    )(place, conductivity, inner, outer)
 
 
 def lane_index(shape):
     return lax.broadcasted_iota(jnp.int32, shape, 1)
 
 
-def sweep_kernel(depth, count, band, place_ref, own_ref, low_ref, high_ref, coef_ref, elec_ref, *refs):
+def sweep_kernel(depth, count, band, place_ref, own_ref, inner_ref, outer_ref, coef_ref, elec_ref, *refs):
     refs = refs[-(count + 6) :]
     pot_ref, outs, (first, second, extra, final) = refs[0], refs[1 : count + 1], refs[count + 1 : count + 5]
     elec_b = refs[count + 5]
-    rows, _, cells = own_ref.shape
+    _, rows, cells = own_ref.shape
     tiles = cells // LANES
-    first[0:LOW] = low_ref[...]
-    first[LOW : LOW + depth] = jnp.swapaxes(own_ref[...].astype(jnp.float32), 0, 1).astype(jnp.bfloat16)
-    first[LOW + depth :] = high_ref[...]
+    first[HALO : HALO + depth] = own_ref[...]
+
+    @pl.when(place_ref[2] == 0)
+    def _():
+        first[0:HALO] = outer_ref[...]
+        first[HALO + depth :] = inner_ref[...]
+
+    @pl.when(place_ref[2] == 1)
+    def _():
+        first[0:HALO] = inner_ref[...]
+        first[HALO + depth :] = outer_ref[...]
+
     elec_b[0] = jnp.broadcast_to(elec_ref[:, 0:1], (rows, LANES))
     elec_b[1] = jnp.broadcast_to(elec_ref[:, 1:2], (rows, LANES))
     lane = lane_index((GROUP, LANES))
@@ -166,19 +206,20 @@
             run([lambda: relax_second(plane - 3, at), lambda: relax_first(plane, at)])
         return carry
 
+    planes = depth + 2
     lax.fori_loop(0, 3, only_first, 0)
-    lax.fori_loop(3, depth + HIGH, both, 0)
-    for plane in range(depth + HIGH - 3, depth + 1):
+    lax.fori_loop(3, planes, both, 0)
+    for plane in range(planes - 3, depth):
         for at in spans:
             run([lambda: relax_second(plane, at)])
-    pot_ref[...] = jnp.swapaxes(final[0:depth].astype(jnp.float32), 0, 1).astype(jnp.bfloat16)
+    pot_ref[...] = final[...]
 
     wide = lane_index((rows, LANES))
     for r in range(count):
         out = outs[r]
         target = lax.rem(place_ref[0] + r, count)
         start = pl.multiple_of(target * band, LANES)
-        for plane in range(depth + 1):
+        for plane in range(depth):
             out[:, plane * band : (plane + 1) * band] = final[plane, :, pl.ds(start, band)]
         after = jnp.minimum(target + 1, count - 1)
         after_start = pl.multiple_of(after * band, LANES)
@@ -192,7 +233,7 @@
                     row = pltpu.roll(row, slot * NY, 1) if slot else row
                     mine = (wide >= slot * NY) & (wide < (slot + 1) * NY)
                     packed = jnp.where(mine, row, packed)
-            begin = (depth + 1) * band + piece * LANES
+            begin = depth * band + piece * LANES
             out[:, begin : begin + LANES] = (packed * kept).astype(jnp.bfloat16)
 
 
@@ -200,24 +241,24 @@
     return -(-depth * NY // LANES) * LANES
 
 
-def sweep(place, own, low, high, coefs, electrodes, before, begin, size, count, band):
-    _, depth, cells = own.shape
-    width = (depth + 1) * band + beside_width(depth)
+def sweep(place, own, inner, outer, coefs, electrodes, before, begin, size, count, band):
+    depth, _, cells = own.shape
+    width = depth * band + beside_width(depth)
     block = begin // ROWS
     in_specs = [
-        pl.BlockSpec((ROWS, depth, cells), lambda i, place: (i + block, 0, 0)),
-        pl.BlockSpec((LOW, ROWS, cells), lambda i, place: (0, i, 0)),
-        pl.BlockSpec((HIGH, ROWS, cells), lambda i, place: (0, i, 0)),
+        pl.BlockSpec((depth, ROWS, cells), lambda i, place: (0, i + block, 0)),
+        pl.BlockSpec((HALO, ROWS, cells), lambda i, place: (0, i, 0)),
+        pl.BlockSpec((HALO, ROWS, cells), lambda i, place: (0, i, 0)),
         pl.BlockSpec(coefs.shape, lambda i, place: (0, 0, 0)),
         pl.BlockSpec((ROWS, 2), lambda i, place: (i + block, 0)),
     ]
-    args = [place, own, low, high, coefs, electrodes]
+    args = [place, own, inner, outer, coefs, electrodes]
     aliases = {}
     if before is not None:
         in_specs.append(pl.BlockSpec(memory_space=pl.ANY))
         args.append(before)
         aliases = {6: 0}
-    planes = depth + HIGH
+    planes = depth + 2
     flops = size * cells * planes * 40
     return pl.pallas_call(
         functools.partial(sweep_kernel, depth, count, band),
@@ -225,13 +266,13 @@
             num_scalar_prefetch=1,
             grid=(size // ROWS,),
             in_specs=in_specs,
-            out_specs=[pl.BlockSpec((ROWS, depth, cells), lambda i, place: (i + block, 0, 0))]
+            out_specs=[pl.BlockSpec((depth, ROWS, cells), lambda i, place: (0, i + block, 0))]
             + [pl.BlockSpec((ROWS, width), lambda i, place: (i, 0))] * count,
             scratch_shapes=[
-                pltpu.VMEM((LOW + depth + HIGH, ROWS, cells), jnp.bfloat16),
+                pltpu.VMEM((2 * HALO + depth, ROWS, cells), jnp.bfloat16),
                 pltpu.VMEM((planes, ROWS, cells), jnp.float32),
                 pltpu.VMEM((planes, ROWS, cells), jnp.float32),
-                pltpu.VMEM((depth + 1, ROWS, cells), jnp.bfloat16),
+                pltpu.VMEM((depth, ROWS, cells), jnp.bfloat16),
                 pltpu.VMEM((2, ROWS, LANES), jnp.int32),
             ],
         ),
@@ -240,7 +281,7 @@
         input_output_aliases=aliases,
         compiler_params=pltpu.CompilerParams(vmem_limit_bytes=24 * 2**20),
         cost_estimate=pl.CostEstimate(
-            flops=flops, bytes_accessed=size * cells * 2 * (3 * depth + LOW + HIGH), transcendentals=0
+            flops=flops, bytes_accessed=size * cells * 2 * (3 * depth + 2 * HALO), transcendentals=0
         ),
         name="sweep",
     )(*args)
@@ -297,21 +338,24 @@
     )(place, weight)
 
 
-def weigh_kernel(depth, band, pieces, row_start, block_rows, chunk_rows, scale, weight_ref, *refs):
-    piece_refs = refs[:pieces]
-    before_ref, out_ref, held, mixed, partial, sems = refs[pieces:]
+def weigh_kernel(depth, band, pieces, above, row_start, block_rows, chunk_rows, scale, weight_ref, *refs):
+    piece_refs, above_refs = refs[:pieces], refs[pieces : pieces + above]
+    before_ref, out_ref, held, mixed, partial, sems = refs[pieces + above :]
     step = pl.program_id(0)
     tiles = band // LANES
+    wide = depth * band + beside_width(depth)
 
     @pl.when(step == 0)
     def _():
-        at = 0
         copies = []
-        for i, piece in enumerate(piece_refs):
-            size = piece.shape[0]
-            copies.append(pltpu.make_async_copy(piece, held.at[pl.ds(at, size)], sems.at[i]))
-            copies[-1].start()
-            at += size
+        for group, column in ((piece_refs, 0), (above_refs, wide)):
+            at = 0
+            for ref in group:
+                size, width = ref.shape
+                into = held.at[pl.ds(at, size), pl.ds(column, width)]
+                copies.append(pltpu.make_async_copy(ref, into, sems.at[len(copies)]))
+                copies[-1].start()
+                at += size
         for copy in copies:
             copy.wait()
         partial[...] = before_ref[...]
@@ -332,7 +376,7 @@
     base = row_start + step * block_rows
 
     for plane in range(depth):
-        beside_tile = (depth + 1) * band + (plane * NY // LANES) * LANES
+        beside_tile = depth * band + (plane * NY // LANES) * LANES
         turn = (LANES - NY - plane * NY) % LANES
 
         def rows_of(group, totals):
@@ -344,7 +388,8 @@
                 return held[at_held, lanes].astype(jnp.float32), mixed[at, lanes]
 
             centre = [read(plane * band + t * LANES) for t in range(tiles)]
-            above = [read((plane + 1) * band + t * LANES) for t in range(tiles)]
+            over = (plane + 1) * band if plane < depth - 1 else wide
+            above = [read(over + t * LANES) for t in range(tiles)]
             ahead = [tuple(pltpu.roll(c, LANES - NY, 1) for c in pair) for pair in centre]
             ahead.append(tuple(pltpu.roll(c, turn, 1) if turn else c for c in read(beside_tile)))
             result = []
@@ -376,19 +421,19 @@
                 out_ref[plane : plane + 1, :] = total * scale
 
 
-def weigh(weight, pieces, before, row_start, rows, chunk_rows, depth, band, scale):
-    width = pieces[0].shape[1]
+def weigh(weight, pieces, above, before, row_start, rows, chunk_rows, depth, band, scale):
+    width = pieces[0].shape[1] + band
     held = sum(piece.shape[0] for piece in pieces)
     block_rows = UNIT
     first = row_start // block_rows
     out = (depth, band) if scale is not None else (depth * 8, band)
     return pl.pallas_call(
         functools.partial(
-            weigh_kernel, depth, band, len(pieces), row_start, block_rows, chunk_rows, scale
+            weigh_kernel, depth, band, len(pieces), len(above), row_start, block_rows, chunk_rows, scale
         ),
         grid=(rows // block_rows,),
         in_specs=[pl.BlockSpec((block_rows, weight.shape[1]), lambda i: (i + first, 0))]
-        + [pl.BlockSpec(memory_space=pl.ANY)] * len(pieces)
+        + [pl.BlockSpec(memory_space=pl.ANY)] * (len(pieces) + len(above))
         + [pl.BlockSpec((depth * 8, band), lambda i: (0, 0))],
         out_specs=pl.BlockSpec(out, lambda i: (0, 0)),
         out_shape=jax.ShapeDtypeStruct(out, jnp.float32),
@@ -396,14 +441,14 @@
             pltpu.VMEM((held, width), jnp.bfloat16),
             pltpu.VMEM((block_rows, width), jnp.float32),
             pltpu.VMEM((depth * 8, band), jnp.float32),
-            pltpu.SemaphoreType.DMA((len(pieces),)),
+            pltpu.SemaphoreType.DMA((len(pieces) + len(above),)),
         ],
         compiler_params=pltpu.CompilerParams(vmem_limit_bytes=32 * 2**20),
         cost_estimate=pl.CostEstimate(
             flops=2 * rows * held * width, bytes_accessed=2 * held * width, transcendentals=0
         ),
         name="weigh",
-    )(weight, *pieces, before)
+    )(weight, *pieces, *above, before)
 
 
 def body(conductivity, prev_fields, electrodes, data_weight):
@@ -413,52 +458,55 @@
     sources = data_weight.shape[0]
     per = local // UNIT
     slab = lax.axis_index("cells")
+    odd = lax.rem(slab, 2)
+    place = jnp.stack([lax.axis_index("src"), slab * (depth * cells), odd]).astype(jnp.int32)
+    own = jnp.swapaxes(prev_fields, 0, 1)
+    bottom, top = jnp.int32(0), jnp.int32(depth - HALO)
     halos = []
-    fields = prev_fields
     for k in range(per):
-        chunk = fields[k * UNIT : (k + 1) * UNIT]
-        up = jnp.swapaxes(chunk[:, depth - LOW :], 0, 1)
-        down = jnp.swapaxes(chunk[:, :HIGH], 0, 1)
-        if k == 0:
-            up = jnp.concatenate([up, split(conductivity[depth - LOW :])], axis=1)
-            down = jnp.concatenate([down, split(conductivity[:HIGH])], axis=1)
-        fields, up, down = lax.optimization_barrier((fields, up, down))
-        low = lax.ppermute(up, "cells", neighbours("cells", 1))
-        high = lax.ppermute(down, "cells", neighbours("cells", -1))
-        halos.append((low, high))
-    low, high = (joined(halo[:, UNIT:]) for halo in halos[0])
-    coefs = stencil_coefficients(conductivity, low, high, slab * depth, depth * lax.axis_size("cells"))
-    place = jnp.stack([lax.axis_index("src"), slab * (depth * cells)]).astype(jnp.int32)
+        received = []
+        for first, start in (
+            (0, jnp.where(odd == 0, top, bottom)), (1, jnp.where(odd == 0, bottom, top))
+        ):
+            planes = lax.dynamic_slice(own, (start, k * UNIT, 0), (HALO, UNIT, cells))
+            if k == 0:
+                sigma = lax.dynamic_slice_in_dim(conductivity, start, HALO, axis=0)
+                planes = jnp.concatenate([planes, split(sigma)], axis=1)
+            received.append(lax.ppermute(planes, "cells", pairs_of("cells", first)))
+        halos.append(received)
+    coefs = stencil_coefficients(place, conductivity, *halos[0], depth * lax.axis_size("cells"))
     weight = fold(place, data_weight, count, per)
+    down = [(i + 1, i) for i in range(lax.axis_size("cells") - 1)]
+    stops = [stop for stop in (per - 2, per - 1, per) if stop > 0]
     potentials = None
-    pieces = []
+    pieces, above = [], []
+    sums = jnp.zeros((depth * 8, band), jnp.float32)
+    done = 0
     for k in range(per):
-        low, high = halos[k]
         potentials, kept, *sent = sweep(
-            place, prev_fields, low, high, coefs, electrodes, potentials, k * UNIT, UNIT, count, band
+            place, own, *halos[k], coefs, electrodes, potentials, k * UNIT, UNIT, count, band
         )
         pieces.append(kept)
         for r in range(1, count):
             pairs = [(i, (i + r) % count) for i in range(count)]
             pieces.append(lax.ppermute(sent[r - 1], "src", pairs))
-    partial = jnp.zeros((depth * 8, band), jnp.float32)
-    done = 0
-    for stop in sorted({max(per - 1, 1), per}):
-        rows = (stop - done) * UNIT * count
-        last = stop == per
-        partial = weigh(
+    for stop in stops:
+        lowest = jnp.concatenate([p[:, :band] for p in pieces[done * count : stop * count]], axis=0)
+        above.append(lax.ppermute(lowest, "cells", down))
+        sums = weigh(
             weight,
             pieces[: stop * count],
-            partial,
+            above,
+            sums,
             done * UNIT * count,
-            rows,
+            (stop - done) * UNIT * count,
             UNIT * count,
             depth,
             band,
-            1.0 / sources if last else None,
+            1.0 / sources if stop == per else None,
         )
         done = stop
-    return (potentials, partial)
+    return (jnp.swapaxes(potentials, 0, 1), sums)
 
 
 def solution(mesh):

time: 167 us -> 131 us (0.78)
  the two profiles are of different devices: /device:TPU:1 before, /device:TPU:17 now
where the time goes in v1:
time: 131 us
  Pallas kernels  56.1 us (43%)
  waiting for transfers between devices  30.9 us (24%)
  starting transfers between devices  23.2 us (18%)
  local copies, waits for them, and re-layouts  16.8 us (13%)
  other arithmetic  2.53 us (2%)
    pallas_call x4, Pallas kernels, sweep(): pl.pallas_call(functools.partial(sweep_kernel, depth, count, band), grid_...  32.9 us
    ppermute x8, waiting for transfers between devices, body(): received.append(lax.ppermute(planes, 'cells', pairs_of('cells', first)))  23.5 us
    pallas_call x3, Pallas kernels, weigh(): pl.pallas_call(functools.partial(weigh_kernel, depth, band, len(pieces),...  19.2 us
    unnamed x21, local copies, waits for them, and re-layouts  14.8 us
    ppermute x8, starting transfers between devices, body(): received.append(lax.ppermute(planes, 'cells', pairs_of('cells', first)))  13.9 us
    ppermute x4, waiting for transfers between devices, body(): pieces.append(lax.ppermute(sent[r - 1], 'src', pairs))  7.45 us
    ppermute x3, starting transfers between devices, body(): above.append(lax.ppermute(lowest, 'cells', down))  6.07 us
    pallas_call x1, Pallas kernels, fold(): pl.pallas_call(functools.partial(fold_kernel, count, per), grid_spec=pltp...  3.3 us
  transfers between devices with their start and end apart: 15, of which 3 were waited for; matrix products, arithmetic and copies ran while one was open for 6% of the time, Pallas kernels for 38%

profile of v1, /device:TPU:17, one launch (start us, length us, event | category | flops | bytes accessed | tf_op | source)
XLA Modules:
  0.0 130.7 jit_solution(15416324249245186749)
XLA Ops:
  0.6 3.6 %copy.85 = bf16[512,4,1024]{2,0,1:T(8,128)(2,1)S(1)} copy(bf16[512,4,1024]{2,1,0:T(4,128)(2,1)} %param.5) | data formatting | bytes 8388608 | tf_op args[1]
  4.2 1.8 %dynamic-slice_bitcast_fusion = (bf16[2,128,1024]{2,1,0:T(8,128)(2,1)}, bf16[2,128,1024]{2,1,0:T(8,128)(2,1)S(1)}, bf16[2,128,1024]{2,1,0:T(8,128)(2,1)}, bf16[2...) fusion(bf16[512,4,1024]{2,0,1:T(8,128)(2,1)S(1)} %copy.85, ...), kind=kLoop, calls=%fused_computation.3 | loop fusion | bytes 8388616 | tf_op jit(solution)/shard_map/dynamic_slice | solution.py:471
  9.6 3.0 %collective-permute-start.3 = (bf16[2,144,1024]{2,1,0:T(8,128)(2,1)}, bf16[2,144,1024]{2,1,0:T(8,128)(2,1)S(1)}, u32[]{:S(2)}, u32[]{:S(2)}) collective-permute-start(bf16[2,144,1024]{2,1,0:T(8,128)(2,1)} %pad_maximum_fusion.1), channel_id=1, source_target_pairs={{2,4},{6,8},{10,12},{14,16},{18,20},{22,24},{26,28},{4,2},{8,6},{1... | collective-permute-start | bytes 1769480 | tf_op jit(solution)/shard_map/ppermute | solution.py:475
  13.1 3.2 %collective-permute-start.7 = (bf16[2,128,1024]{2,1,0:T(8,128)(2,1)}, bf16[2,128,1024]{2,1,0:T(8,128)(2,1)}, u32[]{:S(2)}, u32[]{:S(2)}) collective-permute-start(bf16[2,128,1024]{2,1,0:T(8,128)(2,1)} %get-tuple-element.34), channel_id=1, source_target_pairs={{2,4},{6,8},{10,12},{14,16},{18,20},{22,24},{26,28},{4,2},{8,6},{1... | collective-permute-start | bytes 1572872 | tf_op jit(solution)/shard_map/ppermute | solution.py:475
  17.2 3.5 %collective-permute-start.5 = (bf16[2,128,1024]{2,1,0:T(8,128)(2,1)}, bf16[2,128,1024]{2,1,0:T(8,128)(2,1)S(1)}, u32[]{:S(2)}, u32[]{:S(2)}) collective-permute-start(bf16[2,128,1024]{2,1,0:T(8,128)(2,1)} %get-tuple-element.36), channel_id=1, source_target_pairs={{2,4},{6,8},{10,12},{14,16},{18,20},{22,24},{26,28},{4,2},{8,6},{1... | collective-permute-start | bytes 1572872 | tf_op jit(solution)/shard_map/ppermute | solution.py:475
  20.8 23.4 %collective-permute-done.3.outer_ref = bf16[2,144,1024]{2,1,0:T(8,128)(2,1)S(1)} collective-permute-done((bf16[2,144,1024]{2,1,0:T(8,128)(2,1)}, bf16[2,144,1024]{2,1,0:T(8,128)(2,1)S(1)}, u32[]{:S(2)}, u32[]{:S(2)}) %collective-permute-start.3) | collective-permute-done | bytes 589856 | tf_op jit(solution)/shard_map/ppermute | solution.py:475
  44.2 3.0 %collective-permute-start.1 = (bf16[2,128,1024]{2,1,0:T(8,128)(2,1)}, bf16[2,128,1024]{2,1,0:T(8,128)(2,1)S(1)}, u32[]{:S(2)}, u32[]{:S(2)}) collective-permute-start(bf16[2,128,1024]{2,1,0:T(8,128)(2,1)} %get-tuple-element.40), channel_id=1, source_target_pairs={{2,4},{6,8},{10,12},{14,16},{18,20},{22,24},{26,28},{4,2},{8,6},{1... | collective-permute-start | bytes 1572872 | tf_op jit(solution)/shard_map/ppermute | solution.py:475
  50.1 2.2 %copy-done.1 = bf16[512,4,1024]{2,0,1:T(8,128)(2,1)S(1)} copy-done((bf16[512,4,1024]{2,0,1:T(8,128)(2,1)S(1)}, bf16[512,4,1024]{2,0,1:T(8,128)(2,1)}, u32[]{:S(2)}) %copy-start.1) | copy-done | bytes 4194328
  52.9 8.0 %sweep.4 = (bf16[4,512,1024]{2,1,0:T(8,128)(2,1)S(1)}, bf16[128,2176]{1,0:T(8,128)(2,1)S(1)}, bf16[128,2176]{1,0:T(8,128)(2,1)S(1)}) custom-call(s32[3]{0:T(128)S(1)} %copy-done.8, bf16[4,512,1024]{2,1,0:T(8,128)(2,1)S(1)} %bitcast.34, bf16[2,144,1024]{2,1,0:T(8,128)(2,1)S(1)} %collective-permute-done.2.inner_ref, ...), custom_call_target="tpu_custom_call" | custom-call | flops 31457280 | bytes 4194304 | tf_op jit(solution)/shard_map/sweep/pallas_call | solution.py:263
  61.0 8.8 %sweep.5 = (bf16[4,512,1024]{2,1,0:T(8,128)(2,1)S(1)}, bf16[128,2176]{1,0:T(8,128)(2,1)S(1)}, bf16[128,2176]{1,0:T(8,128)(2,1)S(1)}) custom-call(s32[3]{0:T(128)S(1)} %copy-done.8, bf16[4,512,1024]{2,1,0:T(8,128)(2,1)S(1)} %bitcast.35, bf16[2,128,1024]{2,1,0:T(8,128)(2,1)S(1)} %copy-done.5, ...), custom_call_target="tpu_custom_call", output_to_operand_aliasing={{0}: (6, {})} | custom-call | flops 31457280 | bytes 4194304 | tf_op jit(solution)/shard_map/sweep/pallas_call | solution.py:263
  69.8 1.3 %collective-permute-start.9 = (bf16[128,2176]{1,0:T(8,128)(2,1)S(1)}, bf16[128,2176]{1,0:T(8,128)(2,1)S(1)}, u32[]{:S(2)}, u32[]{:S(2)}) collective-permute-start(bf16[128,2176]{1,0:T(8,128)(2,1)S(1)} %get-tuple-element.21), channel_id=1, source_target_pairs={{0,1},{1,0},{2,3},{3,2},{4,5},{5,4},{6,7},{7,6},{8,9},{9,8},{10,11... | collective-permute-start | bytes 1671176 | tf_op jit(solution)/shard_map/ppermute | solution.py:492
  71.3 8.0 %sweep.6 = (bf16[4,512,1024]{2,1,0:T(8,128)(2,1)S(1)}, bf16[128,2176]{1,0:T(8,128)(2,1)S(1)}, bf16[128,2176]{1,0:T(8,128)(2,1)S(1)}) custom-call(s32[3]{0:T(128)S(1)} %copy-done.8, bf16[4,512,1024]{2,1,0:T(8,128)(2,1)S(1)} %bitcast.36, bf16[2,128,1024]{2,1,0:T(8,128)(2,1)S(1)} %collective-permute-done.4.inner_ref, ...), custom_call_target="tpu_custom_call", output_to_operand_aliasing={{0}: (6, {})} | custom-call | flops 31457280 | bytes 4194304 | tf_op jit(solution)/shard_map/sweep/pallas_call | solution.py:263
  79.3 1.4 %collective-permute-start.10 = (bf16[128,2176]{1,0:T(8,128)(2,1)S(1)}, bf16[128,2176]{1,0:T(8,128)(2,1)S(1)}, u32[]{:S(2)}, u32[]{:S(2)}) collective-permute-start(bf16[128,2176]{1,0:T(8,128)(2,1)S(1)} %get-tuple-element.23), channel_id=1, source_target_pairs={{0,1},{1,0},{2,3},{3,2},{4,5},{5,4},{6,7},{7,6},{8,9},{9,8},{10,11... | collective-permute-start | bytes 1671176 | tf_op jit(solution)/shard_map/ppermute | solution.py:492
  80.7 8.0 %sweep.7 = (bf16[4,512,1024]{2,1,0:T(8,128)(2,1)S(1)}, bf16[128,2176]{1,0:T(8,128)(2,1)S(1)}, bf16[128,2176]{1,0:T(8,128)(2,1)S(1)}) custom-call(s32[3]{0:T(128)S(1)} %copy-done.8, bf16[4,512,1024]{2,1,0:T(8,128)(2,1)S(1)} %bitcast.37, bf16[2,128,1024]{2,1,0:T(8,128)(2,1)S(1)} %collective-permute-done.inner_ref, ...), custom_call_target="tpu_custom_call", output_to_operand_aliasing={{0}: (6, {})} | custom-call | flops 31457280 | bytes 4194304 | tf_op jit(solution)/shard_map/sweep/pallas_call | solution.py:263
  89.1 2.1 %collective-permute-start.12 = (bf16[512,512]{1,0:T(8,128)(2,1)S(1)}, bf16[512,512]{1,0:T(8,128)(2,1)S(1)}, u32[]{:S(2)}, u32[]{:S(2)}) collective-permute-start(bf16[512,512]{1,0:T(8,128)(2,1)S(1)} %pad_maximum_fusion.2), channel_id=1, source_target_pairs={{2,0},{4,2},{6,4},{8,6},{10,8},{12,10},{14,12},{16,14},{18,16},{20... | collective-permute-start | bytes 1572872 | tf_op jit(solution)/shard_map/ppermute | solution.py:495
  91.2 3.4 %collective-permute-done.10.refs_5_ = bf16[128,2176]{1,0:T(8,128)(2,1)S(1)} collective-permute-done((bf16[128,2176]{1,0:T(8,128)(2,1)S(1)}, bf16[128,2176]{1,0:T(8,128)(2,1)S(1)}, u32[]{:S(2)}, u32[]{:S(2)}) %collective-permute-start.10) | collective-permute-done | bytes 557088 | tf_op jit(solution)/shard_map/ppermute | solution.py:492
  94.7 1.9 %collective-permute-start.13 = (bf16[256,512]{1,0:T(8,128)(2,1)S(1)}, bf16[256,512]{1,0:T(8,128)(2,1)S(1)}, u32[]{:S(2)}, u32[]{:S(2)}) collective-permute-start(bf16[256,512]{1,0:T(8,128)(2,1)S(1)} %pad_maximum_fusion.3), channel_id=1, source_target_pairs={{2,0},{4,2},{6,4},{8,6},{10,8},{12,10},{14,12},{16,14},{18,16},{20... | collective-permute-start | bytes 786440 | tf_op jit(solution)/shard_map/ppermute | solution.py:495
  96.6 4.0 %collective-permute-done.11.refs_7_ = bf16[128,2176]{1,0:T(8,128)(2,1)S(1)} collective-permute-done((bf16[128,2176]{1,0:T(8,128)(2,1)S(1)}, bf16[128,2176]{1,0:T(8,128)(2,1)S(1)}, u32[]{:S(2)}, u32[]{:S(2)}) %collective-permute-start.11) | collective-permute-done | bytes 557088 | tf_op jit(solution)/shard_map/ppermute | solution.py:492
  100.7 2.1 %collective-permute-start.14 = (bf16[256,512]{1,0:T(8,128)(2,1)S(1)}, bf16[256,512]{1,0:T(8,128)(2,1)S(1)}, u32[]{:S(2)}, u32[]{:S(2)}) collective-permute-start(bf16[256,512]{1,0:T(8,128)(2,1)S(1)} %pad_maximum_fusion.4), channel_id=1, source_target_pairs={{2,0},{4,2},{6,4},{8,6},{10,8},{12,10},{14,12},{16,14},{18,16},{20... | collective-permute-start | bytes 786440 | tf_op jit(solution)/shard_map/ppermute | solution.py:495
  102.8 3.3 %fold.1.weight_ref = bf16[1024,1024]{1,0:T(8,128)(2,1)S(1)} custom-call(s32[3]{0:T(128)S(1)} %copy-done.8, bf16[1024,1024]{1,0:T(8,128)(2,1)S(1)} %copy-done.3), custom_call_target="tpu_custom_call" | custom-call | flops 1048576 | bytes 4194304 | tf_op jit(solution)/shard_map/fold/pallas_call | solution.py:324
  106.1 5.2 %copy.82 = bf16[512,4,1024]{2,1,0:T(4,128)(2,1)} copy(bf16[512,4,1024]{2,0,1:T(8,128)(2,1)S(1)} %bitcast.38) | data formatting | bytes 8388608
  111.3 8.2 %weigh.3.refs_8_ = f32[32,512]{1,0:T(8,128)S(1)} custom-call(bf16[1024,1024]{1,0:T(8,128)(2,1)S(1)} %fold.1.weight_ref, bf16[128,2176]{1,0:T(8,128)(2,1)S(1)} %get-tuple-element.18.refs_0_, bf16[128,2176]{1,0:T(8,128)(2,1)S(1)} %collective-permute-done.8.refs_1_, bf16[128,2176]{1,0:T(8,128)(2,1)S(1)} %get-tuple-element.20.refs_2_, ...), custom_call_target="tpu_custom_call" | custom-call | flops 1409286144 | bytes 2752512 | tf_op jit(solution)/shard_map/weigh/pallas_call | solution.py:430
  119.6 4.9 %weigh.4.refs_11_ = f32[32,512]{1,0:T(8,128)S(1)} custom-call(bf16[1024,1024]{1,0:T(8,128)(2,1)S(1)} %fold.1.weight_ref, bf16[128,2176]{1,0:T(8,128)(2,1)S(1)} %get-tuple-element.18.refs_0_, bf16[128,2176]{1,0:T(8,128)(2,1)S(1)} %collective-permute-done.8.refs_1_, bf16[128,2176]{1,0:T(8,128)(2,1)S(1)} %get-tuple-element.20.refs_2_, ...), custom_call_target="tpu_custom_call" | custom-call | flops 1056964608 | bytes 4128768 | tf_op jit(solution)/shard_map/weigh/pallas_call | solution.py:430
  124.5 6.1 %weigh.5 = f32[4,512]{1,0:T(4,128)} custom-call(bf16[1024,1024]{1,0:T(8,128)(2,1)S(1)} %fold.1.weight_ref, bf16[128,2176]{1,0:T(8,128)(2,1)S(1)} %get-tuple-element.18.refs_0_, bf16[128,2176]{1,0:T(8,128)(2,1)S(1)} %collective-permute-done.8.refs_1_, bf16[128,2176]{1,0:T(8,128)(2,1)S(1)} %get-tuple-element.20.refs_2_, ...), custom_call_target="tpu_custom_call" | custom-call | flops 1409286144 | bytes 5505024 | tf_op jit(solution)/shard_map/weigh/pallas_call | solution.py:430
  (61 shorter events, 9.0 us)
Async XLA Ops:
  4.2 2.8 %copy-start = (bf16[512,4,1024]{2,0,1:T(8,128)(2,1)}, bf16[512,4,1024]{2,0,1:T(8,128)(2,1)S(1)}, u32[]{:S(2)}) copy-start(bf16[512,4,1024]{2,0,1:T(8,128)(2,1)S(1)} %copy.85) | copy-start | bytes 12582916
  4.2 2.8 %copy-start.6 = (f32[4,1024]{1,0:T(4,128)S(1)}, f32[4,1024]{1,0:T(4,128)}, u32[]{:S(2)}) copy-start(f32[4,1024]{1,0:T(4,128)} %sigma_ref.1) | copy-start | bytes 49156
  8.0 12.7 %collective-permute-start.2 = (bf16[2,144,1024]{2,1,0:T(8,128)(2,1)}, bf16[2,144,1024]{2,1,0:T(8,128)(2,1)S(1)}, u32[]{:S(2)}, u32[]{:S(2)}) collective-permute-start(bf16[2,144,1024]{2,1,0:T(8,128)(2,1)} %pad_maximum_fusion), channel_id=1, source_target_pairs={{0,2},{4,6},{8,10},{12,14},{16,18},{20,22},{24,26},{28,30},{2,0},{... | collective-permute-start | bytes 1769480 | tf_op jit(solution)/shard_map/ppermute | solution.py:475
  9.6 34.6 %collective-permute-start.3 = (bf16[2,144,1024]{2,1,0:T(8,128)(2,1)}, bf16[2,144,1024]{2,1,0:T(8,128)(2,1)S(1)}, u32[]{:S(2)}, u32[]{:S(2)}) collective-permute-start(bf16[2,144,1024]{2,1,0:T(8,128)(2,1)} %pad_maximum_fusion.1), channel_id=1, source_target_pairs={{2,4},{6,8},{10,12},{14,16},{18,20},{22,24},{26,28},{4,2},{8,6},{1... | collective-permute-start | bytes 1769480 | tf_op jit(solution)/shard_map/ppermute | solution.py:475
  12.6 3.7 %collective-permute-start.6 = (bf16[2,128,1024]{2,1,0:T(8,128)(2,1)S(1)}, bf16[2,128,1024]{2,1,0:T(8,128)(2,1)S(1)}, u32[]{:S(2)}, u32[]{:S(2)}) collective-permute-start(bf16[2,128,1024]{2,1,0:T(8,128)(2,1)S(1)} %get-tuple-element.35), channel_id=1, source_target_pairs={{0,2},{4,6},{8,10},{12,14},{16,18},{20,22},{24,26},{28,30},{2,0},{... | collective-permute-start | bytes 1572872 | tf_op jit(solution)/shard_map/ppermute | solution.py:475
  13.1 47.8 %collective-permute-start.7 = (bf16[2,128,1024]{2,1,0:T(8,128)(2,1)}, bf16[2,128,1024]{2,1,0:T(8,128)(2,1)}, u32[]{:S(2)}, u32[]{:S(2)}) collective-permute-start(bf16[2,128,1024]{2,1,0:T(8,128)(2,1)} %get-tuple-element.34), channel_id=1, source_target_pairs={{2,4},{6,8},{10,12},{14,16},{18,20},{22,24},{26,28},{4,2},{8,6},{1... | collective-permute-start | bytes 1572872 | tf_op jit(solution)/shard_map/ppermute | solution.py:475
  16.3 54.8 %collective-permute-start.4 = (bf16[2,128,1024]{2,1,0:T(8,128)(2,1)}, bf16[2,128,1024]{2,1,0:T(8,128)(2,1)S(1)}, u32[]{:S(2)}, u32[]{:S(2)}) collective-permute-start(bf16[2,128,1024]{2,1,0:T(8,128)(2,1)} %get-tuple-element.37), channel_id=1, source_target_pairs={{0,2},{4,6},{8,10},{12,14},{16,18},{20,22},{24,26},{28,30},{2,0},{... | collective-permute-start | bytes 1572872 | tf_op jit(solution)/shard_map/ppermute | solution.py:475
  16.4 0.8 copy-start.4
  17.2 54.1 %collective-permute-start.5 = (bf16[2,128,1024]{2,1,0:T(8,128)(2,1)}, bf16[2,128,1024]{2,1,0:T(8,128)(2,1)S(1)}, u32[]{:S(2)}, u32[]{:S(2)}) collective-permute-start(bf16[2,128,1024]{2,1,0:T(8,128)(2,1)} %get-tuple-element.36), channel_id=1, source_target_pairs={{2,4},{6,8},{10,12},{14,16},{18,20},{22,24},{26,28},{4,2},{8,6},{1... | collective-permute-start | bytes 1572872 | tf_op jit(solution)/shard_map/ppermute | solution.py:475
  20.7 60.0 %collective-permute-start = (bf16[2,128,1024]{2,1,0:T(8,128)(2,1)}, bf16[2,128,1024]{2,1,0:T(8,128)(2,1)S(1)}, u32[]{:S(2)}, u32[]{:S(2)}) collective-permute-start(bf16[2,128,1024]{2,1,0:T(8,128)(2,1)} %get-tuple-element.41), channel_id=1, source_target_pairs={{0,2},{4,6},{8,10},{12,14},{16,18},{20,22},{24,26},{28,30},{2,0},{... | collective-permute-start | bytes 1572872 | tf_op jit(solution)/shard_map/ppermute | solution.py:475
  44.2 36.5 %collective-permute-start.1 = (bf16[2,128,1024]{2,1,0:T(8,128)(2,1)}, bf16[2,128,1024]{2,1,0:T(8,128)(2,1)S(1)}, u32[]{:S(2)}, u32[]{:S(2)}) collective-permute-start(bf16[2,128,1024]{2,1,0:T(8,128)(2,1)} %get-tuple-element.40), channel_id=1, source_target_pairs={{2,4},{6,8},{10,12},{14,16},{18,20},{22,24},{26,28},{4,2},{8,6},{1... | collective-permute-start | bytes 1572872 | tf_op jit(solution)/shard_map/ppermute | solution.py:475
  48.7 0.6 copy-start.7
  49.3 11.7 %copy-start.5 = (bf16[2,128,1024]{2,1,0:T(8,128)(2,1)S(1)}, bf16[2,128,1024]{2,1,0:T(8,128)(2,1)}, u32[]{:S(2)}) copy-start(bf16[2,128,1024]{2,1,0:T(8,128)(2,1)} %copy-done.4) | copy-start | bytes 1572868
  50.1 2.2 %copy-start.1 = (bf16[512,4,1024]{2,0,1:T(8,128)(2,1)S(1)}, bf16[512,4,1024]{2,0,1:T(8,128)(2,1)}, u32[]{:S(2)}) copy-start(bf16[512,4,1024]{2,0,1:T(8,128)(2,1)} %copy-done) | copy-start | bytes 12582916
  52.3 0.6 copy-start.8
  52.9 8.1 %copy-start.2 = (bf16[512,4,1024]{2,0,1:T(8,128)(2,1)S(1)}, bf16[512,4,1024]{2,0,1:T(8,128)(2,1)}, u32[]{:S(2)}) copy-start(bf16[512,4,1024]{2,0,1:T(8,128)(2,1)} %copy-done) | copy-start | bytes 12582916
  69.8 19.2 %collective-permute-start.9 = (bf16[128,2176]{1,0:T(8,128)(2,1)S(1)}, bf16[128,2176]{1,0:T(8,128)(2,1)S(1)}, u32[]{:S(2)}, u32[]{:S(2)}) collective-permute-start(bf16[128,2176]{1,0:T(8,128)(2,1)S(1)} %get-tuple-element.21), channel_id=1, source_target_pairs={{0,1},{1,0},{2,3},{3,2},{4,5},{5,4},{6,7},{7,6},{8,9},{9,8},{10,11... | collective-permute-start | bytes 1671176 | tf_op jit(solution)/shard_map/ppermute | solution.py:492
  71.1 17.9 %collective-permute-start.8 = (bf16[128,2176]{1,0:T(8,128)(2,1)S(1)}, bf16[128,2176]{1,0:T(8,128)(2,1)S(1)}, u32[]{:S(2)}, u32[]{:S(2)}) collective-permute-start(bf16[128,2176]{1,0:T(8,128)(2,1)S(1)} %get-tuple-element.19), channel_id=1, source_target_pairs={{0,1},{1,0},{2,3},{3,2},{4,5},{5,4},{6,7},{7,6},{8,9},{9,8},{10,11... | collective-permute-start | bytes 1671176 | tf_op jit(solution)/shard_map/ppermute | solution.py:492
  79.3 15.3 %collective-permute-start.10 = (bf16[128,2176]{1,0:T(8,128)(2,1)S(1)}, bf16[128,2176]{1,0:T(8,128)(2,1)S(1)}, u32[]{:S(2)}, u32[]{:S(2)}) collective-permute-start(bf16[128,2176]{1,0:T(8,128)(2,1)S(1)} %get-tuple-element.23), channel_id=1, source_target_pairs={{0,1},{1,0},{2,3},{3,2},{4,5},{5,4},{6,7},{7,6},{8,9},{9,8},{10,11... | collective-permute-start | bytes 1671176 | tf_op jit(solution)/shard_map/ppermute | solution.py:492
  88.7 14.1 %copy-start.3 = (bf16[1024,1024]{1,0:T(8,128)(2,1)S(1)}, bf16[1024,1024]{1,0:T(8,128)(2,1)}, u32[]{:S(2)}) copy-start(bf16[1024,1024]{1,0:T(8,128)(2,1)} %weight_ref.1) | copy-start | bytes 6291460
  88.7 11.9 %collective-permute-start.11 = (bf16[128,2176]{1,0:T(8,128)(2,1)S(1)}, bf16[128,2176]{1,0:T(8,128)(2,1)S(1)}, u32[]{:S(2)}, u32[]{:S(2)}) collective-permute-start(bf16[128,2176]{1,0:T(8,128)(2,1)S(1)} %get-tuple-element.25), channel_id=1, source_target_pairs={{0,1},{1,0},{2,3},{3,2},{4,5},{5,4},{6,7},{7,6},{8,9},{9,8},{10,11... | collective-permute-start | bytes 1671176 | tf_op jit(solution)/shard_map/ppermute | solution.py:492
  89.1 22.2 %collective-permute-start.12 = (bf16[512,512]{1,0:T(8,128)(2,1)S(1)}, bf16[512,512]{1,0:T(8,128)(2,1)S(1)}, u32[]{:S(2)}, u32[]{:S(2)}) collective-permute-start(bf16[512,512]{1,0:T(8,128)(2,1)S(1)} %pad_maximum_fusion.2), channel_id=1, source_target_pairs={{2,0},{4,2},{6,4},{8,6},{10,8},{12,10},{14,12},{16,14},{18,16},{20... | collective-permute-start | bytes 1572872 | tf_op jit(solution)/shard_map/ppermute | solution.py:495
  94.7 24.9 %collective-permute-start.13 = (bf16[256,512]{1,0:T(8,128)(2,1)S(1)}, bf16[256,512]{1,0:T(8,128)(2,1)S(1)}, u32[]{:S(2)}, u32[]{:S(2)}) collective-permute-start(bf16[256,512]{1,0:T(8,128)(2,1)S(1)} %pad_maximum_fusion.3), channel_id=1, source_target_pairs={{2,0},{4,2},{6,4},{8,6},{10,8},{12,10},{14,12},{16,14},{18,16},{20... | collective-permute-start | bytes 786440 | tf_op jit(solution)/shard_map/ppermute | solution.py:495
  100.7 23.8 %collective-permute-start.14 = (bf16[256,512]{1,0:T(8,128)(2,1)S(1)}, bf16[256,512]{1,0:T(8,128)(2,1)S(1)}, u32[]{:S(2)}, u32[]{:S(2)}) collective-permute-start(bf16[256,512]{1,0:T(8,128)(2,1)S(1)} %pad_maximum_fusion.4), channel_id=1, source_target_pairs={{2,0},{4,2},{6,4},{8,6},{10,8},{12,10},{14,12},{16,14},{18,16},{20... | collective-permute-start | bytes 786440 | tf_op jit(solution)/shard_map/ppermute | solution.py:495

commit v2 on v1

--- a/solution.py
+++ b/solution.py
@@ -24,19 +24,11 @@
     return pairs + [(b, a) for a, b in pairs]
 
 
-def split(values):
-    parts = []
-    for _ in range(3):
-        parts.append(lax.reduce_precision(values, 8, 7))
-        values = values - parts[-1]
-    rows = jnp.stack(parts, axis=1).astype(jnp.bfloat16)
-    return jnp.pad(rows, ((0, 0), (0, PART - 3), (0, 0)))
-
-
-def coefficient_kernel(depth, planes_total, place_ref, sigma_ref, inner_ref, outer_ref, out_ref, padded):
+def coefficient_kernel(depth, planes_total, sigma_ref, inner_ref, outer_ref, out_ref, padded):
     cells = sigma_ref.shape[1]
     planes = depth + 2
-    odd = place_ref[2]
+    slab = lax.axis_index("cells")
+    odd = lax.rem(slab, 2)
 
     def put(at, ref):
         for i in range(HALO):
@@ -58,7 +50,7 @@
     sigma = padded[1 : planes + 1, :]
     column = lax.broadcasted_iota(jnp.int32, sigma.shape, 1)
     row = lax.rem(column, NY)
-    plane = lax.div(place_ref[1], cells) - 1 + lax.broadcasted_iota(jnp.int32, sigma.shape, 0)
+    plane = slab * depth - 1 + lax.broadcasted_iota(jnp.int32, sigma.shape, 0)
     inside = (plane >= 0) & (plane < planes_total)
     zero = jnp.zeros_like(sigma)
     upper, lower = row != NY - 1, row != 0
@@ -86,44 +78,98 @@
             out_ref[i, kind : kind + 1, :] = values[i : i + 1, :]
 
 
-def stencil_coefficients(place, conductivity, inner, outer, planes_total):
+def stencil_coefficients(conductivity, inner, outer, planes_total):
     depth, cells = conductivity.shape
     part = inner.shape[1] // PART - 1
     shape = (depth + 2, 8, cells)
     return pl.pallas_call(
         functools.partial(coefficient_kernel, depth, planes_total),
-        grid_spec=pltpu.PrefetchScalarGridSpec(
-            num_scalar_prefetch=1,
-            grid=(1,),
-            in_specs=[pl.BlockSpec((depth, cells), lambda i, place: (0, 0))]
-            + [pl.BlockSpec((HALO, PART, cells), lambda i, place: (0, part, 0))] * 2,
-            out_specs=pl.BlockSpec(shape, lambda i, place: (0, 0, 0)),
-            scratch_shapes=[pltpu.VMEM((2 * HALO + depth, cells), jnp.float32)],
-        ),
+        grid=(1,),
+        in_specs=[pl.BlockSpec((depth, cells), lambda i: (0, 0))]
+        + [pl.BlockSpec((HALO, PART, cells), lambda i: (0, part, 0))] * 2,
+        out_specs=pl.BlockSpec(shape, lambda i: (0, 0, 0)),
         out_shape=jax.ShapeDtypeStruct(shape, jnp.float32),
+        scratch_shapes=[pltpu.VMEM((2 * HALO + depth, cells), jnp.float32)],
         compiler_params=pltpu.CompilerParams(vmem_limit_bytes=8 * 2**20),
         name="coefficients",
-    )(place, conductivity, inner, outer)
+    )(conductivity, inner, outer)
+
+
+def pack_kernel(extra, fields_ref, sigma_ref, own_ref, inner_ref, outer_ref):
+    rows, depth, cells = fields_ref.shape
+    odd = lax.rem(lax.axis_index("cells"), 2)
+    own_ref[...] = jnp.swapaxes(fields_ref[...].astype(jnp.float32), 0, 1).astype(jnp.bfloat16)
+
+    def part(plane):
+        rest = jnp.broadcast_to(sigma_ref[plane : plane + 1, :], (PART, cells))
+        row = lax.broadcasted_iota(jnp.int32, rest.shape, 0)
+        parts = jnp.zeros_like(rest)
+        for i in range(3):
+            rounded = rest.astype(jnp.bfloat16).astype(jnp.float32)
+            parts = jnp.where(row == i, rounded, parts)
+            rest = rest - rounded
+        return parts.astype(jnp.bfloat16)
+
+    def pick(out_ref, start):
+        out_ref[:, 0:rows] = own_ref[start : start + HALO]
+        if extra:
+            for i in range(HALO):
+                out_ref[i, rows : rows + PART, :] = part(start + i)
+
+    @pl.when(odd == 0)
+    def _():
+        pick(inner_ref, depth - HALO)
+        pick(outer_ref, 0)
+
+    @pl.when(odd == 1)
+    def _():
+        pick(inner_ref, 0)
+        pick(outer_ref, depth - HALO)
+
+
+def pack(fields, conductivity, k):
+    _, depth, cells = fields.shape
+    extra = k == 0
+    rows = UNIT if extra else ROWS
+    steps = UNIT // rows
+    sent = UNIT + (PART if extra else 0)
+    block = sent if extra else rows
+    return pl.pallas_call(
+        functools.partial(pack_kernel, extra),
+        grid=(steps,),
+        in_specs=[
+            pl.BlockSpec((rows, depth, cells), lambda i: (i + k * steps, 0, 0)),
+            pl.BlockSpec((depth, cells), lambda i: (0, 0)),
+        ],
+        out_specs=[pl.BlockSpec((depth, rows, cells), lambda i: (0, i, 0))]
+        + [pl.BlockSpec((HALO, block, cells), lambda i: (0, i, 0))] * 2,
+        out_shape=[jax.ShapeDtypeStruct((depth, UNIT, cells), jnp.bfloat16)]
+        + [jax.ShapeDtypeStruct((HALO, sent, cells), jnp.bfloat16)] * 2,
+        compiler_params=pltpu.CompilerParams(vmem_limit_bytes=60 * 2**20),
+        name="pack",
+    )(fields, conductivity)
 
 
 def lane_index(shape):
     return lax.broadcasted_iota(jnp.int32, shape, 1)
 
 
-def sweep_kernel(depth, count, band, place_ref, own_ref, inner_ref, outer_ref, coef_ref, elec_ref, *refs):
+def sweep_kernel(count, band, own_ref, inner_ref, outer_ref, coef_ref, elec_ref, *refs):
     refs = refs[-(count + 6) :]
     pot_ref, outs, (first, second, extra, final) = refs[0], refs[1 : count + 1], refs[count + 1 : count + 5]
     elec_b = refs[count + 5]
-    _, rows, cells = own_ref.shape
+    depth, rows, cells = own_ref.shape
+    slab = lax.axis_index("cells")
+    odd = lax.rem(slab, 2)
     tiles = cells // LANES
     first[HALO : HALO + depth] = own_ref[...]
 
-    @pl.when(place_ref[2] == 0)
+    @pl.when(odd == 0)
     def _():
         first[0:HALO] = outer_ref[...]
         first[HALO + depth :] = inner_ref[...]
 
-    @pl.when(place_ref[2] == 1)
+    @pl.when(odd == 1)
     def _():
         first[0:HALO] = inner_ref[...]
         first[HALO + depth :] = outer_ref[...]
@@ -163,7 +209,7 @@
 
     def relax_first(plane, at):
         sums = stencil(first, plane + 1, plane, at)
-        base = place_ref[1] + (plane - 1) * cells
+        base = (slab * depth + plane - 1) * cells
         plus = elec_b[0, at, :] - base
         minus = elec_b[1, at, :] - base
 
@@ -212,12 +258,12 @@
     for plane in range(planes - 3, depth):
         for at in spans:
             run([lambda: relax_second(plane, at)])
-    pot_ref[...] = final[...]
+    pot_ref[...] = jnp.swapaxes(final[...].astype(jnp.float32), 0, 1).astype(jnp.bfloat16)
 
     wide = lane_index((rows, LANES))
     for r in range(count):
         out = outs[r]
-        target = lax.rem(place_ref[0] + r, count)
+        target = lax.rem(lax.axis_index("src") + r, count)
         start = pl.multiple_of(target * band, LANES)
         for plane in range(depth):
             out[:, plane * band : (plane + 1) * band] = final[plane, :, pl.ds(start, band)]
@@ -241,57 +287,55 @@
     return -(-depth * NY // LANES) * LANES
 
 
-def sweep(place, own, inner, outer, coefs, electrodes, before, begin, size, count, band):
-    depth, _, cells = own.shape
+def sweep(own, inner, outer, coefs, electrodes, before, total, begin, count, band):
+    depth, size, cells = own.shape
     width = depth * band + beside_width(depth)
     block = begin // ROWS
     in_specs = [
-        pl.BlockSpec((depth, ROWS, cells), lambda i, place: (0, i + block, 0)),
-        pl.BlockSpec((HALO, ROWS, cells), lambda i, place: (0, i, 0)),
-        pl.BlockSpec((HALO, ROWS, cells), lambda i, place: (0, i, 0)),
-        pl.BlockSpec(coefs.shape, lambda i, place: (0, 0, 0)),
-        pl.BlockSpec((ROWS, 2), lambda i, place: (i + block, 0)),
+        pl.BlockSpec((depth, ROWS, cells), lambda i: (0, i, 0)),
+        pl.BlockSpec((HALO, ROWS, cells), lambda i: (0, i, 0)),
+        pl.BlockSpec((HALO, ROWS, cells), lambda i: (0, i, 0)),
+        pl.BlockSpec(coefs.shape, lambda i: (0, 0, 0)),
+        pl.BlockSpec((ROWS, 2), lambda i: (i + block, 0)),
     ]
-    args = [place, own, inner, outer, coefs, electrodes]
+    args = [own, inner, outer, coefs, electrodes]
     aliases = {}
     if before is not None:
         in_specs.append(pl.BlockSpec(memory_space=pl.ANY))
         args.append(before)
-        aliases = {6: 0}
+        aliases = {5: 0}
     planes = depth + 2
-    flops = size * cells * planes * 40
     return pl.pallas_call(
-        functools.partial(sweep_kernel, depth, count, band),
-        grid_spec=pltpu.PrefetchScalarGridSpec(
-            num_scalar_prefetch=1,
-            grid=(size // ROWS,),
-            in_specs=in_specs,
-            out_specs=[pl.BlockSpec((depth, ROWS, cells), lambda i, place: (0, i + block, 0))]
-            + [pl.BlockSpec((ROWS, width), lambda i, place: (i, 0))] * count,
-            scratch_shapes=[
-                pltpu.VMEM((2 * HALO + depth, ROWS, cells), jnp.bfloat16),
-                pltpu.VMEM((planes, ROWS, cells), jnp.float32),
-                pltpu.VMEM((planes, ROWS, cells), jnp.float32),
-                pltpu.VMEM((depth, ROWS, cells), jnp.bfloat16),
-                pltpu.VMEM((2, ROWS, LANES), jnp.int32),
-            ],
-        ),
-        out_shape=[jax.ShapeDtypeStruct(own.shape, jnp.bfloat16)]
+        functools.partial(sweep_kernel, count, band),
+        grid=(size // ROWS,),
+        in_specs=in_specs,
+        out_specs=[pl.BlockSpec((ROWS, depth, cells), lambda i: (i + block, 0, 0))]
+        + [pl.BlockSpec((ROWS, width), lambda i: (i, 0))] * count,
+        scratch_shapes=[
+            pltpu.VMEM((2 * HALO + depth, ROWS, cells), jnp.bfloat16),
+            pltpu.VMEM((planes, ROWS, cells), jnp.float32),
+            pltpu.VMEM((planes, ROWS, cells), jnp.float32),
+            pltpu.VMEM((depth, ROWS, cells), jnp.bfloat16),
+            pltpu.VMEM((2, ROWS, LANES), jnp.int32),
+        ],
+        out_shape=[jax.ShapeDtypeStruct((total, depth, cells), jnp.bfloat16)]
         + [jax.ShapeDtypeStruct((size, width), jnp.bfloat16)] * count,
         input_output_aliases=aliases,
-        compiler_params=pltpu.CompilerParams(vmem_limit_bytes=24 * 2**20),
+        compiler_params=pltpu.CompilerParams(vmem_limit_bytes=44 * 2**20),
         cost_estimate=pl.CostEstimate(
-            flops=flops, bytes_accessed=size * cells * 2 * (3 * depth + 2 * HALO), transcendentals=0
+            flops=size * cells * planes * 40,
+            bytes_accessed=size * cells * 2 * (3 * depth + 2 * HALO),
+            transcendentals=0,
         ),
         name="sweep",
     )(*args)
 
 
-def fold_kernel(count, per, place_ref, weight_ref, out_ref):
+def fold_kernel(count, per, weight_ref, out_ref):
     total = count * per
 
     def where_is(block):
-        holder = lax.rem(place_ref[0] + count - lax.rem(block, count), count)
+        holder = lax.rem(lax.axis_index("src") + count - lax.rem(block, count), count)
         return pl.multiple_of((holder * per + lax.div(block, count)) * UNIT, UNIT)
 
     for q in range(total):
@@ -320,22 +364,19 @@
             )
 
 
-def fold(place, weight, count, per):
+def fold(weight, count, per):
     return pl.pallas_call(
         functools.partial(fold_kernel, count, per),
-        grid_spec=pltpu.PrefetchScalarGridSpec(
-            num_scalar_prefetch=1,
-            grid=(1,),
-            in_specs=[pl.BlockSpec(weight.shape, lambda i, place: (0, 0))],
-            out_specs=pl.BlockSpec(weight.shape, lambda i, place: (0, 0)),
-        ),
+        grid=(1,),
+        in_specs=[pl.BlockSpec(weight.shape, lambda i: (0, 0))],
+        out_specs=pl.BlockSpec(weight.shape, lambda i: (0, 0)),
         out_shape=jax.ShapeDtypeStruct(weight.shape, jnp.bfloat16),
-        compiler_params=pltpu.CompilerParams(vmem_limit_bytes=24 * 2**20),
+        compiler_params=pltpu.CompilerParams(vmem_limit_bytes=16 * 2**20),
         cost_estimate=pl.CostEstimate(
             flops=weight.size, bytes_accessed=weight.size * 4, transcendentals=0
         ),
         name="fold",
-    )(place, weight)
+    )(weight)
 
 
 def weigh_kernel(depth, band, pieces, above, row_start, block_rows, chunk_rows, scale, weight_ref, *refs):
@@ -457,25 +498,14 @@
     band = cells // count
     sources = data_weight.shape[0]
     per = local // UNIT
-    slab = lax.axis_index("cells")
-    odd = lax.rem(slab, 2)
-    place = jnp.stack([lax.axis_index("src"), slab * (depth * cells), odd]).astype(jnp.int32)
-    own = jnp.swapaxes(prev_fields, 0, 1)
-    bottom, top = jnp.int32(0), jnp.int32(depth - HALO)
     halos = []
     for k in range(per):
-        received = []
-        for first, start in (
-            (0, jnp.where(odd == 0, top, bottom)), (1, jnp.where(odd == 0, bottom, top))
-        ):
-            planes = lax.dynamic_slice(own, (start, k * UNIT, 0), (HALO, UNIT, cells))
-            if k == 0:
-                sigma = lax.dynamic_slice_in_dim(conductivity, start, HALO, axis=0)
-                planes = jnp.concatenate([planes, split(sigma)], axis=1)
-            received.append(lax.ppermute(planes, "cells", pairs_of("cells", first)))
-        halos.append(received)
-    coefs = stencil_coefficients(place, conductivity, *halos[0], depth * lax.axis_size("cells"))
-    weight = fold(place, data_weight, count, per)
+        own, inner, outer = pack(prev_fields, conductivity, k)
+        outer = lax.ppermute(outer, "cells", pairs_of("cells", 1))
+        inner = lax.ppermute(inner, "cells", pairs_of("cells", 0))
+        halos.append((own, inner, outer))
+    coefs = stencil_coefficients(conductivity, *halos[0][1:], depth * lax.axis_size("cells"))
+    weight = fold(data_weight, count, per)
     down = [(i + 1, i) for i in range(lax.axis_size("cells") - 1)]
     stops = [stop for stop in (per - 2, per - 1, per) if stop > 0]
     potentials = None
@@ -484,7 +514,7 @@
     done = 0
     for k in range(per):
         potentials, kept, *sent = sweep(
-            place, own, *halos[k], coefs, electrodes, potentials, k * UNIT, UNIT, count, band
+            *halos[k], coefs, electrodes, potentials, local, k * UNIT, count, band
         )
         pieces.append(kept)
         for r in range(1, count):
@@ -506,7 +536,7 @@
             1.0 / sources if stop == per else None,
         )
         done = stop
-    return (jnp.swapaxes(potentials, 0, 1), sums)
+    return (potentials, sums)
 
 
 def solution(mesh):

time: 131 us -> 124 us (0.947)
  the two profiles are of different devices: /device:TPU:17 before, /device:TPU:1 now
where the time goes in v2:
time: 124 us; the launch traced here: 122 us
  Pallas kernels  72.2 us (58%)
  starting transfers between devices  24.9 us (20%)
  waiting for transfers between devices  23.2 us (19%)
    pallas_call x4, Pallas kernels, sweep(): pl.pallas_call(functools.partial(sweep_kernel, count, band), grid=(size /...  35.4 us
    pallas_call x3, Pallas kernels, weigh(): pl.pallas_call(functools.partial(weigh_kernel, depth, band, len(pieces),...  19.2 us
    ppermute x4, waiting for transfers between devices, body(): outer = lax.ppermute(outer, 'cells', pairs_of('cells', 1))  15.8 us
    ppermute x4, starting transfers between devices, body(): outer = lax.ppermute(outer, 'cells', pairs_of('cells', 1))  15.5 us
    pallas_call x4, Pallas kernels, pack(): pl.pallas_call(functools.partial(pack_kernel, extra), grid=(steps,), in_s...  14.7 us
    ppermute x4, waiting for transfers between devices, body(): pieces.append(lax.ppermute(sent[r - 1], 'src', pairs))  7.35 us
    ppermute x3, starting transfers between devices, body(): above.append(lax.ppermute(lowest, 'cells', down))  5.94 us
    ppermute x4, starting transfers between devices, body(): pieces.append(lax.ppermute(sent[r - 1], 'src', pairs))  2.94 us
  transfers between devices with their start and end apart: 15, of which 3 were waited for; matrix products, arithmetic and copies ran while one was open for 1% of the time, Pallas kernels for 51%

profile of v2, /device:TPU:1, one launch (start us, length us, event | category | flops | bytes accessed | tf_op | source)
XLA Modules:
  0.0 122.4 jit_solution(12078056400536479582)
XLA Ops:
  0.6 3.8 %pack.7 = (bf16[4,128,1024]{2,1,0:T(8,128)(2,1)}, bf16[2,128,1024]{2,1,0:T(8,128)(2,1)}, bf16[2,128,1024]{2,1,0:T(8,128)(2,1)}) custom-call(bf16[512,4,1024]{2,1,0:T(4,128)(2,1)} %fields_ref.7, f32[4,1024]{1,0:T(4,128)} %sigma_ref.9), custom_call_target="tpu_custom_call" | custom-call | tf_op jit(solution)/shard_map/pack/pallas_call | solution.py:137
  4.5 3.2 %pack.5 = (bf16[4,128,1024]{2,1,0:T(8,128)(2,1)}, bf16[2,144,1024]{2,1,0:T(8,128)(2,1)}, bf16[2,144,1024]{2,1,0:T(8,128)(2,1)}) custom-call(bf16[512,4,1024]{2,1,0:T(4,128)(2,1)} %fields_ref.7, f32[4,1024]{1,0:T(4,128)} %sigma_ref.9), custom_call_target="tpu_custom_call" | custom-call | tf_op jit(solution)/shard_map/pack/pallas_call | solution.py:137
  8.2 4.5 %collective-permute-start.3 = (bf16[2,144,1024]{2,1,0:T(8,128)(2,1)}, bf16[2,144,1024]{2,1,0:T(8,128)(2,1)S(1)}, u32[]{:S(2)}, u32[]{:S(2)}) collective-permute-start(bf16[2,144,1024]{2,1,0:T(8,128)(2,1)} %get-tuple-element.30), channel_id=1, source_target_pairs={{2,4},{6,8},{10,12},{14,16},{18,20},{22,24},{26,28},{4,2},{8,6},{1... | collective-permute-start | bytes 1769480 | tf_op jit(solution)/shard_map/ppermute | solution.py:504
  12.7 2.1 %collective-permute-start.7 = (bf16[2,128,1024]{2,1,0:T(8,128)(2,1)}, bf16[2,128,1024]{2,1,0:T(8,128)(2,1)}, u32[]{:S(2)}, u32[]{:S(2)}) collective-permute-start(bf16[2,128,1024]{2,1,0:T(8,128)(2,1)} %get-tuple-element.36), channel_id=1, source_target_pairs={{2,4},{6,8},{10,12},{14,16},{18,20},{22,24},{26,28},{4,2},{8,6},{1... | collective-permute-start | bytes 1572872 | tf_op jit(solution)/shard_map/ppermute | solution.py:504
  14.7 3.9 %pack.6 = (bf16[4,128,1024]{2,1,0:T(8,128)(2,1)}, bf16[2,128,1024]{2,1,0:T(8,128)(2,1)}, bf16[2,128,1024]{2,1,0:T(8,128)(2,1)}) custom-call(bf16[512,4,1024]{2,1,0:T(4,128)(2,1)} %fields_ref.7, f32[4,1024]{1,0:T(4,128)} %sigma_ref.9), custom_call_target="tpu_custom_call" | custom-call | tf_op jit(solution)/shard_map/pack/pallas_call | solution.py:137
  18.7 4.6 %collective-permute-start.5 = (bf16[2,128,1024]{2,1,0:T(8,128)(2,1)}, bf16[2,128,1024]{2,1,0:T(8,128)(2,1)}, u32[]{:S(2)}, u32[]{:S(2)}) collective-permute-start(bf16[2,128,1024]{2,1,0:T(8,128)(2,1)} %get-tuple-element.33), channel_id=1, source_target_pairs={{2,4},{6,8},{10,12},{14,16},{18,20},{22,24},{26,28},{4,2},{8,6},{1... | collective-permute-start | bytes 1572872 | tf_op jit(solution)/shard_map/ppermute | solution.py:504
  23.3 3.8 %pack.4 = (bf16[4,128,1024]{2,1,0:T(8,128)(2,1)}, bf16[2,128,1024]{2,1,0:T(8,128)(2,1)}, bf16[2,128,1024]{2,1,0:T(8,128)(2,1)}) custom-call(bf16[512,4,1024]{2,1,0:T(4,128)(2,1)} %fields_ref.7, f32[4,1024]{1,0:T(4,128)} %sigma_ref.9), custom_call_target="tpu_custom_call" | custom-call | tf_op jit(solution)/shard_map/pack/pallas_call | solution.py:137
  27.2 15.8 %collective-permute-done.3.outer_ref = bf16[2,144,1024]{2,1,0:T(8,128)(2,1)S(1)} collective-permute-done((bf16[2,144,1024]{2,1,0:T(8,128)(2,1)}, bf16[2,144,1024]{2,1,0:T(8,128)(2,1)S(1)}, u32[]{:S(2)}, u32[]{:S(2)}) %collective-permute-start.3) | collective-permute-done | bytes 589856 | tf_op jit(solution)/shard_map/ppermute | solution.py:504
  43.0 4.3 %collective-permute-start.1 = (bf16[2,128,1024]{2,1,0:T(8,128)(2,1)}, bf16[2,128,1024]{2,1,0:T(8,128)(2,1)}, u32[]{:S(2)}, u32[]{:S(2)}) collective-permute-start(bf16[2,128,1024]{2,1,0:T(8,128)(2,1)} %get-tuple-element.28), channel_id=1, source_target_pairs={{2,4},{6,8},{10,12},{14,16},{18,20},{22,24},{26,28},{4,2},{8,6},{1... | collective-permute-start | bytes 1572872 | tf_op jit(solution)/shard_map/ppermute | solution.py:504
  48.4 8.2 %sweep.4 = (bf16[512,4,1024]{2,1,0:T(4,128)(2,1)}, bf16[128,2176]{1,0:T(8,128)(2,1)S(1)}, bf16[128,2176]{1,0:T(8,128)(2,1)S(1)}) custom-call(bf16[4,128,1024]{2,1,0:T(8,128)(2,1)S(1)} %copy-done.4, bf16[2,144,1024]{2,1,0:T(8,128)(2,1)S(1)} %collective-permute-done.2.inner_ref, bf16[2,144,1024]{2,1,0:T(8,128)(2,1)S(1)} %collective-permute-done.3.outer_ref, ...), custom_call_target="tpu_custom_call" | custom-call | flops 31457280 | bytes 4194304 | tf_op jit(solution)/shard_map/sweep/pallas_call | solution.py:308
  56.6 9.0 %sweep.5 = (bf16[512,4,1024]{2,1,0:T(4,128)(2,1)}, bf16[128,2176]{1,0:T(8,128)(2,1)S(1)}, bf16[128,2176]{1,0:T(8,128)(2,1)S(1)}) custom-call(bf16[4,128,1024]{2,1,0:T(8,128)(2,1)S(1)} %copy-done.3, bf16[2,128,1024]{2,1,0:T(8,128)(2,1)S(1)} %copy-done.6, bf16[2,128,1024]{2,1,0:T(8,128)(2,1)} %collective-permute-done.7.outer_ref, ...), custom_call_target="tpu_custom_call", output_to_operand_aliasing={{0}: (5, {})} | custom-call | flops 31457280 | bytes 4194304 | tf_op jit(solution)/shard_map/sweep/pallas_call | solution.py:308
  65.6 1.3 %collective-permute-start.9 = (bf16[128,2176]{1,0:T(8,128)(2,1)S(1)}, bf16[128,2176]{1,0:T(8,128)(2,1)S(1)}, u32[]{:S(2)}, u32[]{:S(2)}) collective-permute-start(bf16[128,2176]{1,0:T(8,128)(2,1)S(1)} %get-tuple-element.45), channel_id=1, source_target_pairs={{0,1},{1,0},{2,3},{3,2},{4,5},{5,4},{6,7},{7,6},{8,9},{9,8},{10,11... | collective-permute-start | bytes 1671176 | tf_op jit(solution)/shard_map/ppermute | solution.py:522
  67.0 9.0 %sweep.6 = (bf16[512,4,1024]{2,1,0:T(4,128)(2,1)}, bf16[128,2176]{1,0:T(8,128)(2,1)S(1)}, bf16[128,2176]{1,0:T(8,128)(2,1)S(1)}) custom-call(bf16[4,128,1024]{2,1,0:T(8,128)(2,1)S(1)} %copy-done.2, bf16[2,128,1024]{2,1,0:T(8,128)(2,1)} %collective-permute-done.4.inner_ref, ...), custom_call_target="tpu_custom_call", output_to_operand_aliasing={{0}: (5, {})} | custom-call | flops 31457280 | bytes 4194304 | tf_op jit(solution)/shard_map/sweep/pallas_call | solution.py:308
  76.1 1.3 %collective-permute-start.10 = (bf16[128,2176]{1,0:T(8,128)(2,1)S(1)}, bf16[128,2176]{1,0:T(8,128)(2,1)S(1)}, u32[]{:S(2)}, u32[]{:S(2)}) collective-permute-start(bf16[128,2176]{1,0:T(8,128)(2,1)S(1)} %get-tuple-element.47), channel_id=1, source_target_pairs={{0,1},{1,0},{2,3},{3,2},{4,5},{5,4},{6,7},{7,6},{8,9},{9,8},{10,11... | collective-permute-start | bytes 1671176 | tf_op jit(solution)/shard_map/ppermute | solution.py:522
  77.3 9.2 %sweep.7 = (bf16[512,4,1024]{2,1,0:T(4,128)(2,1)}, bf16[128,2176]{1,0:T(8,128)(2,1)S(1)}, bf16[128,2176]{1,0:T(8,128)(2,1)S(1)}) custom-call(bf16[4,128,1024]{2,1,0:T(8,128)(2,1)S(1)} %copy-done.1, bf16[2,128,1024]{2,1,0:T(8,128)(2,1)} %collective-permute-done.inner_ref, ...), custom_call_target="tpu_custom_call", output_to_operand_aliasing={{0}: (5, {})} | custom-call | flops 31457280 | bytes 4194304 | tf_op jit(solution)/shard_map/sweep/pallas_call | solution.py:308
  86.8 1.9 %collective-permute-start.12 = (bf16[512,512]{1,0:T(8,128)(2,1)S(1)}, bf16[512,512]{1,0:T(8,128)(2,1)S(1)}, u32[]{:S(2)}, u32[]{:S(2)}) collective-permute-start(bf16[512,512]{1,0:T(8,128)(2,1)S(1)} %pad_maximum_fusion), channel_id=1, source_target_pairs={{2,0},{4,2},{6,4},{8,6},{10,8},{12,10},{14,12},{16,14},{18,16},{20... | collective-permute-start | bytes 1572872 | tf_op jit(solution)/shard_map/ppermute | solution.py:525
  88.8 3.4 %collective-permute-done.10.refs_5_ = bf16[128,2176]{1,0:T(8,128)(2,1)S(1)} collective-permute-done((bf16[128,2176]{1,0:T(8,128)(2,1)S(1)}, bf16[128,2176]{1,0:T(8,128)(2,1)S(1)}, u32[]{:S(2)}, u32[]{:S(2)}) %collective-permute-start.10) | collective-permute-done | bytes 557088 | tf_op jit(solution)/shard_map/ppermute | solution.py:522
  92.2 1.9 %collective-permute-start.13 = (bf16[256,512]{1,0:T(8,128)(2,1)S(1)}, bf16[256,512]{1,0:T(8,128)(2,1)S(1)}, u32[]{:S(2)}, u32[]{:S(2)}) collective-permute-start(bf16[256,512]{1,0:T(8,128)(2,1)S(1)} %pad_maximum_fusion.1), channel_id=1, source_target_pairs={{2,0},{4,2},{6,4},{8,6},{10,8},{12,10},{14,12},{16,14},{18,16},{20... | collective-permute-start | bytes 786440 | tf_op jit(solution)/shard_map/ppermute | solution.py:525
  94.1 4.0 %collective-permute-done.11.refs_7_ = bf16[128,2176]{1,0:T(8,128)(2,1)S(1)} collective-permute-done((bf16[128,2176]{1,0:T(8,128)(2,1)S(1)}, bf16[128,2176]{1,0:T(8,128)(2,1)S(1)}, u32[]{:S(2)}, u32[]{:S(2)}) %collective-permute-start.11) | collective-permute-done | bytes 557088 | tf_op jit(solution)/shard_map/ppermute | solution.py:522
  98.2 2.1 %collective-permute-start.14 = (bf16[256,512]{1,0:T(8,128)(2,1)S(1)}, bf16[256,512]{1,0:T(8,128)(2,1)S(1)}, u32[]{:S(2)}, u32[]{:S(2)}) collective-permute-start(bf16[256,512]{1,0:T(8,128)(2,1)S(1)} %pad_maximum_fusion.2), channel_id=1, source_target_pairs={{2,0},{4,2},{6,4},{8,6},{10,8},{12,10},{14,12},{16,14},{18,16},{20... | collective-permute-start | bytes 786440 | tf_op jit(solution)/shard_map/ppermute | solution.py:525
  100.3 2.7 %fold.1.weight_ref = bf16[1024,1024]{1,0:T(8,128)(2,1)S(1)} custom-call(bf16[1024,1024]{1,0:T(8,128)(2,1)S(1)} %copy-done), custom_call_target="tpu_custom_call" | custom-call | flops 1048576 | bytes 4194304 | tf_op jit(solution)/shard_map/fold/pallas_call | solution.py:368
  103.0 8.2 %weigh.3.refs_8_ = f32[32,512]{1,0:T(8,128)S(1)} custom-call(bf16[1024,1024]{1,0:T(8,128)(2,1)S(1)} %fold.1.weight_ref, bf16[128,2176]{1,0:T(8,128)(2,1)S(1)} %get-tuple-element.42.refs_0_, bf16[128,2176]{1,0:T(8,128)(2,1)S(1)} %collective-permute-done.8.refs_1_, bf16[128,2176]{1,0:T(8,128)(2,1)S(1)} %get-tuple-element.44.refs_2_, ...), custom_call_target="tpu_custom_call" | custom-call | flops 1409286144 | bytes 2752512 | tf_op jit(solution)/shard_map/weigh/pallas_call | solution.py:471
  111.2 4.9 %weigh.4.refs_11_ = f32[32,512]{1,0:T(8,128)S(1)} custom-call(bf16[1024,1024]{1,0:T(8,128)(2,1)S(1)} %fold.1.weight_ref, bf16[128,2176]{1,0:T(8,128)(2,1)S(1)} %get-tuple-element.42.refs_0_, bf16[128,2176]{1,0:T(8,128)(2,1)S(1)} %collective-permute-done.8.refs_1_, bf16[128,2176]{1,0:T(8,128)(2,1)S(1)} %get-tuple-element.44.refs_2_, ...), custom_call_target="tpu_custom_call" | custom-call | flops 1056964608 | bytes 4128768 | tf_op jit(solution)/shard_map/weigh/pallas_call | solution.py:471
  116.1 6.1 %weigh.5 = f32[4,512]{1,0:T(4,128)} custom-call(bf16[1024,1024]{1,0:T(8,128)(2,1)S(1)} %fold.1.weight_ref, bf16[128,2176]{1,0:T(8,128)(2,1)S(1)} %get-tuple-element.42.refs_0_, bf16[128,2176]{1,0:T(8,128)(2,1)S(1)} %collective-permute-done.8.refs_1_, bf16[128,2176]{1,0:T(8,128)(2,1)S(1)} %get-tuple-element.44.refs_2_, ...), custom_call_target="tpu_custom_call" | custom-call | flops 1409286144 | bytes 5505024 | tf_op jit(solution)/shard_map/weigh/pallas_call | solution.py:471
  (48 shorter events, 2.2 us)
Async XLA Ops:
  4.5 14.2 %collective-permute-start.6 = (bf16[2,128,1024]{2,1,0:T(8,128)(2,1)}, bf16[2,128,1024]{2,1,0:T(8,128)(2,1)S(1)}, u32[]{:S(2)}, u32[]{:S(2)}) collective-permute-start(bf16[2,128,1024]{2,1,0:T(8,128)(2,1)} %get-tuple-element.35), channel_id=1, source_target_pairs={{0,2},{4,6},{8,10},{12,14},{16,18},{20,22},{24,26},{28,30},{2,0},{... | collective-permute-start | bytes 1572872 | tf_op jit(solution)/shard_map/ppermute | solution.py:505
  7.7 19.5 %collective-permute-start.2 = (bf16[2,144,1024]{2,1,0:T(8,128)(2,1)}, bf16[2,144,1024]{2,1,0:T(8,128)(2,1)S(1)}, u32[]{:S(2)}, u32[]{:S(2)}) collective-permute-start(bf16[2,144,1024]{2,1,0:T(8,128)(2,1)} %get-tuple-element.29), channel_id=1, source_target_pairs={{0,2},{4,6},{8,10},{12,14},{16,18},{20,22},{24,26},{28,30},{2,0},{... | collective-permute-start | bytes 1769480 | tf_op jit(solution)/shard_map/ppermute | solution.py:505
  8.2 34.8 %collective-permute-start.3 = (bf16[2,144,1024]{2,1,0:T(8,128)(2,1)}, bf16[2,144,1024]{2,1,0:T(8,128)(2,1)S(1)}, u32[]{:S(2)}, u32[]{:S(2)}) collective-permute-start(bf16[2,144,1024]{2,1,0:T(8,128)(2,1)} %get-tuple-element.30), channel_id=1, source_target_pairs={{2,4},{6,8},{10,12},{14,16},{18,20},{22,24},{26,28},{4,2},{8,6},{1... | collective-permute-start | bytes 1769480 | tf_op jit(solution)/shard_map/ppermute | solution.py:504
  12.7 35.4 %copy-start.7 = (f32[4,1024]{1,0:T(4,128)S(1)}, f32[4,1024]{1,0:T(4,128)}, u32[]{:S(2)}) copy-start(f32[4,1024]{1,0:T(4,128)} %sigma_ref.9) | copy-start | bytes 49156
  12.7 35.7 %copy-start.4 = (bf16[4,128,1024]{2,1,0:T(8,128)(2,1)S(1)}, bf16[4,128,1024]{2,1,0:T(8,128)(2,1)}, u32[]{:S(2)}) copy-start(bf16[4,128,1024]{2,1,0:T(8,128)(2,1)} %get-tuple-element.37.own_ref) | copy-start | bytes 3145732
  12.7 43.9 %collective-permute-start.7 = (bf16[2,128,1024]{2,1,0:T(8,128)(2,1)}, bf16[2,128,1024]{2,1,0:T(8,128)(2,1)}, u32[]{:S(2)}, u32[]{:S(2)}) collective-permute-start(bf16[2,128,1024]{2,1,0:T(8,128)(2,1)} %get-tuple-element.36), channel_id=1, source_target_pairs={{2,4},{6,8},{10,12},{14,16},{18,20},{22,24},{26,28},{4,2},{8,6},{1... | collective-permute-start | bytes 1572872 | tf_op jit(solution)/shard_map/ppermute | solution.py:504
  18.6 48.2 %collective-permute-start.4 = (bf16[2,128,1024]{2,1,0:T(8,128)(2,1)}, bf16[2,128,1024]{2,1,0:T(8,128)(2,1)}, u32[]{:S(2)}, u32[]{:S(2)}) collective-permute-start(bf16[2,128,1024]{2,1,0:T(8,128)(2,1)} %get-tuple-element.32), channel_id=1, source_target_pairs={{0,2},{4,6},{8,10},{12,14},{16,18},{20,22},{24,26},{28,30},{2,0},{... | collective-permute-start | bytes 1572872 | tf_op jit(solution)/shard_map/ppermute | solution.py:505
  18.6 24.3 %copy-start.5 = (bf16[2,128,1024]{2,1,0:T(8,128)(2,1)}, bf16[2,128,1024]{2,1,0:T(8,128)(2,1)S(1)}, u32[]{:S(2)}) copy-start(bf16[2,128,1024]{2,1,0:T(8,128)(2,1)S(1)} %collective-permute-done.6.inner_ref) | copy-start | bytes 1572868
  18.6 38.0 %copy-start.3 = (bf16[4,128,1024]{2,1,0:T(8,128)(2,1)S(1)}, bf16[4,128,1024]{2,1,0:T(8,128)(2,1)}, u32[]{:S(2)}) copy-start(bf16[4,128,1024]{2,1,0:T(8,128)(2,1)} %get-tuple-element.34.own_ref) | copy-start | bytes 3145732
  18.7 48.4 %collective-permute-start.5 = (bf16[2,128,1024]{2,1,0:T(8,128)(2,1)}, bf16[2,128,1024]{2,1,0:T(8,128)(2,1)}, u32[]{:S(2)}, u32[]{:S(2)}) collective-permute-start(bf16[2,128,1024]{2,1,0:T(8,128)(2,1)} %get-tuple-element.33), channel_id=1, source_target_pairs={{2,4},{6,8},{10,12},{14,16},{18,20},{22,24},{26,28},{4,2},{8,6},{1... | collective-permute-start | bytes 1572872 | tf_op jit(solution)/shard_map/ppermute | solution.py:504
  27.2 50.2 %collective-permute-start = (bf16[2,128,1024]{2,1,0:T(8,128)(2,1)}, bf16[2,128,1024]{2,1,0:T(8,128)(2,1)}, u32[]{:S(2)}, u32[]{:S(2)}) collective-permute-start(bf16[2,128,1024]{2,1,0:T(8,128)(2,1)} %get-tuple-element.27), channel_id=1, source_target_pairs={{0,2},{4,6},{8,10},{12,14},{16,18},{20,22},{24,26},{28,30},{2,0},{... | collective-permute-start | bytes 1572872 | tf_op jit(solution)/shard_map/ppermute | solution.py:505
  43.0 34.4 %collective-permute-start.1 = (bf16[2,128,1024]{2,1,0:T(8,128)(2,1)}, bf16[2,128,1024]{2,1,0:T(8,128)(2,1)}, u32[]{:S(2)}, u32[]{:S(2)}) collective-permute-start(bf16[2,128,1024]{2,1,0:T(8,128)(2,1)} %get-tuple-element.28), channel_id=1, source_target_pairs={{2,4},{6,8},{10,12},{14,16},{18,20},{22,24},{26,28},{4,2},{8,6},{1... | collective-permute-start | bytes 1572872 | tf_op jit(solution)/shard_map/ppermute | solution.py:504
  48.1 8.5 %copy-start.6 = (bf16[2,128,1024]{2,1,0:T(8,128)(2,1)S(1)}, bf16[2,128,1024]{2,1,0:T(8,128)(2,1)}, u32[]{:S(2)}) copy-start(bf16[2,128,1024]{2,1,0:T(8,128)(2,1)} %copy-done.5) | copy-start | bytes 1572868
  48.4 18.7 %copy-start.2 = (bf16[4,128,1024]{2,1,0:T(8,128)(2,1)S(1)}, bf16[4,128,1024]{2,1,0:T(8,128)(2,1)}, u32[]{:S(2)}) copy-start(bf16[4,128,1024]{2,1,0:T(8,128)(2,1)} %get-tuple-element.31.own_ref) | copy-start | bytes 3145732
  65.6 11.8 %copy-start.1 = (bf16[4,128,1024]{2,1,0:T(8,128)(2,1)S(1)}, bf16[4,128,1024]{2,1,0:T(8,128)(2,1)}, u32[]{:S(2)}) copy-start(bf16[4,128,1024]{2,1,0:T(8,128)(2,1)} %get-tuple-element.26.own_ref) | copy-start | bytes 3145732
  65.6 21.2 %collective-permute-start.9 = (bf16[128,2176]{1,0:T(8,128)(2,1)S(1)}, bf16[128,2176]{1,0:T(8,128)(2,1)S(1)}, u32[]{:S(2)}, u32[]{:S(2)}) collective-permute-start(bf16[128,2176]{1,0:T(8,128)(2,1)S(1)} %get-tuple-element.45), channel_id=1, source_target_pairs={{0,1},{1,0},{2,3},{3,2},{4,5},{5,4},{6,7},{7,6},{8,9},{9,8},{10,11... | collective-permute-start | bytes 1671176 | tf_op jit(solution)/shard_map/ppermute | solution.py:522
  66.8 19.9 %collective-permute-start.8 = (bf16[128,2176]{1,0:T(8,128)(2,1)S(1)}, bf16[128,2176]{1,0:T(8,128)(2,1)S(1)}, u32[]{:S(2)}, u32[]{:S(2)}) collective-permute-start(bf16[128,2176]{1,0:T(8,128)(2,1)S(1)} %get-tuple-element.43), channel_id=1, source_target_pairs={{0,1},{1,0},{2,3},{3,2},{4,5},{5,4},{6,7},{7,6},{8,9},{9,8},{10,11... | collective-permute-start | bytes 1671176 | tf_op jit(solution)/shard_map/ppermute | solution.py:522
  76.1 16.1 %collective-permute-start.10 = (bf16[128,2176]{1,0:T(8,128)(2,1)S(1)}, bf16[128,2176]{1,0:T(8,128)(2,1)S(1)}, u32[]{:S(2)}, u32[]{:S(2)}) collective-permute-start(bf16[128,2176]{1,0:T(8,128)(2,1)S(1)} %get-tuple-element.47), channel_id=1, source_target_pairs={{0,1},{1,0},{2,3},{3,2},{4,5},{5,4},{6,7},{7,6},{8,9},{9,8},{10,11... | collective-permute-start | bytes 1671176 | tf_op jit(solution)/shard_map/ppermute | solution.py:522
  77.3 22.9 %copy-start = (bf16[1024,1024]{1,0:T(8,128)(2,1)S(1)}, bf16[1024,1024]{1,0:T(8,128)(2,1)}, u32[]{:S(2)}) copy-start(bf16[1024,1024]{1,0:T(8,128)(2,1)} %weight_ref.1) | copy-start | bytes 6291460
  86.5 11.6 %collective-permute-start.11 = (bf16[128,2176]{1,0:T(8,128)(2,1)S(1)}, bf16[128,2176]{1,0:T(8,128)(2,1)S(1)}, u32[]{:S(2)}, u32[]{:S(2)}) collective-permute-start(bf16[128,2176]{1,0:T(8,128)(2,1)S(1)} %get-tuple-element.49), channel_id=1, source_target_pairs={{0,1},{1,0},{2,3},{3,2},{4,5},{5,4},{6,7},{7,6},{8,9},{9,8},{10,11... | collective-permute-start | bytes 1671176 | tf_op jit(solution)/shard_map/ppermute | solution.py:522
  86.8 16.1 %collective-permute-start.12 = (bf16[512,512]{1,0:T(8,128)(2,1)S(1)}, bf16[512,512]{1,0:T(8,128)(2,1)S(1)}, u32[]{:S(2)}, u32[]{:S(2)}) collective-permute-start(bf16[512,512]{1,0:T(8,128)(2,1)S(1)} %pad_maximum_fusion), channel_id=1, source_target_pairs={{2,0},{4,2},{6,4},{8,6},{10,8},{12,10},{14,12},{16,14},{18,16},{20... | collective-permute-start | bytes 1572872 | tf_op jit(solution)/shard_map/ppermute | solution.py:525
  92.2 19.0 %collective-permute-start.13 = (bf16[256,512]{1,0:T(8,128)(2,1)S(1)}, bf16[256,512]{1,0:T(8,128)(2,1)S(1)}, u32[]{:S(2)}, u32[]{:S(2)}) collective-permute-start(bf16[256,512]{1,0:T(8,128)(2,1)S(1)} %pad_maximum_fusion.1), channel_id=1, source_target_pairs={{2,0},{4,2},{6,4},{8,6},{10,8},{12,10},{14,12},{16,14},{18,16},{20... | collective-permute-start | bytes 786440 | tf_op jit(solution)/shard_map/ppermute | solution.py:525
  98.2 18.0 %collective-permute-start.14 = (bf16[256,512]{1,0:T(8,128)(2,1)S(1)}, bf16[256,512]{1,0:T(8,128)(2,1)S(1)}, u32[]{:S(2)}, u32[]{:S(2)}) collective-permute-start(bf16[256,512]{1,0:T(8,128)(2,1)S(1)} %pad_maximum_fusion.2), channel_id=1, source_target_pairs={{2,0},{4,2},{6,4},{8,6},{10,8},{12,10},{14,12},{16,14},{18,16},{20... | collective-permute-start | bytes 786440 | tf_op jit(solution)/shard_map/ppermute | solution.py:525

commit v3 on v2

--- a/solution.py
+++ b/solution.py
@@ -95,10 +95,10 @@
     )(conductivity, inner, outer)
 
 
-def pack_kernel(extra, fields_ref, sigma_ref, own_ref, inner_ref, outer_ref):
+def pack_kernel(extra, fields_ref, sigma_ref, inner_ref, outer_ref):
     rows, depth, cells = fields_ref.shape
     odd = lax.rem(lax.axis_index("cells"), 2)
-    own_ref[...] = jnp.swapaxes(fields_ref[...].astype(jnp.float32), 0, 1).astype(jnp.bfloat16)
+    turned = jnp.swapaxes(fields_ref[...].astype(jnp.float32), 0, 1).astype(jnp.bfloat16)
 
     def part(plane):
         rest = jnp.broadcast_to(sigma_ref[plane : plane + 1, :], (PART, cells))
@@ -111,7 +111,7 @@
         return parts.astype(jnp.bfloat16)
 
     def pick(out_ref, start):
-        out_ref[:, 0:rows] = own_ref[start : start + HALO]
+        out_ref[:, 0:rows] = turned[start : start + HALO]
         if extra:
             for i in range(HALO):
                 out_ref[i, rows : rows + PART, :] = part(start + i)
@@ -141,10 +141,8 @@
             pl.BlockSpec((rows, depth, cells), lambda i: (i + k * steps, 0, 0)),
             pl.BlockSpec((depth, cells), lambda i: (0, 0)),
         ],
-        out_specs=[pl.BlockSpec((depth, rows, cells), lambda i: (0, i, 0))]
-        + [pl.BlockSpec((HALO, block, cells), lambda i: (0, i, 0))] * 2,
-        out_shape=[jax.ShapeDtypeStruct((depth, UNIT, cells), jnp.bfloat16)]
-        + [jax.ShapeDtypeStruct((HALO, sent, cells), jnp.bfloat16)] * 2,
+        out_specs=[pl.BlockSpec((HALO, block, cells), lambda i: (0, i, 0))] * 2,
+        out_shape=[jax.ShapeDtypeStruct((HALO, sent, cells), jnp.bfloat16)] * 2,
         compiler_params=pltpu.CompilerParams(vmem_limit_bytes=60 * 2**20),
         name="pack",
     )(fields, conductivity)
@@ -158,11 +156,12 @@
     refs = refs[-(count + 6) :]
     pot_ref, outs, (first, second, extra, final) = refs[0], refs[1 : count + 1], refs[count + 1 : count + 5]
     elec_b = refs[count + 5]
-    depth, rows, cells = own_ref.shape
+    rows, depth, cells = own_ref.shape
     slab = lax.axis_index("cells")
     odd = lax.rem(slab, 2)
     tiles = cells // LANES
-    first[HALO : HALO + depth] = own_ref[...]
+    turned = jnp.swapaxes(own_ref[...].astype(jnp.float32), 0, 1)
+    first[HALO : HALO + depth] = turned.astype(jnp.bfloat16)
 
     @pl.when(odd == 0)
     def _():
@@ -287,18 +286,18 @@
     return -(-depth * NY // LANES) * LANES
 
 
-def sweep(own, inner, outer, coefs, electrodes, before, total, begin, count, band):
-    depth, size, cells = own.shape
+def sweep(fields, inner, outer, coefs, electrodes, before, begin, size, count, band):
+    total, depth, cells = fields.shape
     width = depth * band + beside_width(depth)
     block = begin // ROWS
     in_specs = [
-        pl.BlockSpec((depth, ROWS, cells), lambda i: (0, i, 0)),
+        pl.BlockSpec((ROWS, depth, cells), lambda i: (i + block, 0, 0)),
         pl.BlockSpec((HALO, ROWS, cells), lambda i: (0, i, 0)),
         pl.BlockSpec((HALO, ROWS, cells), lambda i: (0, i, 0)),
         pl.BlockSpec(coefs.shape, lambda i: (0, 0, 0)),
         pl.BlockSpec((ROWS, 2), lambda i: (i + block, 0)),
     ]
-    args = [own, inner, outer, coefs, electrodes]
+    args = [fields, inner, outer, coefs, electrodes]
     aliases = {}
     if before is not None:
         in_specs.append(pl.BlockSpec(memory_space=pl.ANY))
@@ -321,7 +320,7 @@
         out_shape=[jax.ShapeDtypeStruct((total, depth, cells), jnp.bfloat16)]
         + [jax.ShapeDtypeStruct((size, width), jnp.bfloat16)] * count,
         input_output_aliases=aliases,
-        compiler_params=pltpu.CompilerParams(vmem_limit_bytes=44 * 2**20),
+        compiler_params=pltpu.CompilerParams(vmem_limit_bytes=60 * 2**20),
         cost_estimate=pl.CostEstimate(
             flops=size * cells * planes * 40,
             bytes_accessed=size * cells * 2 * (3 * depth + 2 * HALO),
@@ -500,11 +499,11 @@
     per = local // UNIT
     halos = []
     for k in range(per):
-        own, inner, outer = pack(prev_fields, conductivity, k)
+        inner, outer = pack(prev_fields, conductivity, k)
         outer = lax.ppermute(outer, "cells", pairs_of("cells", 1))
         inner = lax.ppermute(inner, "cells", pairs_of("cells", 0))
-        halos.append((own, inner, outer))
-    coefs = stencil_coefficients(conductivity, *halos[0][1:], depth * lax.axis_size("cells"))
+        halos.append((inner, outer))
+    coefs = stencil_coefficients(conductivity, *halos[0], depth * lax.axis_size("cells"))
     weight = fold(data_weight, count, per)
     down = [(i + 1, i) for i in range(lax.axis_size("cells") - 1)]
     stops = [stop for stop in (per - 2, per - 1, per) if stop > 0]
@@ -514,7 +513,7 @@
     done = 0
     for k in range(per):
         potentials, kept, *sent = sweep(
-            *halos[k], coefs, electrodes, potentials, local, k * UNIT, count, band
+            prev_fields, *halos[k], coefs, electrodes, potentials, k * UNIT, UNIT, count, band
         )
         pieces.append(kept)
         for r in range(1, count):

time: 124 us -> 127 us (1.024)
  local copies, waits for them, and re-layouts: 0.95 us -> 4.21 us
  waiting for transfers between devices: 23.2 us -> 20 us
  Pallas kernels: 72.2 us -> 74.9 us
    ppermute x4, waiting for transfers between devices: 7.35 us -> 3.69 us  [body(): pieces.append(lax.ppermute(sent[r - 1], 'src', pairs))]
    pallas_call x4, Pallas kernels: 35.4 us -> 38.6 us  [sweep(): pl.pallas_call(functools.partial(sweep_kernel, count, band), grid=(size /...]
    unnamed x17 -> x29, local copies, waits for them, and re-layouts: 0.87 us -> 3.22 us
  transfers between devices with their start and end apart: 15 -> 15, of which waited for: 3 -> 2; matrix products, arithmetic and copies ran while one was open for 1% -> 2% of each run, Pallas kernels for 51% -> 52%
where the time goes in v3:
time: 127 us; the launch traced here: 125 us
  Pallas kernels  74.9 us (59%)
  starting transfers between devices  24.8 us (20%)
  waiting for transfers between devices  20 us (16%)
  local copies, waits for them, and re-layouts  4.21 us (3%)
    pallas_call x4, Pallas kernels, sweep(): pl.pallas_call(functools.partial(sweep_kernel, count, band), grid=(size /...  38.6 us
    pallas_call x3, Pallas kernels, weigh(): pl.pallas_call(functools.partial(weigh_kernel, depth, band, len(pieces),...  19.2 us
    ppermute x4, waiting for transfers between devices, body(): outer = lax.ppermute(outer, 'cells', pairs_of('cells', 1))  16.3 us
    ppermute x4, starting transfers between devices, body(): outer = lax.ppermute(outer, 'cells', pairs_of('cells', 1))  15.2 us
    pallas_call x4, Pallas kernels, pack(): pl.pallas_call(functools.partial(pack_kernel, extra), grid=(steps,), in_s...  14.2 us
    ppermute x3, starting transfers between devices, body(): above.append(lax.ppermute(lowest, 'cells', down))  6.07 us
    ppermute x4, waiting for transfers between devices, body(): pieces.append(lax.ppermute(sent[r - 1], 'src', pairs))  3.69 us
    unnamed x29, local copies, waits for them, and re-layouts  3.22 us
  transfers between devices with their start and end apart: 15, of which 2 were waited for; matrix products, arithmetic and copies ran while one was open for 2% of the time, Pallas kernels for 52%

profile of v3, /device:TPU:1, one launch (start us, length us, event | category | flops | bytes accessed | tf_op | source)
XLA Modules:
  0.0 125.1 jit_solution(129615801630877906)
XLA Ops:
  0.6 3.7 %pack.7 = (bf16[2,128,1024]{2,1,0:T(8,128)(2,1)}, bf16[2,128,1024]{2,1,0:T(8,128)(2,1)}) custom-call(bf16[512,4,1024]{2,1,0:T(4,128)(2,1)} %own_ref.7, f32[4,1024]{1,0:T(4,128)} %sigma_ref.9), custom_call_target="tpu_custom_call" | custom-call | tf_op jit(solution)/shard_map/pack/pallas_call | solution.py:137
  4.4 3.0 %pack.5 = (bf16[2,144,1024]{2,1,0:T(8,128)(2,1)}, bf16[2,144,1024]{2,1,0:T(8,128)(2,1)}) custom-call(bf16[512,4,1024]{2,1,0:T(4,128)(2,1)} %own_ref.7, f32[4,1024]{1,0:T(4,128)} %sigma_ref.9), custom_call_target="tpu_custom_call" | custom-call | tf_op jit(solution)/shard_map/pack/pallas_call | solution.py:137
  7.9 4.5 %collective-permute-start.3 = (bf16[2,144,1024]{2,1,0:T(8,128)(2,1)}, bf16[2,144,1024]{2,1,0:T(8,128)(2,1)S(1)}, u32[]{:S(2)}, u32[]{:S(2)}) collective-permute-start(bf16[2,144,1024]{2,1,0:T(8,128)(2,1)} %get-tuple-element.25), channel_id=1, source_target_pairs={{2,4},{6,8},{10,12},{14,16},{18,20},{22,24},{26,28},{4,2},{8,6},{1... | collective-permute-start | bytes 1769480 | tf_op jit(solution)/shard_map/ppermute | solution.py:503
  12.4 1.9 %collective-permute-start.7 = (bf16[2,128,1024]{2,1,0:T(8,128)(2,1)}, bf16[2,128,1024]{2,1,0:T(8,128)(2,1)}, u32[]{:S(2)}, u32[]{:S(2)}) collective-permute-start(bf16[2,128,1024]{2,1,0:T(8,128)(2,1)} %get-tuple-element.29), channel_id=1, source_target_pairs={{2,4},{6,8},{10,12},{14,16},{18,20},{22,24},{26,28},{4,2},{8,6},{1... | collective-permute-start | bytes 1572872 | tf_op jit(solution)/shard_map/ppermute | solution.py:503
  14.3 3.7 %pack.6 = (bf16[2,128,1024]{2,1,0:T(8,128)(2,1)}, bf16[2,128,1024]{2,1,0:T(8,128)(2,1)}) custom-call(bf16[512,4,1024]{2,1,0:T(4,128)(2,1)} %own_ref.7, f32[4,1024]{1,0:T(4,128)} %sigma_ref.9), custom_call_target="tpu_custom_call" | custom-call | tf_op jit(solution)/shard_map/pack/pallas_call | solution.py:137
  18.1 4.5 %collective-permute-start.5 = (bf16[2,128,1024]{2,1,0:T(8,128)(2,1)}, bf16[2,128,1024]{2,1,0:T(8,128)(2,1)S(1)}, u32[]{:S(2)}, u32[]{:S(2)}) collective-permute-start(bf16[2,128,1024]{2,1,0:T(8,128)(2,1)} %get-tuple-element.27), channel_id=1, source_target_pairs={{2,4},{6,8},{10,12},{14,16},{18,20},{22,24},{26,28},{4,2},{8,6},{1... | collective-permute-start | bytes 1572872 | tf_op jit(solution)/shard_map/ppermute | solution.py:503
  22.6 3.7 %pack.4 = (bf16[2,128,1024]{2,1,0:T(8,128)(2,1)}, bf16[2,128,1024]{2,1,0:T(8,128)(2,1)}) custom-call(bf16[512,4,1024]{2,1,0:T(4,128)(2,1)} %own_ref.7, f32[4,1024]{1,0:T(4,128)} %sigma_ref.9), custom_call_target="tpu_custom_call" | custom-call | tf_op jit(solution)/shard_map/pack/pallas_call | solution.py:137
  26.4 16.3 %collective-permute-done.3.outer_ref = bf16[2,144,1024]{2,1,0:T(8,128)(2,1)S(1)} collective-permute-done((bf16[2,144,1024]{2,1,0:T(8,128)(2,1)}, bf16[2,144,1024]{2,1,0:T(8,128)(2,1)S(1)}, u32[]{:S(2)}, u32[]{:S(2)}) %collective-permute-start.3) | collective-permute-done | bytes 589856 | tf_op jit(solution)/shard_map/ppermute | solution.py:503
  42.7 4.3 %collective-permute-start.1 = (bf16[2,128,1024]{2,1,0:T(8,128)(2,1)}, bf16[2,128,1024]{2,1,0:T(8,128)(2,1)}, u32[]{:S(2)}, u32[]{:S(2)}) collective-permute-start(bf16[2,128,1024]{2,1,0:T(8,128)(2,1)} %get-tuple-element.23), channel_id=1, source_target_pairs={{2,4},{6,8},{10,12},{14,16},{18,20},{22,24},{26,28},{4,2},{8,6},{1... | collective-permute-start | bytes 1572872 | tf_op jit(solution)/shard_map/ppermute | solution.py:503
  48.8 9.6 %sweep.4 = (bf16[512,4,1024]{2,1,0:T(4,128)(2,1)}, bf16[128,2176]{1,0:T(8,128)(2,1)}, bf16[128,2176]{1,0:T(8,128)(2,1)}) custom-call(bf16[512,4,1024]{2,1,0:T(4,128)(2,1)} %own_ref.7, bf16[2,144,1024]{2,1,0:T(8,128)(2,1)} %copy-done.4, bf16[2,144,1024]{2,1,0:T(8,128)(2,1)} %copy-done.5, f32[6,8,1024]{2,1,0:T(8,128)} %copy-done, s32[512,2]{1,0:T(8,128)} %copy.12.elec_ref), custom_call_target="tpu_custom_call" | custom-call | flops 31457280 | bytes 4194304 | tf_op jit(solution)/shard_map/sweep/pallas_call | solution.py:307
  58.4 9.6 %sweep.5 = (bf16[512,4,1024]{2,1,0:T(4,128)(2,1)}, bf16[128,2176]{1,0:T(8,128)(2,1)}, bf16[128,2176]{1,0:T(8,128)(2,1)}) custom-call(bf16[512,4,1024]{2,1,0:T(4,128)(2,1)} %own_ref.7, bf16[2,128,1024]{2,1,0:T(8,128)(2,1)} %copy-done.9, bf16[2,128,1024]{2,1,0:T(8,128)(2,1)} %collective-permute-done.7.outer_ref, ...), custom_call_target="tpu_custom_call", output_to_operand_aliasing={{0}: (5, {})} | custom-call | flops 31457280 | bytes 4194304 | tf_op jit(solution)/shard_map/sweep/pallas_call | solution.py:307
  68.1 1.3 %collective-permute-start.9 = (bf16[128,2176]{1,0:T(8,128)(2,1)}, bf16[128,2176]{1,0:T(8,128)(2,1)S(1)}, u32[]{:S(2)}, u32[]{:S(2)}) collective-permute-start(bf16[128,2176]{1,0:T(8,128)(2,1)} %get-tuple-element.37), channel_id=1, source_target_pairs={{0,1},{1,0},{2,3},{3,2},{4,5},{5,4},{6,7},{7,6},{8,9},{9,8},{10,11... | collective-permute-start | bytes 1671176 | tf_op jit(solution)/shard_map/ppermute | solution.py:521
  70.4 9.6 %sweep.6 = (bf16[512,4,1024]{2,1,0:T(4,128)(2,1)}, bf16[128,2176]{1,0:T(8,128)(2,1)}, bf16[128,2176]{1,0:T(8,128)(2,1)}) custom-call(bf16[512,4,1024]{2,1,0:T(4,128)(2,1)} %own_ref.7, bf16[2,128,1024]{2,1,0:T(8,128)(2,1)} %copy-done.10, bf16[2,128,1024]{2,1,0:T(8,128)(2,1)} %copy-done.12, f32[6,8,1024]{2,1,0:T(8,128)} %copy-done, ...), custom_call_target="tpu_custom_call", output_to_operand_aliasing={{0}: (5, {})} | custom-call | flops 31457280 | bytes 4194304 | tf_op jit(solution)/shard_map/sweep/pallas_call | solution.py:307
  80.0 1.3 %collective-permute-start.10 = (bf16[128,2176]{1,0:T(8,128)(2,1)}, bf16[128,2176]{1,0:T(8,128)(2,1)S(1)}, u32[]{:S(2)}, u32[]{:S(2)}) collective-permute-start(bf16[128,2176]{1,0:T(8,128)(2,1)} %get-tuple-element.39), channel_id=1, source_target_pairs={{0,1},{1,0},{2,3},{3,2},{4,5},{5,4},{6,7},{7,6},{8,9},{9,8},{10,11... | collective-permute-start | bytes 1671176 | tf_op jit(solution)/shard_map/ppermute | solution.py:521
  82.0 9.7 %sweep.7 = (bf16[512,4,1024]{2,1,0:T(4,128)(2,1)}, bf16[128,2176]{1,0:T(8,128)(2,1)}, bf16[128,2176]{1,0:T(8,128)(2,1)}) custom-call(bf16[512,4,1024]{2,1,0:T(4,128)(2,1)} %own_ref.7, bf16[2,128,1024]{2,1,0:T(8,128)(2,1)} %copy-done.11, bf16[2,128,1024]{2,1,0:T(8,128)(2,1)} %collective-permute-done.1.outer_ref, ...), custom_call_target="tpu_custom_call", output_to_operand_aliasing={{0}: (5, {})} | custom-call | flops 31457280 | bytes 4194304 | tf_op jit(solution)/shard_map/sweep/pallas_call | solution.py:307
  92.2 2.1 %collective-permute-start.12 = (bf16[512,512]{1,0:T(8,128)(2,1)S(1)}, bf16[512,512]{1,0:T(8,128)(2,1)S(1)}, u32[]{:S(2)}, u32[]{:S(2)}) collective-permute-start(bf16[512,512]{1,0:T(8,128)(2,1)S(1)} %pad_maximum_fusion), channel_id=1, source_target_pairs={{2,0},{4,2},{6,4},{8,6},{10,8},{12,10},{14,12},{16,14},{18,16},{20... | collective-permute-start | bytes 1572872 | tf_op jit(solution)/shard_map/ppermute | solution.py:524
  94.3 0.9 slice.30
  95.2 1.9 %collective-permute-start.13 = (bf16[256,512]{1,0:T(8,128)(2,1)S(1)}, bf16[256,512]{1,0:T(8,128)(2,1)S(1)}, u32[]{:S(2)}, u32[]{:S(2)}) collective-permute-start(bf16[256,512]{1,0:T(8,128)(2,1)S(1)} %pad_maximum_fusion.1), channel_id=1, source_target_pairs={{2,0},{4,2},{6,4},{8,6},{10,8},{12,10},{14,12},{16,14},{18,16},{20... | collective-permute-start | bytes 786440 | tf_op jit(solution)/shard_map/ppermute | solution.py:524
  97.2 3.7 %collective-permute-done.11.refs_7_ = bf16[128,2176]{1,0:T(8,128)(2,1)S(1)} collective-permute-done((bf16[128,2176]{1,0:T(8,128)(2,1)}, bf16[128,2176]{1,0:T(8,128)(2,1)S(1)}, u32[]{:S(2)}, u32[]{:S(2)}) %collective-permute-start.11) | collective-permute-done | bytes 557088 | tf_op jit(solution)/shard_map/ppermute | solution.py:521
  100.9 2.1 %collective-permute-start.14 = (bf16[256,512]{1,0:T(8,128)(2,1)S(1)}, bf16[256,512]{1,0:T(8,128)(2,1)S(1)}, u32[]{:S(2)}, u32[]{:S(2)}) collective-permute-start(bf16[256,512]{1,0:T(8,128)(2,1)S(1)} %pad_maximum_fusion.2), channel_id=1, source_target_pairs={{2,0},{4,2},{6,4},{8,6},{10,8},{12,10},{14,12},{16,14},{18,16},{20... | collective-permute-start | bytes 786440 | tf_op jit(solution)/shard_map/ppermute | solution.py:524
  103.0 2.7 %fold.1.weight_ref = bf16[1024,1024]{1,0:T(8,128)(2,1)S(1)} custom-call(bf16[1024,1024]{1,0:T(8,128)(2,1)S(1)} %copy-done.6), custom_call_target="tpu_custom_call" | custom-call | flops 1048576 | bytes 4194304 | tf_op jit(solution)/shard_map/fold/pallas_call | solution.py:367
  105.7 8.2 %weigh.3.refs_8_ = f32[32,512]{1,0:T(8,128)S(1)} custom-call(bf16[1024,1024]{1,0:T(8,128)(2,1)S(1)} %fold.1.weight_ref, bf16[128,2176]{1,0:T(8,128)(2,1)S(1)} %copy-done.1, bf16[128,2176]{1,0:T(8,128)(2,1)S(1)} %collective-permute-done.8.refs_1_, bf16[128,2176]{1,0:T(8,128)(2,1)S(1)} %copy-done.2, bf16[128,2176]{1,0:T(8,128)(2,1)S(1)} %collective-permute-done.9.refs_3_, ...), custom_call_target="tpu_custom_call" | custom-call | flops 1409286144 | bytes 2752512 | tf_op jit(solution)/shard_map/weigh/pallas_call | solution.py:470
  113.9 4.9 %weigh.4.refs_11_ = f32[32,512]{1,0:T(8,128)S(1)} custom-call(bf16[1024,1024]{1,0:T(8,128)(2,1)S(1)} %fold.1.weight_ref, bf16[128,2176]{1,0:T(8,128)(2,1)S(1)} %copy-done.1, bf16[128,2176]{1,0:T(8,128)(2,1)S(1)} %collective-permute-done.8.refs_1_, bf16[128,2176]{1,0:T(8,128)(2,1)S(1)} %copy-done.2, bf16[128,2176]{1,0:T(8,128)(2,1)S(1)} %collective-permute-done.9.refs_3_, ...), custom_call_target="tpu_custom_call" | custom-call | flops 1056964608 | bytes 4128768 | tf_op jit(solution)/shard_map/weigh/pallas_call | solution.py:470
  118.9 6.1 %weigh.5 = f32[4,512]{1,0:T(4,128)} custom-call(bf16[1024,1024]{1,0:T(8,128)(2,1)S(1)} %fold.1.weight_ref, bf16[128,2176]{1,0:T(8,128)(2,1)S(1)} %copy-done.1, bf16[128,2176]{1,0:T(8,128)(2,1)S(1)} %collective-permute-done.8.refs_1_, bf16[128,2176]{1,0:T(8,128)(2,1)S(1)} %copy-done.2, bf16[128,2176]{1,0:T(8,128)(2,1)S(1)} %collective-permute-done.9.refs_3_, ...), custom_call_target="tpu_custom_call" | custom-call | flops 1409286144 | bytes 5505024 | tf_op jit(solution)/shard_map/weigh/pallas_call | solution.py:470
  (60 shorter events, 4.7 us)
Async XLA Ops:
  4.3 13.7 %collective-permute-start.6 = (bf16[2,128,1024]{2,1,0:T(8,128)(2,1)}, bf16[2,128,1024]{2,1,0:T(8,128)(2,1)S(1)}, u32[]{:S(2)}, u32[]{:S(2)}) collective-permute-start(bf16[2,128,1024]{2,1,0:T(8,128)(2,1)} %get-tuple-element.28), channel_id=1, source_target_pairs={{0,2},{4,6},{8,10},{12,14},{16,18},{20,22},{24,26},{28,30},{2,0},{... | collective-permute-start | bytes 1572872 | tf_op jit(solution)/shard_map/ppermute | solution.py:504
  7.4 18.9 %collective-permute-start.2 = (bf16[2,144,1024]{2,1,0:T(8,128)(2,1)}, bf16[2,144,1024]{2,1,0:T(8,128)(2,1)S(1)}, u32[]{:S(2)}, u32[]{:S(2)}) collective-permute-start(bf16[2,144,1024]{2,1,0:T(8,128)(2,1)} %get-tuple-element.24), channel_id=1, source_target_pairs={{0,2},{4,6},{8,10},{12,14},{16,18},{20,22},{24,26},{28,30},{2,0},{... | collective-permute-start | bytes 1769480 | tf_op jit(solution)/shard_map/ppermute | solution.py:504
  7.9 34.8 %collective-permute-start.3 = (bf16[2,144,1024]{2,1,0:T(8,128)(2,1)}, bf16[2,144,1024]{2,1,0:T(8,128)(2,1)S(1)}, u32[]{:S(2)}, u32[]{:S(2)}) collective-permute-start(bf16[2,144,1024]{2,1,0:T(8,128)(2,1)} %get-tuple-element.25), channel_id=1, source_target_pairs={{2,4},{6,8},{10,12},{14,16},{18,20},{22,24},{26,28},{4,2},{8,6},{1... | collective-permute-start | bytes 1769480 | tf_op jit(solution)/shard_map/ppermute | solution.py:503
  12.4 34.6 %copy-start.13 = (s32[512,2]{0,1:T(2,128)S(1)}, s32[512,2]{0,1:T(2,128)}, u32[]{:S(2)}) copy-start(s32[512,2]{0,1:T(2,128)} %param.6) | copy-start | bytes 12292
  12.4 35.5 %copy-start.8 = (f32[4,1024]{1,0:T(4,128)S(1)}, f32[4,1024]{1,0:T(4,128)}, u32[]{:S(2)}) copy-start(f32[4,1024]{1,0:T(4,128)} %sigma_ref.9) | copy-start | bytes 49156
  12.4 46.0 %collective-permute-start.7 = (bf16[2,128,1024]{2,1,0:T(8,128)(2,1)}, bf16[2,128,1024]{2,1,0:T(8,128)(2,1)}, u32[]{:S(2)}, u32[]{:S(2)}) collective-permute-start(bf16[2,128,1024]{2,1,0:T(8,128)(2,1)} %get-tuple-element.29), channel_id=1, source_target_pairs={{2,4},{6,8},{10,12},{14,16},{18,20},{22,24},{26,28},{4,2},{8,6},{1... | collective-permute-start | bytes 1572872 | tf_op jit(solution)/shard_map/ppermute | solution.py:503
  18.0 51.3 %collective-permute-start.4 = (bf16[2,128,1024]{2,1,0:T(8,128)(2,1)}, bf16[2,128,1024]{2,1,0:T(8,128)(2,1)S(1)}, u32[]{:S(2)}, u32[]{:S(2)}) collective-permute-start(bf16[2,128,1024]{2,1,0:T(8,128)(2,1)} %get-tuple-element.26), channel_id=1, source_target_pairs={{0,2},{4,6},{8,10},{12,14},{16,18},{20,22},{24,26},{28,30},{2,0},{... | collective-permute-start | bytes 1572872 | tf_op jit(solution)/shard_map/ppermute | solution.py:504
  18.0 40.4 %copy-start.9 = (bf16[2,128,1024]{2,1,0:T(8,128)(2,1)}, bf16[2,128,1024]{2,1,0:T(8,128)(2,1)S(1)}, u32[]{:S(2)}) copy-start(bf16[2,128,1024]{2,1,0:T(8,128)(2,1)S(1)} %collective-permute-done.6.inner_ref) | copy-start | bytes 1572868
  18.1 51.5 %collective-permute-start.5 = (bf16[2,128,1024]{2,1,0:T(8,128)(2,1)}, bf16[2,128,1024]{2,1,0:T(8,128)(2,1)S(1)}, u32[]{:S(2)}, u32[]{:S(2)}) collective-permute-start(bf16[2,128,1024]{2,1,0:T(8,128)(2,1)} %get-tuple-element.27), channel_id=1, source_target_pairs={{2,4},{6,8},{10,12},{14,16},{18,20},{22,24},{26,28},{4,2},{8,6},{1... | collective-permute-start | bytes 1572872 | tf_op jit(solution)/shard_map/ppermute | solution.py:503
  26.3 21.8 %copy-start.4 = (bf16[2,144,1024]{2,1,0:T(8,128)(2,1)}, bf16[2,144,1024]{2,1,0:T(8,128)(2,1)S(1)}, u32[]{:S(2)}) copy-start(bf16[2,144,1024]{2,1,0:T(8,128)(2,1)S(1)} %collective-permute-done.2.inner_ref) | copy-start | bytes 1769476
  26.3 54.9 %collective-permute-start = (bf16[2,128,1024]{2,1,0:T(8,128)(2,1)}, bf16[2,128,1024]{2,1,0:T(8,128)(2,1)S(1)}, u32[]{:S(2)}, u32[]{:S(2)}) collective-permute-start(bf16[2,128,1024]{2,1,0:T(8,128)(2,1)} %get-tuple-element.22), channel_id=1, source_target_pairs={{0,2},{4,6},{8,10},{12,14},{16,18},{20,22},{24,26},{28,30},{2,0},{... | collective-permute-start | bytes 1572872 | tf_op jit(solution)/shard_map/ppermute | solution.py:504
  42.7 5.4 %copy-start.5 = (bf16[2,144,1024]{2,1,0:T(8,128)(2,1)}, bf16[2,144,1024]{2,1,0:T(8,128)(2,1)S(1)}, u32[]{:S(2)}) copy-start(bf16[2,144,1024]{2,1,0:T(8,128)(2,1)S(1)} %collective-permute-done.3.outer_ref) | copy-start | bytes 1769476
  42.7 38.5 %collective-permute-start.1 = (bf16[2,128,1024]{2,1,0:T(8,128)(2,1)}, bf16[2,128,1024]{2,1,0:T(8,128)(2,1)}, u32[]{:S(2)}, u32[]{:S(2)}) collective-permute-start(bf16[2,128,1024]{2,1,0:T(8,128)(2,1)} %get-tuple-element.23), channel_id=1, source_target_pairs={{2,4},{6,8},{10,12},{14,16},{18,20},{22,24},{26,28},{4,2},{8,6},{1... | collective-permute-start | bytes 1572872 | tf_op jit(solution)/shard_map/ppermute | solution.py:503
  68.1 24.0 %collective-permute-start.9 = (bf16[128,2176]{1,0:T(8,128)(2,1)}, bf16[128,2176]{1,0:T(8,128)(2,1)S(1)}, u32[]{:S(2)}, u32[]{:S(2)}) collective-permute-start(bf16[128,2176]{1,0:T(8,128)(2,1)} %get-tuple-element.37), channel_id=1, source_target_pairs={{0,1},{1,0},{2,3},{3,2},{4,5},{5,4},{6,7},{7,6},{8,9},{9,8},{10,11... | collective-permute-start | bytes 1671176 | tf_op jit(solution)/shard_map/ppermute | solution.py:521
  69.3 22.8 %collective-permute-start.8 = (bf16[128,2176]{1,0:T(8,128)(2,1)}, bf16[128,2176]{1,0:T(8,128)(2,1)S(1)}, u32[]{:S(2)}, u32[]{:S(2)}) collective-permute-start(bf16[128,2176]{1,0:T(8,128)(2,1)} %get-tuple-element.35), channel_id=1, source_target_pairs={{0,1},{1,0},{2,3},{3,2},{4,5},{5,4},{6,7},{7,6},{8,9},{9,8},{10,11... | collective-permute-start | bytes 1671176 | tf_op jit(solution)/shard_map/ppermute | solution.py:521
  80.0 15.2 %collective-permute-start.10 = (bf16[128,2176]{1,0:T(8,128)(2,1)}, bf16[128,2176]{1,0:T(8,128)(2,1)S(1)}, u32[]{:S(2)}, u32[]{:S(2)}) collective-permute-start(bf16[128,2176]{1,0:T(8,128)(2,1)} %get-tuple-element.39), channel_id=1, source_target_pairs={{0,1},{1,0},{2,3},{3,2},{4,5},{5,4},{6,7},{7,6},{8,9},{9,8},{10,11... | collective-permute-start | bytes 1671176 | tf_op jit(solution)/shard_map/ppermute | solution.py:521
  82.0 10.0 %copy-start.2 = (bf16[128,2176]{1,0:T(8,128)(2,1)S(1)}, bf16[128,2176]{1,0:T(8,128)(2,1)}, u32[]{:S(2)}) copy-start(bf16[128,2176]{1,0:T(8,128)(2,1)} %get-tuple-element.36.refs_2_) | copy-start | bytes 1671172
  82.0 10.0 %copy-start.1 = (bf16[128,2176]{1,0:T(8,128)(2,1)S(1)}, bf16[128,2176]{1,0:T(8,128)(2,1)}, u32[]{:S(2)}) copy-start(bf16[128,2176]{1,0:T(8,128)(2,1)} %get-tuple-element.34.refs_0_) | copy-start | bytes 1671172
  82.0 12.2 %copy-start.3 = (bf16[128,2176]{1,0:T(8,128)(2,1)S(1)}, bf16[128,2176]{1,0:T(8,128)(2,1)}, u32[]{:S(2)}) copy-start(bf16[128,2176]{1,0:T(8,128)(2,1)} %get-tuple-element.38.refs_4_) | copy-start | bytes 1671172
  91.8 11.2 %copy-start.6 = (bf16[1024,1024]{1,0:T(8,128)(2,1)S(1)}, bf16[1024,1024]{1,0:T(8,128)(2,1)}, u32[]{:S(2)}) copy-start(bf16[1024,1024]{1,0:T(8,128)(2,1)} %weight_ref.1) | copy-start | bytes 6291460
  91.8 9.1 %collective-permute-start.11 = (bf16[128,2176]{1,0:T(8,128)(2,1)}, bf16[128,2176]{1,0:T(8,128)(2,1)S(1)}, u32[]{:S(2)}, u32[]{:S(2)}) collective-permute-start(bf16[128,2176]{1,0:T(8,128)(2,1)} %get-tuple-element.41), channel_id=1, source_target_pairs={{0,1},{1,0},{2,3},{3,2},{4,5},{5,4},{6,7},{7,6},{8,9},{9,8},{10,11... | collective-permute-start | bytes 1671176 | tf_op jit(solution)/shard_map/ppermute | solution.py:521
  92.2 13.5 %collective-permute-start.12 = (bf16[512,512]{1,0:T(8,128)(2,1)S(1)}, bf16[512,512]{1,0:T(8,128)(2,1)S(1)}, u32[]{:S(2)}, u32[]{:S(2)}) collective-permute-start(bf16[512,512]{1,0:T(8,128)(2,1)S(1)} %pad_maximum_fusion), channel_id=1, source_target_pairs={{2,0},{4,2},{6,4},{8,6},{10,8},{12,10},{14,12},{16,14},{18,16},{20... | collective-permute-start | bytes 1572872 | tf_op jit(solution)/shard_map/ppermute | solution.py:524
  95.2 18.7 %collective-permute-start.13 = (bf16[256,512]{1,0:T(8,128)(2,1)S(1)}, bf16[256,512]{1,0:T(8,128)(2,1)S(1)}, u32[]{:S(2)}, u32[]{:S(2)}) collective-permute-start(bf16[256,512]{1,0:T(8,128)(2,1)S(1)} %pad_maximum_fusion.1), channel_id=1, source_target_pairs={{2,0},{4,2},{6,4},{8,6},{10,8},{12,10},{14,12},{16,14},{18,16},{20... | collective-permute-start | bytes 786440 | tf_op jit(solution)/shard_map/ppermute | solution.py:524
  100.9 18.0 %collective-permute-start.14 = (bf16[256,512]{1,0:T(8,128)(2,1)S(1)}, bf16[256,512]{1,0:T(8,128)(2,1)S(1)}, u32[]{:S(2)}, u32[]{:S(2)}) collective-permute-start(bf16[256,512]{1,0:T(8,128)(2,1)S(1)} %pad_maximum_fusion.2), channel_id=1, source_target_pairs={{2,0},{4,2},{6,4},{8,6},{10,8},{12,10},{14,12},{16,14},{18,16},{20... | collective-permute-start | bytes 786440 | tf_op jit(solution)/shard_map/ppermute | solution.py:524
  (5 other events, 8.1 us)

commit v4 on v2

--- a/solution.py
+++ b/solution.py
@@ -130,10 +130,10 @@
 def pack(fields, conductivity, k):
     _, depth, cells = fields.shape
     extra = k == 0
-    rows = UNIT if extra else ROWS
+    rows = UNIT
     steps = UNIT // rows
     sent = UNIT + (PART if extra else 0)
-    block = sent if extra else rows
+    block = sent
     return pl.pallas_call(
         functools.partial(pack_kernel, extra),
         grid=(steps,),
@@ -340,7 +340,6 @@
 
     for q in range(total):
         here = where_is(q)
-        chunk = q // count
         rows = pl.ds(q * UNIT, UNIT)
 
         def folded(other, carry):
@@ -351,17 +350,12 @@
             out_ref[rows, columns] = (straight + turned.T).astype(jnp.bfloat16)
             return carry
 
-        if chunk:
-            lax.fori_loop(0, chunk * count, folded, 0)
-        for other in range(chunk * count, (chunk + 1) * count):
-            there = where_is(other)
-            out_ref[rows, other * UNIT : (other + 1) * UNIT] = weight_ref[
-                pl.ds(here, UNIT), pl.ds(there, UNIT)
-            ]
-        if chunk + 1 < per:
-            out_ref[rows, (chunk + 1) * count * UNIT :] = jnp.zeros(
-                (UNIT, (per - chunk - 1) * count * UNIT), jnp.bfloat16
-            )
+        if q:
+            lax.fori_loop(0, q, folded, 0)
+        out_ref[rows, q * UNIT : (q + 1) * UNIT] = weight_ref[pl.ds(here, UNIT), pl.ds(here, UNIT)]
+        if q + 1 < total:
+            rest = (UNIT, (total - q - 1) * UNIT)
+            out_ref[rows, (q + 1) * UNIT :] = jnp.zeros(rest, jnp.bfloat16)
 
 
 def fold(weight, count, per):
@@ -379,7 +373,7 @@
     )(weight)
 
 
-def weigh_kernel(depth, band, pieces, above, row_start, block_rows, chunk_rows, scale, weight_ref, *refs):
+def weigh_kernel(depth, band, pieces, above, row_start, block_rows, scale, weight_ref, *refs):
     piece_refs, above_refs = refs[:pieces], refs[pieces : pieces + above]
     before_ref, out_ref, held, mixed, partial, sems = refs[pieces + above :]
     step = pl.program_id(0)
@@ -401,11 +395,10 @@
             copy.wait()
         partial[...] = before_ref[...]
 
-    chunk = (row_start + step * block_rows) // chunk_rows
-    for c in range(row_start // chunk_rows, held.shape[0] // chunk_rows):
-        reach = (c + 1) * chunk_rows
-
-        @pl.when(chunk == c)
+    for c in range(row_start // UNIT, held.shape[0] // UNIT):
+        reach = (c + 1) * UNIT
+
+        @pl.when(step == c - row_start // UNIT)
         def _():
             mixed[...] = jnp.dot(
                 weight_ref[:, :reach], held[:reach], preferred_element_type=jnp.float32
@@ -448,7 +441,7 @@
 
         rows = pl.ds(plane * 8, 8)
         start = tuple(partial[rows, t * LANES : (t + 1) * LANES] for t in range(tiles))
-        sums = lax.fori_loop(0, block_rows // GROUP, rows_of, start, unroll=4)
+        sums = lax.fori_loop(0, block_rows // GROUP, rows_of, start, unroll=True)
         for t in range(tiles):
             partial[rows, t * LANES : (t + 1) * LANES] = sums[t]
 
@@ -462,7 +455,7 @@
                 out_ref[plane : plane + 1, :] = total * scale
 
 
-def weigh(weight, pieces, above, before, row_start, rows, chunk_rows, depth, band, scale):
+def weigh(weight, pieces, above, before, row_start, rows, depth, band, scale):
     width = pieces[0].shape[1] + band
     held = sum(piece.shape[0] for piece in pieces)
     block_rows = UNIT
@@ -470,7 +463,7 @@
     out = (depth, band) if scale is not None else (depth * 8, band)
     return pl.pallas_call(
         functools.partial(
-            weigh_kernel, depth, band, len(pieces), len(above), row_start, block_rows, chunk_rows, scale
+            weigh_kernel, depth, band, len(pieces), len(above), row_start, block_rows, scale
         ),
         grid=(rows // block_rows,),
         in_specs=[pl.BlockSpec((block_rows, weight.shape[1]), lambda i: (i + first, 0))]
@@ -507,7 +500,7 @@
     coefs = stencil_coefficients(conductivity, *halos[0][1:], depth * lax.axis_size("cells"))
     weight = fold(data_weight, count, per)
     down = [(i + 1, i) for i in range(lax.axis_size("cells") - 1)]
-    stops = [stop for stop in (per - 2, per - 1, per) if stop > 0]
+    stops = sorted({max(per - 2, 0) * count, (per - 1) * count + 1, per * count} - {0})
     potentials = None
     pieces, above = [], []
     sums = jnp.zeros((depth * 8, band), jnp.float32)
@@ -521,19 +514,18 @@
             pairs = [(i, (i + r) % count) for i in range(count)]
             pieces.append(lax.ppermute(sent[r - 1], "src", pairs))
     for stop in stops:
-        lowest = jnp.concatenate([p[:, :band] for p in pieces[done * count : stop * count]], axis=0)
+        lowest = jnp.concatenate([p[:, :band] for p in pieces[done:stop]], axis=0)
         above.append(lax.ppermute(lowest, "cells", down))
         sums = weigh(
             weight,
-            pieces[: stop * count],
+            pieces[:stop],
             above,
             sums,
-            done * UNIT * count,
-            (stop - done) * UNIT * count,
-            UNIT * count,
+            done * UNIT,
+            (stop - done) * UNIT,
             depth,
             band,
-            1.0 / sources if stop == per else None,
+            1.0 / sources if stop == per * count else None,
         )
         done = stop
     return (potentials, sums)

time: 124 us -> 114 us (0.919)
  the two profiles are of different devices: /device:TPU:1 before, /device:TPU:21 now
where the time goes in v4:
time: 114 us
  Pallas kernels  65.1 us (57%)
  starting transfers between devices  23.4 us (21%)
  waiting for transfers between devices  22.6 us (20%)
  local copies, waits for them, and re-layouts  1.48 us (1%)
    pallas_call x4, Pallas kernels, sweep(): pl.pallas_call(functools.partial(sweep_kernel, count, band), grid=(size /...  34.6 us
    ppermute x4, waiting for transfers between devices, body(): outer = lax.ppermute(outer, 'cells', pairs_of('cells', 1))  16.2 us
    pallas_call x3, Pallas kernels, weigh(): pl.pallas_call(functools.partial(weigh_kernel, depth, band, len(pieces),...  14.8 us
    ppermute x4, starting transfers between devices, body(): outer = lax.ppermute(outer, 'cells', pairs_of('cells', 1))  13.6 us
    pallas_call x4, Pallas kernels, pack(): pl.pallas_call(functools.partial(pack_kernel, extra), grid=(steps,), in_s...  12.5 us
    ppermute x3, starting transfers between devices, body(): above.append(lax.ppermute(lowest, 'cells', down))  6.96 us
    ppermute x4, waiting for transfers between devices, body(): pieces.append(lax.ppermute(sent[r - 1], 'src', pairs))  6.38 us
    pallas_call x1, Pallas kernels, fold(): pl.pallas_call(functools.partial(fold_kernel, count, per), grid=(1,), in_...  3.03 us
  transfers between devices with their start and end apart: 15, of which 3 were waited for; matrix products, arithmetic and copies ran while one was open for 0% of the time, Pallas kernels for 52%

profile of v4, /device:TPU:21, one launch (start us, length us, event | category | flops | bytes accessed | tf_op | source)
XLA Modules:
  0.0 113.7 jit_solution(4912127139957419545)
XLA Ops:
  0.6 3.2 %pack.5 = (bf16[4,128,1024]{2,1,0:T(8,128)(2,1)}, bf16[2,144,1024]{2,1,0:T(8,128)(2,1)}, bf16[2,144,1024]{2,1,0:T(8,128)(2,1)}) custom-call(bf16[512,4,1024]{2,1,0:T(4,128)(2,1)} %fields_ref.7, f32[4,1024]{1,0:T(4,128)} %sigma_ref.9), custom_call_target="tpu_custom_call" | custom-call | tf_op jit(solution)/shard_map/pack/pallas_call | solution.py:137
  4.5 3.2 %collective-permute-start.3 = (bf16[2,144,1024]{2,1,0:T(8,128)(2,1)}, bf16[2,144,1024]{2,1,0:T(8,128)(2,1)S(1)}, u32[]{:S(2)}, u32[]{:S(2)}) collective-permute-start(bf16[2,144,1024]{2,1,0:T(8,128)(2,1)} %get-tuple-element.30), channel_id=1, source_target_pairs={{2,4},{6,8},{10,12},{14,16},{18,20},{22,24},{26,28},{4,2},{8,6},{1... | collective-permute-start | bytes 1769480 | tf_op jit(solution)/shard_map/ppermute | solution.py:497
  7.7 3.1 %pack.7 = (bf16[4,128,1024]{2,1,0:T(8,128)(2,1)}, bf16[2,128,1024]{2,1,0:T(8,128)(2,1)}, bf16[2,128,1024]{2,1,0:T(8,128)(2,1)}) custom-call(bf16[512,4,1024]{2,1,0:T(4,128)(2,1)} %fields_ref.7, f32[4,1024]{1,0:T(4,128)} %sigma_ref.9), custom_call_target="tpu_custom_call" | custom-call | tf_op jit(solution)/shard_map/pack/pallas_call | solution.py:137
  11.2 3.2 %collective-permute-start.7 = (bf16[2,128,1024]{2,1,0:T(8,128)(2,1)}, bf16[2,128,1024]{2,1,0:T(8,128)(2,1)}, u32[]{:S(2)}, u32[]{:S(2)}) collective-permute-start(bf16[2,128,1024]{2,1,0:T(8,128)(2,1)} %get-tuple-element.36), channel_id=1, source_target_pairs={{2,4},{6,8},{10,12},{14,16},{18,20},{22,24},{26,28},{4,2},{8,6},{1... | collective-permute-start | bytes 1572872 | tf_op jit(solution)/shard_map/ppermute | solution.py:497
  14.4 3.1 %pack.6 = (bf16[4,128,1024]{2,1,0:T(8,128)(2,1)}, bf16[2,128,1024]{2,1,0:T(8,128)(2,1)}, bf16[2,128,1024]{2,1,0:T(8,128)(2,1)}) custom-call(bf16[512,4,1024]{2,1,0:T(4,128)(2,1)} %fields_ref.7, f32[4,1024]{1,0:T(4,128)} %sigma_ref.9), custom_call_target="tpu_custom_call" | custom-call | tf_op jit(solution)/shard_map/pack/pallas_call | solution.py:137
  17.5 3.5 %collective-permute-start.5 = (bf16[2,128,1024]{2,1,0:T(8,128)(2,1)}, bf16[2,128,1024]{2,1,0:T(8,128)(2,1)}, u32[]{:S(2)}, u32[]{:S(2)}) collective-permute-start(bf16[2,128,1024]{2,1,0:T(8,128)(2,1)} %get-tuple-element.33), channel_id=1, source_target_pairs={{2,4},{6,8},{10,12},{14,16},{18,20},{22,24},{26,28},{4,2},{8,6},{1... | collective-permute-start | bytes 1572872 | tf_op jit(solution)/shard_map/ppermute | solution.py:497
  21.2 12.4 %collective-permute-done.3.outer_ref = bf16[2,144,1024]{2,1,0:T(8,128)(2,1)S(1)} collective-permute-done((bf16[2,144,1024]{2,1,0:T(8,128)(2,1)}, bf16[2,144,1024]{2,1,0:T(8,128)(2,1)S(1)}, u32[]{:S(2)}, u32[]{:S(2)}) %collective-permute-start.3) | collective-permute-done | bytes 589856 | tf_op jit(solution)/shard_map/ppermute | solution.py:497
  33.8 8.3 %sweep.4 = (bf16[512,4,1024]{2,1,0:T(4,128)(2,1)}, bf16[128,2176]{1,0:T(8,128)(2,1)S(1)}, bf16[128,2176]{1,0:T(8,128)(2,1)}) custom-call(bf16[4,128,1024]{2,1,0:T(8,128)(2,1)S(1)} %copy-done.4, bf16[2,144,1024]{2,1,0:T(8,128)(2,1)S(1)} %collective-permute-done.2.inner_ref, bf16[2,144,1024]{2,1,0:T(8,128)(2,1)S(1)} %collective-permute-done.3.outer_ref, ...), custom_call_target="tpu_custom_call" | custom-call | flops 31457280 | bytes 4194304 | tf_op jit(solution)/shard_map/sweep/pallas_call | solution.py:308
  42.1 1.2 %copy-done.2 = bf16[4,128,1024]{2,1,0:T(8,128)(2,1)S(1)} copy-done((bf16[4,128,1024]{2,1,0:T(8,128)(2,1)S(1)}, bf16[4,128,1024]{2,1,0:T(8,128)(2,1)}, u32[]{:S(2)}) %copy-start.2) | copy-done | bytes 1048600
  43.4 9.1 %sweep.5 = (bf16[512,4,1024]{2,1,0:T(4,128)(2,1)}, bf16[128,2176]{1,0:T(8,128)(2,1)S(1)}, bf16[128,2176]{1,0:T(8,128)(2,1)}) custom-call(bf16[4,128,1024]{2,1,0:T(8,128)(2,1)S(1)} %copy-done.2, bf16[2,128,1024]{2,1,0:T(8,128)(2,1)} %collective-permute-done.6.inner_ref, ...), custom_call_target="tpu_custom_call", output_to_operand_aliasing={{0}: (5, {})} | custom-call | flops 31457280 | bytes 4194304 | tf_op jit(solution)/shard_map/sweep/pallas_call | solution.py:308
  52.7 1.3 %collective-permute-start.8 = (bf16[128,2176]{1,0:T(8,128)(2,1)}, bf16[128,2176]{1,0:T(8,128)(2,1)S(1)}, u32[]{:S(2)}, u32[]{:S(2)}) collective-permute-start(bf16[128,2176]{1,0:T(8,128)(2,1)} %get-tuple-element.43), channel_id=1, source_target_pairs={{0,1},{1,0},{2,3},{3,2},{4,5},{5,4},{6,7},{7,6},{8,9},{9,8},{10,11... | collective-permute-start | bytes 1671176 | tf_op jit(solution)/shard_map/ppermute | solution.py:515
  54.0 3.1 %pack.4 = (bf16[4,128,1024]{2,1,0:T(8,128)(2,1)}, bf16[2,128,1024]{2,1,0:T(8,128)(2,1)}, bf16[2,128,1024]{2,1,0:T(8,128)(2,1)}) custom-call(bf16[512,4,1024]{2,1,0:T(4,128)(2,1)} %fields_ref.7, f32[4,1024]{1,0:T(4,128)} %sigma_ref.9), custom_call_target="tpu_custom_call" | custom-call | tf_op jit(solution)/shard_map/pack/pallas_call | solution.py:137
  57.0 3.7 %collective-permute-start.1 = (bf16[2,128,1024]{2,1,0:T(8,128)(2,1)}, bf16[2,128,1024]{2,1,0:T(8,128)(2,1)S(1)}, u32[]{:S(2)}, u32[]{:S(2)}) collective-permute-start(bf16[2,128,1024]{2,1,0:T(8,128)(2,1)} %get-tuple-element.28), channel_id=1, source_target_pairs={{2,4},{6,8},{10,12},{14,16},{18,20},{22,24},{26,28},{4,2},{8,6},{1... | collective-permute-start | bytes 1572872 | tf_op jit(solution)/shard_map/ppermute | solution.py:497
  60.8 9.0 %sweep.6 = (bf16[512,4,1024]{2,1,0:T(4,128)(2,1)}, bf16[128,2176]{1,0:T(8,128)(2,1)S(1)}, bf16[128,2176]{1,0:T(8,128)(2,1)S(1)}) custom-call(bf16[4,128,1024]{2,1,0:T(8,128)(2,1)S(1)} %copy-done.1, bf16[2,128,1024]{2,1,0:T(8,128)(2,1)} %collective-permute-done.4.inner_ref, ...), custom_call_target="tpu_custom_call", output_to_operand_aliasing={{0}: (5, {})} | custom-call | flops 31457280 | bytes 4194304 | tf_op jit(solution)/shard_map/sweep/pallas_call | solution.py:308
  70.0 3.8 %collective-permute-done.1.outer_ref = bf16[2,128,1024]{2,1,0:T(8,128)(2,1)S(1)} collective-permute-done((bf16[2,128,1024]{2,1,0:T(8,128)(2,1)}, bf16[2,128,1024]{2,1,0:T(8,128)(2,1)S(1)}, u32[]{:S(2)}, u32[]{:S(2)}) %collective-permute-start.1) | collective-permute-done | bytes 524320 | tf_op jit(solution)/shard_map/ppermute | solution.py:497
  73.8 8.1 %sweep.7 = (bf16[512,4,1024]{2,1,0:T(4,128)(2,1)}, bf16[128,2176]{1,0:T(8,128)(2,1)S(1)}, bf16[128,2176]{1,0:T(8,128)(2,1)S(1)}) custom-call(bf16[4,128,1024]{2,1,0:T(8,128)(2,1)S(1)} %copy-done.3, bf16[2,128,1024]{2,1,0:T(8,128)(2,1)S(1)} %collective-permute-done.inner_ref, ...), custom_call_target="tpu_custom_call", output_to_operand_aliasing={{0}: (5, {})} | custom-call | flops 31457280 | bytes 4194304 | tf_op jit(solution)/shard_map/sweep/pallas_call | solution.py:308
  82.3 1.9 %collective-permute-start.12 = (bf16[512,512]{1,0:T(8,128)(2,1)S(1)}, bf16[512,512]{1,0:T(8,128)(2,1)S(1)}, u32[]{:S(2)}, u32[]{:S(2)}) collective-permute-start(bf16[512,512]{1,0:T(8,128)(2,1)S(1)} %pad_maximum_fusion), channel_id=1, source_target_pairs={{2,0},{4,2},{6,4},{8,6},{10,8},{12,10},{14,12},{16,14},{18,16},{20... | collective-permute-start | bytes 1572872 | tf_op jit(solution)/shard_map/ppermute | solution.py:518
  84.3 2.6 %collective-permute-start.13 = (bf16[384,512]{1,0:T(8,128)(2,1)S(1)}, bf16[384,512]{1,0:T(8,128)(2,1)S(1)}, u32[]{:S(2)}, u32[]{:S(2)}) collective-permute-start(bf16[384,512]{1,0:T(8,128)(2,1)S(1)} %pad_maximum_fusion.1), channel_id=1, source_target_pairs={{2,0},{4,2},{6,4},{8,6},{10,8},{12,10},{14,12},{16,14},{18,16},{20... | collective-permute-start | bytes 1179656 | tf_op jit(solution)/shard_map/ppermute | solution.py:518
  86.9 3.0 %fold.1.weight_ref = bf16[1024,1024]{1,0:T(8,128)(2,1)S(1)} custom-call(bf16[1024,1024]{1,0:T(8,128)(2,1)S(1)} %copy-done), custom_call_target="tpu_custom_call" | custom-call | flops 1048576 | bytes 4194304 | tf_op jit(solution)/shard_map/fold/pallas_call | solution.py:362
  89.9 6.4 %collective-permute-done.11.refs_7_ = bf16[128,2176]{1,0:T(8,128)(2,1)S(1)} collective-permute-done((bf16[128,2176]{1,0:T(8,128)(2,1)S(1)}, bf16[128,2176]{1,0:T(8,128)(2,1)S(1)}, u32[]{:S(2)}, u32[]{:S(2)}) %collective-permute-start.11) | collective-permute-done | bytes 557088 | tf_op jit(solution)/shard_map/ppermute | solution.py:515
  96.3 2.5 %collective-permute-start.14 = (bf16[128,512]{1,0:T(8,128)(2,1)S(1)}, bf16[128,512]{1,0:T(8,128)(2,1)S(1)}, u32[]{:S(2)}, u32[]{:S(2)}) collective-permute-start(bf16[128,512]{1,0:T(8,128)(2,1)S(1)} %slice.35), channel_id=1, source_target_pairs={{2,0},{4,2},{6,4},{8,6},{10,8},{12,10},{14,12},{16,14},{18,16},{20... | collective-permute-start | bytes 393224 | tf_op jit(solution)/shard_map/ppermute | solution.py:518
  98.8 6.3 %weigh.3.refs_9_ = f32[32,512]{1,0:T(8,128)S(1)} custom-call(bf16[1024,1024]{1,0:T(8,128)(2,1)S(1)} %fold.1.weight_ref, bf16[128,2176]{1,0:T(8,128)(2,1)S(1)} %get-tuple-element.42.refs_0_, bf16[128,2176]{1,0:T(8,128)(2,1)S(1)} %collective-permute-done.8.refs_1_, bf16[128,2176]{1,0:T(8,128)(2,1)S(1)} %get-tuple-element.44.refs_2_, ...), custom_call_target="tpu_custom_call" | custom-call | flops 1409286144 | bytes 2752512 | tf_op jit(solution)/shard_map/weigh/pallas_call | solution.py:464
  105.1 6.0 %weigh.4.refs_11_ = f32[32,512]{1,0:T(8,128)S(1)} custom-call(bf16[1024,1024]{1,0:T(8,128)(2,1)S(1)} %fold.1.weight_ref, bf16[128,2176]{1,0:T(8,128)(2,1)S(1)} %get-tuple-element.42.refs_0_, bf16[128,2176]{1,0:T(8,128)(2,1)S(1)} %collective-permute-done.8.refs_1_, bf16[128,2176]{1,0:T(8,128)(2,1)S(1)} %get-tuple-element.44.refs_2_, ...), custom_call_target="tpu_custom_call" | custom-call | flops 1849688064 | bytes 4816896 | tf_op jit(solution)/shard_map/weigh/pallas_call | solution.py:464
  111.2 2.4 %weigh.5 = f32[4,512]{1,0:T(4,128)} custom-call(bf16[1024,1024]{1,0:T(8,128)(2,1)S(1)} %fold.1.weight_ref, bf16[128,2176]{1,0:T(8,128)(2,1)S(1)} %get-tuple-element.42.refs_0_, bf16[128,2176]{1,0:T(8,128)(2,1)S(1)} %collective-permute-done.8.refs_1_, bf16[128,2176]{1,0:T(8,128)(2,1)S(1)} %get-tuple-element.44.refs_2_, ...), custom_call_target="tpu_custom_call" | custom-call | flops 704643072 | bytes 5505024 | tf_op jit(solution)/shard_map/weigh/pallas_call | solution.py:464
  (45 shorter events, 2.2 us)
Async XLA Ops:
  3.8 13.7 %collective-permute-start.2 = (bf16[2,144,1024]{2,1,0:T(8,128)(2,1)}, bf16[2,144,1024]{2,1,0:T(8,128)(2,1)S(1)}, u32[]{:S(2)}, u32[]{:S(2)}) collective-permute-start(bf16[2,144,1024]{2,1,0:T(8,128)(2,1)} %get-tuple-element.29), channel_id=1, source_target_pairs={{0,2},{4,6},{8,10},{12,14},{16,18},{20,22},{24,26},{28,30},{2,0},{... | collective-permute-start | bytes 1769480 | tf_op jit(solution)/shard_map/ppermute | solution.py:498
  4.5 16.5 %copy-start.6 = (s32[512,2]{0,1:T(2,128)S(1)}, s32[512,2]{0,1:T(2,128)}, u32[]{:S(2)}) copy-start(s32[512,2]{0,1:T(2,128)} %param.6) | copy-start | bytes 12292
  4.5 29.1 %copy-start.5 = (f32[4,1024]{1,0:T(4,128)S(1)}, f32[4,1024]{1,0:T(4,128)}, u32[]{:S(2)}) copy-start(f32[4,1024]{1,0:T(4,128)} %sigma_ref.9) | copy-start | bytes 49156
  4.5 29.3 %copy-start.4 = (bf16[4,128,1024]{2,1,0:T(8,128)(2,1)S(1)}, bf16[4,128,1024]{2,1,0:T(8,128)(2,1)}, u32[]{:S(2)}) copy-start(bf16[4,128,1024]{2,1,0:T(8,128)(2,1)} %get-tuple-element.37.own_ref) | copy-start | bytes 3145732
  4.5 29.1 %collective-permute-start.3 = (bf16[2,144,1024]{2,1,0:T(8,128)(2,1)}, bf16[2,144,1024]{2,1,0:T(8,128)(2,1)S(1)}, u32[]{:S(2)}, u32[]{:S(2)}) collective-permute-start(bf16[2,144,1024]{2,1,0:T(8,128)(2,1)} %get-tuple-element.30), channel_id=1, source_target_pairs={{2,4},{6,8},{10,12},{14,16},{18,20},{22,24},{26,28},{4,2},{8,6},{1... | collective-permute-start | bytes 1769480 | tf_op jit(solution)/shard_map/ppermute | solution.py:497
  10.8 31.3 %collective-permute-start.6 = (bf16[2,128,1024]{2,1,0:T(8,128)(2,1)}, bf16[2,128,1024]{2,1,0:T(8,128)(2,1)}, u32[]{:S(2)}, u32[]{:S(2)}) collective-permute-start(bf16[2,128,1024]{2,1,0:T(8,128)(2,1)} %get-tuple-element.35), channel_id=1, source_target_pairs={{0,2},{4,6},{8,10},{12,14},{16,18},{20,22},{24,26},{28,30},{2,0},{... | collective-permute-start | bytes 1572872 | tf_op jit(solution)/shard_map/ppermute | solution.py:498
  11.2 31.0 %collective-permute-start.7 = (bf16[2,128,1024]{2,1,0:T(8,128)(2,1)}, bf16[2,128,1024]{2,1,0:T(8,128)(2,1)}, u32[]{:S(2)}, u32[]{:S(2)}) collective-permute-start(bf16[2,128,1024]{2,1,0:T(8,128)(2,1)} %get-tuple-element.36), channel_id=1, source_target_pairs={{2,4},{6,8},{10,12},{14,16},{18,20},{22,24},{26,28},{4,2},{8,6},{1... | collective-permute-start | bytes 1572872 | tf_op jit(solution)/shard_map/ppermute | solution.py:497
  17.5 39.6 %collective-permute-start.4 = (bf16[2,128,1024]{2,1,0:T(8,128)(2,1)}, bf16[2,128,1024]{2,1,0:T(8,128)(2,1)}, u32[]{:S(2)}, u32[]{:S(2)}) collective-permute-start(bf16[2,128,1024]{2,1,0:T(8,128)(2,1)} %get-tuple-element.32), channel_id=1, source_target_pairs={{0,2},{4,6},{8,10},{12,14},{16,18},{20,22},{24,26},{28,30},{2,0},{... | collective-permute-start | bytes 1572872 | tf_op jit(solution)/shard_map/ppermute | solution.py:498
  17.5 43.3 %collective-permute-start.5 = (bf16[2,128,1024]{2,1,0:T(8,128)(2,1)}, bf16[2,128,1024]{2,1,0:T(8,128)(2,1)}, u32[]{:S(2)}, u32[]{:S(2)}) collective-permute-start(bf16[2,128,1024]{2,1,0:T(8,128)(2,1)} %get-tuple-element.33), channel_id=1, source_target_pairs={{2,4},{6,8},{10,12},{14,16},{18,20},{22,24},{26,28},{4,2},{8,6},{1... | collective-permute-start | bytes 1572872 | tf_op jit(solution)/shard_map/ppermute | solution.py:497
  42.1 1.2 %copy-start.2 = (bf16[4,128,1024]{2,1,0:T(8,128)(2,1)S(1)}, bf16[4,128,1024]{2,1,0:T(8,128)(2,1)}, u32[]{:S(2)}) copy-start(bf16[4,128,1024]{2,1,0:T(8,128)(2,1)} %get-tuple-element.34.own_ref) | copy-start | bytes 3145732
  43.4 17.5 %copy-start.1 = (bf16[4,128,1024]{2,1,0:T(8,128)(2,1)S(1)}, bf16[4,128,1024]{2,1,0:T(8,128)(2,1)}, u32[]{:S(2)}) copy-start(bf16[4,128,1024]{2,1,0:T(8,128)(2,1)} %get-tuple-element.31.own_ref) | copy-start | bytes 3145732
  52.5 29.7 %collective-permute-start.9 = (bf16[128,2176]{1,0:T(8,128)(2,1)}, bf16[128,2176]{1,0:T(8,128)(2,1)S(1)}, u32[]{:S(2)}, u32[]{:S(2)}) collective-permute-start(bf16[128,2176]{1,0:T(8,128)(2,1)} %get-tuple-element.45), channel_id=1, source_target_pairs={{0,1},{1,0},{2,3},{3,2},{4,5},{5,4},{6,7},{7,6},{8,9},{9,8},{10,11... | collective-permute-start | bytes 1671176 | tf_op jit(solution)/shard_map/ppermute | solution.py:515
  52.7 29.5 %collective-permute-start.8 = (bf16[128,2176]{1,0:T(8,128)(2,1)}, bf16[128,2176]{1,0:T(8,128)(2,1)S(1)}, u32[]{:S(2)}, u32[]{:S(2)}) collective-permute-start(bf16[128,2176]{1,0:T(8,128)(2,1)} %get-tuple-element.43), channel_id=1, source_target_pairs={{0,1},{1,0},{2,3},{3,2},{4,5},{5,4},{6,7},{7,6},{8,9},{9,8},{10,11... | collective-permute-start | bytes 1671176 | tf_op jit(solution)/shard_map/ppermute | solution.py:515
  57.0 16.8 %copy-start.3 = (bf16[4,128,1024]{2,1,0:T(8,128)(2,1)S(1)}, bf16[4,128,1024]{2,1,0:T(8,128)(2,1)}, u32[]{:S(2)}) copy-start(bf16[4,128,1024]{2,1,0:T(8,128)(2,1)} %get-tuple-element.26.own_ref) | copy-start | bytes 3145732
  57.0 13.0 %collective-permute-start = (bf16[2,128,1024]{2,1,0:T(8,128)(2,1)}, bf16[2,128,1024]{2,1,0:T(8,128)(2,1)S(1)}, u32[]{:S(2)}, u32[]{:S(2)}) collective-permute-start(bf16[2,128,1024]{2,1,0:T(8,128)(2,1)} %get-tuple-element.27), channel_id=1, source_target_pairs={{0,2},{4,6},{8,10},{12,14},{16,18},{20,22},{24,26},{28,30},{2,0},{... | collective-permute-start | bytes 1572872 | tf_op jit(solution)/shard_map/ppermute | solution.py:498
  57.0 16.8 %collective-permute-start.1 = (bf16[2,128,1024]{2,1,0:T(8,128)(2,1)}, bf16[2,128,1024]{2,1,0:T(8,128)(2,1)S(1)}, u32[]{:S(2)}, u32[]{:S(2)}) collective-permute-start(bf16[2,128,1024]{2,1,0:T(8,128)(2,1)} %get-tuple-element.28), channel_id=1, source_target_pairs={{2,4},{6,8},{10,12},{14,16},{18,20},{22,24},{26,28},{4,2},{8,6},{1... | collective-permute-start | bytes 1572872 | tf_op jit(solution)/shard_map/ppermute | solution.py:497
  69.8 14.4 %collective-permute-start.10 = (bf16[128,2176]{1,0:T(8,128)(2,1)S(1)}, bf16[128,2176]{1,0:T(8,128)(2,1)S(1)}, u32[]{:S(2)}, u32[]{:S(2)}) collective-permute-start(bf16[128,2176]{1,0:T(8,128)(2,1)S(1)} %get-tuple-element.47), channel_id=1, source_target_pairs={{0,1},{1,0},{2,3},{3,2},{4,5},{5,4},{6,7},{7,6},{8,9},{9,8},{10,11... | collective-permute-start | bytes 1671176 | tf_op jit(solution)/shard_map/ppermute | solution.py:515
  73.8 13.0 %copy-start = (bf16[1024,1024]{1,0:T(8,128)(2,1)S(1)}, bf16[1024,1024]{1,0:T(8,128)(2,1)}, u32[]{:S(2)}) copy-start(bf16[1024,1024]{1,0:T(8,128)(2,1)} %weight_ref.1) | copy-start | bytes 6291460
  81.9 14.3 %collective-permute-start.11 = (bf16[128,2176]{1,0:T(8,128)(2,1)S(1)}, bf16[128,2176]{1,0:T(8,128)(2,1)S(1)}, u32[]{:S(2)}, u32[]{:S(2)}) collective-permute-start(bf16[128,2176]{1,0:T(8,128)(2,1)S(1)} %get-tuple-element.49), channel_id=1, source_target_pairs={{0,1},{1,0},{2,3},{3,2},{4,5},{5,4},{6,7},{7,6},{8,9},{9,8},{10,11... | collective-permute-start | bytes 1671176 | tf_op jit(solution)/shard_map/ppermute | solution.py:515
  82.3 16.5 %collective-permute-start.12 = (bf16[512,512]{1,0:T(8,128)(2,1)S(1)}, bf16[512,512]{1,0:T(8,128)(2,1)S(1)}, u32[]{:S(2)}, u32[]{:S(2)}) collective-permute-start(bf16[512,512]{1,0:T(8,128)(2,1)S(1)} %pad_maximum_fusion), channel_id=1, source_target_pairs={{2,0},{4,2},{6,4},{8,6},{10,8},{12,10},{14,12},{16,14},{18,16},{20... | collective-permute-start | bytes 1572872 | tf_op jit(solution)/shard_map/ppermute | solution.py:518
  84.3 20.8 %collective-permute-start.13 = (bf16[384,512]{1,0:T(8,128)(2,1)S(1)}, bf16[384,512]{1,0:T(8,128)(2,1)S(1)}, u32[]{:S(2)}, u32[]{:S(2)}) collective-permute-start(bf16[384,512]{1,0:T(8,128)(2,1)S(1)} %pad_maximum_fusion.1), channel_id=1, source_target_pairs={{2,0},{4,2},{6,4},{8,6},{10,8},{12,10},{14,12},{16,14},{18,16},{20... | collective-permute-start | bytes 1179656 | tf_op jit(solution)/shard_map/ppermute | solution.py:518
  96.3 14.9 %collective-permute-start.14 = (bf16[128,512]{1,0:T(8,128)(2,1)S(1)}, bf16[128,512]{1,0:T(8,128)(2,1)S(1)}, u32[]{:S(2)}, u32[]{:S(2)}) collective-permute-start(bf16[128,512]{1,0:T(8,128)(2,1)S(1)} %slice.35), channel_id=1, source_target_pairs={{2,0},{4,2},{6,4},{8,6},{10,8},{12,10},{14,12},{16,14},{18,16},{20... | collective-permute-start | bytes 393224 | tf_op jit(solution)/shard_map/ppermute | solution.py:518

commit v5 on v4

--- a/solution.py
+++ b/solution.py
@@ -12,7 +12,7 @@
 current = 4.0
 LANES = 128
 GROUP = 16
-ROWS = 32
+ROWS = 64
 UNIT = 128
 HALO = 2
 PART = 16
@@ -174,8 +174,13 @@
         first[0:HALO] = inner_ref[...]
         first[HALO + depth :] = outer_ref[...]
 
-    elec_b[0] = jnp.broadcast_to(elec_ref[:, 0:1], (rows, LANES))
-    elec_b[1] = jnp.broadcast_to(elec_ref[:, 1:2], (rows, LANES))
+
+    @pl.when(pl.program_id(0) == 0)
+    def _():
+        for e in range(2):
+            line = jnp.broadcast_to(elec_ref[e : e + 1, :].astype(jnp.float32), (LANES, UNIT))
+            elec_b[e] = line.T.astype(jnp.int32)
+
     lane = lane_index((GROUP, LANES))
     left = lane < LANES - NY
     right = lane >= NY
@@ -210,8 +215,9 @@
     def relax_first(plane, at):
         sums = stencil(first, plane + 1, plane, at)
         base = (slab * depth + plane - 1) * cells
-        plus = elec_b[0, at, :] - base
-        minus = elec_b[1, at, :] - base
+        mine = pl.ds(pl.multiple_of(pl.program_id(0) * rows + at.start, GROUP), GROUP)
+        plus = elec_b[0, mine, :] - base
+        minus = elec_b[1, mine, :] - base
 
         def tile(v):
             lanes = pl.ds(v * LANES, LANES)
@@ -296,7 +302,7 @@
         pl.BlockSpec((HALO, ROWS, cells), lambda i: (0, i, 0)),
         pl.BlockSpec((HALO, ROWS, cells), lambda i: (0, i, 0)),
         pl.BlockSpec(coefs.shape, lambda i: (0, 0, 0)),
-        pl.BlockSpec((ROWS, 2), lambda i: (i + block, 0)),
+        pl.BlockSpec((2, UNIT), lambda i: (0, begin // UNIT)),
     ]
     args = [own, inner, outer, coefs, electrodes]
     aliases = {}
@@ -316,7 +322,7 @@
             pltpu.VMEM((planes, ROWS, cells), jnp.float32),
             pltpu.VMEM((planes, ROWS, cells), jnp.float32),
             pltpu.VMEM((depth, ROWS, cells), jnp.bfloat16),
-            pltpu.VMEM((2, ROWS, LANES), jnp.int32),
+            pltpu.VMEM((2, UNIT, LANES), jnp.int32),
         ],
         out_shape=[jax.ShapeDtypeStruct((total, depth, cells), jnp.bfloat16)]
         + [jax.ShapeDtypeStruct((size, width), jnp.bfloat16)] * count,
@@ -487,6 +493,7 @@
 
 def body(conductivity, prev_fields, electrodes, data_weight):
     local, depth, cells = prev_fields.shape
+    ends = electrodes.T
     count = lax.axis_size("src")
     band = cells // count
     sources = data_weight.shape[0]
@@ -507,7 +514,7 @@
     done = 0
     for k in range(per):
         potentials, kept, *sent = sweep(
-            *halos[k], coefs, electrodes, potentials, local, k * UNIT, count, band
+            *halos[k], coefs, ends, potentials, local, k * UNIT, count, band
         )
         pieces.append(kept)
         for r in range(1, count):

time: 114 us -> 111 us (0.974)
  Pallas kernels: 65.1 us -> 62.6 us
  local copies, waits for them, and re-layouts: 1.48 us -> 0.11 us
    pallas_call x4, Pallas kernels: 34.6 us -> 32 us  [sweep(): pl.pallas_call(functools.partial(sweep_kernel, count, band), grid=(size /...]
    unnamed x15 -> x14, local copies, waits for them, and re-layouts: 1.39 us -> 0.03 us
  transfers between devices with their start and end apart: 15 -> 15, of which waited for: 3 -> 3; matrix products, arithmetic and copies ran while one was open for 0% -> 0% of each run, Pallas kernels for 52% -> 51%
where the time goes in v5:
time: 111 us
  Pallas kernels  62.6 us (56%)
  starting transfers between devices  23.4 us (21%)
  waiting for transfers between devices  23.4 us (21%)
    pallas_call x4, Pallas kernels, sweep(): pl.pallas_call(functools.partial(sweep_kernel, count, band), grid=(size /...  32 us
    ppermute x4, waiting for transfers between devices, body(): outer = lax.ppermute(outer, 'cells', pairs_of('cells', 1))  17 us
    pallas_call x3, Pallas kernels, weigh(): pl.pallas_call(functools.partial(weigh_kernel, depth, band, len(pieces),...  14.8 us
    ppermute x4, starting transfers between devices, body(): outer = lax.ppermute(outer, 'cells', pairs_of('cells', 1))  13.6 us
    pallas_call x4, Pallas kernels, pack(): pl.pallas_call(functools.partial(pack_kernel, extra), grid=(steps,), in_s...  12.5 us
    ppermute x3, starting transfers between devices, body(): above.append(lax.ppermute(lowest, 'cells', down))  6.9 us
    ppermute x4, waiting for transfers between devices, body(): pieces.append(lax.ppermute(sent[r - 1], 'src', pairs))  6.33 us
    pallas_call x1, Pallas kernels, fold(): pl.pallas_call(functools.partial(fold_kernel, count, per), grid=(1,), in_...  3.03 us
  transfers between devices with their start and end apart: 15, of which 3 were waited for; matrix products, arithmetic and copies ran while one was open for 0% of the time, Pallas kernels for 51%

profile of v5, /device:TPU:21, one launch (start us, length us, event | category | flops | bytes accessed | tf_op | source)
XLA Modules:
  0.0 110.6 jit_solution(790904619820783912)
XLA Ops:
  0.6 3.2 %pack.5 = (bf16[4,128,1024]{2,1,0:T(8,128)(2,1)}, bf16[2,144,1024]{2,1,0:T(8,128)(2,1)}, bf16[2,144,1024]{2,1,0:T(8,128)(2,1)}) custom-call(bf16[512,4,1024]{2,1,0:T(4,128)(2,1)} %fields_ref.7, f32[4,1024]{1,0:T(4,128)} %sigma_ref.9), custom_call_target="tpu_custom_call" | custom-call | tf_op jit(solution)/shard_map/pack/pallas_call | solution.py:137
  3.8 0.7 collective-permute-start.2
  4.5 3.2 %collective-permute-start.3 = (bf16[2,144,1024]{2,1,0:T(8,128)(2,1)}, bf16[2,144,1024]{2,1,0:T(8,128)(2,1)S(1)}, u32[]{:S(2)}, u32[]{:S(2)}) collective-permute-start(bf16[2,144,1024]{2,1,0:T(8,128)(2,1)} %get-tuple-element.30), channel_id=1, source_target_pairs={{2,4},{6,8},{10,12},{14,16},{18,20},{22,24},{26,28},{4,2},{8,6},{1... | collective-permute-start | bytes 1769480 | tf_op jit(solution)/shard_map/ppermute | solution.py:504
  7.7 3.1 %pack.7 = (bf16[4,128,1024]{2,1,0:T(8,128)(2,1)}, bf16[2,128,1024]{2,1,0:T(8,128)(2,1)}, bf16[2,128,1024]{2,1,0:T(8,128)(2,1)}) custom-call(bf16[512,4,1024]{2,1,0:T(4,128)(2,1)} %fields_ref.7, f32[4,1024]{1,0:T(4,128)} %sigma_ref.9), custom_call_target="tpu_custom_call" | custom-call | tf_op jit(solution)/shard_map/pack/pallas_call | solution.py:137
  11.2 3.2 %collective-permute-start.7 = (bf16[2,128,1024]{2,1,0:T(8,128)(2,1)}, bf16[2,128,1024]{2,1,0:T(8,128)(2,1)}, u32[]{:S(2)}, u32[]{:S(2)}) collective-permute-start(bf16[2,128,1024]{2,1,0:T(8,128)(2,1)} %get-tuple-element.36), channel_id=1, source_target_pairs={{2,4},{6,8},{10,12},{14,16},{18,20},{22,24},{26,28},{4,2},{8,6},{1... | collective-permute-start | bytes 1572872 | tf_op jit(solution)/shard_map/ppermute | solution.py:504
  14.4 3.1 %pack.6 = (bf16[4,128,1024]{2,1,0:T(8,128)(2,1)}, bf16[2,128,1024]{2,1,0:T(8,128)(2,1)}, bf16[2,128,1024]{2,1,0:T(8,128)(2,1)}) custom-call(bf16[512,4,1024]{2,1,0:T(4,128)(2,1)} %fields_ref.7, f32[4,1024]{1,0:T(4,128)} %sigma_ref.9), custom_call_target="tpu_custom_call" | custom-call | tf_op jit(solution)/shard_map/pack/pallas_call | solution.py:137
  17.5 3.5 %collective-permute-start.5 = (bf16[2,128,1024]{2,1,0:T(8,128)(2,1)}, bf16[2,128,1024]{2,1,0:T(8,128)(2,1)}, u32[]{:S(2)}, u32[]{:S(2)}) collective-permute-start(bf16[2,128,1024]{2,1,0:T(8,128)(2,1)} %get-tuple-element.33), channel_id=1, source_target_pairs={{2,4},{6,8},{10,12},{14,16},{18,20},{22,24},{26,28},{4,2},{8,6},{1... | collective-permute-start | bytes 1572872 | tf_op jit(solution)/shard_map/ppermute | solution.py:504
  21.0 12.6 %collective-permute-done.3.outer_ref = bf16[2,144,1024]{2,1,0:T(8,128)(2,1)S(1)} collective-permute-done((bf16[2,144,1024]{2,1,0:T(8,128)(2,1)}, bf16[2,144,1024]{2,1,0:T(8,128)(2,1)S(1)}, u32[]{:S(2)}, u32[]{:S(2)}) %collective-permute-start.3) | collective-permute-done | bytes 589856 | tf_op jit(solution)/shard_map/ppermute | solution.py:504
  33.9 7.6 %sweep.4 = (bf16[512,4,1024]{2,1,0:T(4,128)(2,1)}, bf16[128,2176]{1,0:T(8,128)(2,1)S(1)}, bf16[128,2176]{1,0:T(8,128)(2,1)}) custom-call(bf16[4,128,1024]{2,1,0:T(8,128)(2,1)S(1)} %copy-done.1, bf16[2,144,1024]{2,1,0:T(8,128)(2,1)S(1)} %collective-permute-done.2.inner_ref, bf16[2,144,1024]{2,1,0:T(8,128)(2,1)S(1)} %collective-permute-done.3.outer_ref, ...), custom_call_target="tpu_custom_call" | custom-call | flops 31457280 | bytes 4194304 | tf_op jit(solution)/shard_map/sweep/pallas_call | solution.py:314
  41.5 8.6 %sweep.5 = (bf16[512,4,1024]{2,1,0:T(4,128)(2,1)}, bf16[128,2176]{1,0:T(8,128)(2,1)S(1)}, bf16[128,2176]{1,0:T(8,128)(2,1)}) custom-call(bf16[4,128,1024]{2,1,0:T(8,128)(2,1)S(1)} %copy-done.3, bf16[2,128,1024]{2,1,0:T(8,128)(2,1)} %collective-permute-done.6.inner_ref, ...), custom_call_target="tpu_custom_call", output_to_operand_aliasing={{0}: (5, {})} | custom-call | flops 31457280 | bytes 4194304 | tf_op jit(solution)/shard_map/sweep/pallas_call | solution.py:314
  50.3 1.2 %collective-permute-start.8 = (bf16[128,2176]{1,0:T(8,128)(2,1)}, bf16[128,2176]{1,0:T(8,128)(2,1)S(1)}, u32[]{:S(2)}, u32[]{:S(2)}) collective-permute-start(bf16[128,2176]{1,0:T(8,128)(2,1)} %get-tuple-element.43), channel_id=1, source_target_pairs={{0,1},{1,0},{2,3},{3,2},{4,5},{5,4},{6,7},{7,6},{8,9},{9,8},{10,11... | collective-permute-start | bytes 1671176 | tf_op jit(solution)/shard_map/ppermute | solution.py:522
  51.5 3.1 %pack.4 = (bf16[4,128,1024]{2,1,0:T(8,128)(2,1)}, bf16[2,128,1024]{2,1,0:T(8,128)(2,1)}, bf16[2,128,1024]{2,1,0:T(8,128)(2,1)}) custom-call(bf16[512,4,1024]{2,1,0:T(4,128)(2,1)} %fields_ref.7, f32[4,1024]{1,0:T(4,128)} %sigma_ref.9), custom_call_target="tpu_custom_call" | custom-call | tf_op jit(solution)/shard_map/pack/pallas_call | solution.py:137
  54.6 3.7 %collective-permute-start.1 = (bf16[2,128,1024]{2,1,0:T(8,128)(2,1)}, bf16[2,128,1024]{2,1,0:T(8,128)(2,1)S(1)}, u32[]{:S(2)}, u32[]{:S(2)}) collective-permute-start(bf16[2,128,1024]{2,1,0:T(8,128)(2,1)} %get-tuple-element.28), channel_id=1, source_target_pairs={{2,4},{6,8},{10,12},{14,16},{18,20},{22,24},{26,28},{4,2},{8,6},{1... | collective-permute-start | bytes 1572872 | tf_op jit(solution)/shard_map/ppermute | solution.py:504
  58.4 8.3 %sweep.6 = (bf16[512,4,1024]{2,1,0:T(4,128)(2,1)}, bf16[128,2176]{1,0:T(8,128)(2,1)S(1)}, bf16[128,2176]{1,0:T(8,128)(2,1)S(1)}) custom-call(bf16[4,128,1024]{2,1,0:T(8,128)(2,1)S(1)} %copy-done.2, bf16[2,128,1024]{2,1,0:T(8,128)(2,1)S(1)} %collective-permute-done.4.inner_ref, ...), custom_call_target="tpu_custom_call", output_to_operand_aliasing={{0}: (5, {})} | custom-call | flops 31457280 | bytes 4194304 | tf_op jit(solution)/shard_map/sweep/pallas_call | solution.py:314
  66.9 4.5 %collective-permute-done.1.outer_ref = bf16[2,128,1024]{2,1,0:T(8,128)(2,1)S(1)} collective-permute-done((bf16[2,128,1024]{2,1,0:T(8,128)(2,1)}, bf16[2,128,1024]{2,1,0:T(8,128)(2,1)S(1)}, u32[]{:S(2)}, u32[]{:S(2)}) %collective-permute-start.1) | collective-permute-done | bytes 524320 | tf_op jit(solution)/shard_map/ppermute | solution.py:504
  71.4 7.5 %sweep.7 = (bf16[512,4,1024]{2,1,0:T(4,128)(2,1)}, bf16[128,2176]{1,0:T(8,128)(2,1)S(1)}, bf16[128,2176]{1,0:T(8,128)(2,1)S(1)}) custom-call(bf16[4,128,1024]{2,1,0:T(8,128)(2,1)S(1)} %copy-done.4, bf16[2,128,1024]{2,1,0:T(8,128)(2,1)S(1)} %collective-permute-done.inner_ref, ...), custom_call_target="tpu_custom_call", output_to_operand_aliasing={{0}: (5, {})} | custom-call | flops 31457280 | bytes 4194304 | tf_op jit(solution)/shard_map/sweep/pallas_call | solution.py:314
  79.2 1.9 %collective-permute-start.12 = (bf16[512,512]{1,0:T(8,128)(2,1)S(1)}, bf16[512,512]{1,0:T(8,128)(2,1)S(1)}, u32[]{:S(2)}, u32[]{:S(2)}) collective-permute-start(bf16[512,512]{1,0:T(8,128)(2,1)S(1)} %pad_maximum_fusion), channel_id=1, source_target_pairs={{2,0},{4,2},{6,4},{8,6},{10,8},{12,10},{14,12},{16,14},{18,16},{20... | collective-permute-start | bytes 1572872 | tf_op jit(solution)/shard_map/ppermute | solution.py:525
  81.2 2.5 %collective-permute-start.13 = (bf16[384,512]{1,0:T(8,128)(2,1)S(1)}, bf16[384,512]{1,0:T(8,128)(2,1)S(1)}, u32[]{:S(2)}, u32[]{:S(2)}) collective-permute-start(bf16[384,512]{1,0:T(8,128)(2,1)S(1)} %pad_maximum_fusion.1), channel_id=1, source_target_pairs={{2,0},{4,2},{6,4},{8,6},{10,8},{12,10},{14,12},{16,14},{18,16},{20... | collective-permute-start | bytes 1179656 | tf_op jit(solution)/shard_map/ppermute | solution.py:525
  83.7 3.0 %fold.1.weight_ref = bf16[1024,1024]{1,0:T(8,128)(2,1)S(1)} custom-call(bf16[1024,1024]{1,0:T(8,128)(2,1)S(1)} %copy-done), custom_call_target="tpu_custom_call" | custom-call | flops 1048576 | bytes 4194304 | tf_op jit(solution)/shard_map/fold/pallas_call | solution.py:368
  86.8 6.3 %collective-permute-done.11.refs_7_ = bf16[128,2176]{1,0:T(8,128)(2,1)S(1)} collective-permute-done((bf16[128,2176]{1,0:T(8,128)(2,1)S(1)}, bf16[128,2176]{1,0:T(8,128)(2,1)S(1)}, u32[]{:S(2)}, u32[]{:S(2)}) %collective-permute-start.11) | collective-permute-done | bytes 557088 | tf_op jit(solution)/shard_map/ppermute | solution.py:522
  93.1 2.5 %collective-permute-start.14 = (bf16[128,512]{1,0:T(8,128)(2,1)S(1)}, bf16[128,512]{1,0:T(8,128)(2,1)S(1)}, u32[]{:S(2)}, u32[]{:S(2)}) collective-permute-start(bf16[128,512]{1,0:T(8,128)(2,1)S(1)} %slice.35), channel_id=1, source_target_pairs={{2,0},{4,2},{6,4},{8,6},{10,8},{12,10},{14,12},{16,14},{18,16},{20... | collective-permute-start | bytes 393224 | tf_op jit(solution)/shard_map/ppermute | solution.py:525
  95.6 6.3 %weigh.3.refs_9_ = f32[32,512]{1,0:T(8,128)S(1)} custom-call(bf16[1024,1024]{1,0:T(8,128)(2,1)S(1)} %fold.1.weight_ref, bf16[128,2176]{1,0:T(8,128)(2,1)S(1)} %get-tuple-element.42.refs_0_, bf16[128,2176]{1,0:T(8,128)(2,1)S(1)} %collective-permute-done.8.refs_1_, bf16[128,2176]{1,0:T(8,128)(2,1)S(1)} %get-tuple-element.44.refs_2_, ...), custom_call_target="tpu_custom_call" | custom-call | flops 1409286144 | bytes 2752512 | tf_op jit(solution)/shard_map/weigh/pallas_call | solution.py:470
  101.9 6.0 %weigh.4.refs_11_ = f32[32,512]{1,0:T(8,128)S(1)} custom-call(bf16[1024,1024]{1,0:T(8,128)(2,1)S(1)} %fold.1.weight_ref, bf16[128,2176]{1,0:T(8,128)(2,1)S(1)} %get-tuple-element.42.refs_0_, bf16[128,2176]{1,0:T(8,128)(2,1)S(1)} %collective-permute-done.8.refs_1_, bf16[128,2176]{1,0:T(8,128)(2,1)S(1)} %get-tuple-element.44.refs_2_, ...), custom_call_target="tpu_custom_call" | custom-call | flops 1849688064 | bytes 4816896 | tf_op jit(solution)/shard_map/weigh/pallas_call | solution.py:470
  108.0 2.4 %weigh.5 = f32[4,512]{1,0:T(4,128)} custom-call(bf16[1024,1024]{1,0:T(8,128)(2,1)S(1)} %fold.1.weight_ref, bf16[128,2176]{1,0:T(8,128)(2,1)S(1)} %get-tuple-element.42.refs_0_, bf16[128,2176]{1,0:T(8,128)(2,1)S(1)} %collective-permute-done.8.refs_1_, bf16[128,2176]{1,0:T(8,128)(2,1)S(1)} %get-tuple-element.44.refs_2_, ...), custom_call_target="tpu_custom_call" | custom-call | flops 704643072 | bytes 5505024 | tf_op jit(solution)/shard_map/weigh/pallas_call | solution.py:470
  (44 shorter events, 1.4 us)
Async XLA Ops:
  3.8 13.7 %collective-permute-start.2 = (bf16[2,144,1024]{2,1,0:T(8,128)(2,1)}, bf16[2,144,1024]{2,1,0:T(8,128)(2,1)S(1)}, u32[]{:S(2)}, u32[]{:S(2)}) collective-permute-start(bf16[2,144,1024]{2,1,0:T(8,128)(2,1)} %get-tuple-element.29), channel_id=1, source_target_pairs={{0,2},{4,6},{8,10},{12,14},{16,18},{20,22},{24,26},{28,30},{2,0},{... | collective-permute-start | bytes 1769480 | tf_op jit(solution)/shard_map/ppermute | solution.py:505
  4.5 29.1 %copy-start.5 = (f32[4,1024]{1,0:T(4,128)S(1)}, f32[4,1024]{1,0:T(4,128)}, u32[]{:S(2)}) copy-start(f32[4,1024]{1,0:T(4,128)} %sigma_ref.9) | copy-start | bytes 49156
  4.5 29.3 %copy-start.1 = (bf16[4,128,1024]{2,1,0:T(8,128)(2,1)S(1)}, bf16[4,128,1024]{2,1,0:T(8,128)(2,1)}, u32[]{:S(2)}) copy-start(bf16[4,128,1024]{2,1,0:T(8,128)(2,1)} %get-tuple-element.37.own_ref) | copy-start | bytes 3145732
  4.5 29.3 %copy-start.6 = (s32[512,2]{0,1:T(2,128)S(1)}, s32[512,2]{0,1:T(2,128)}, u32[]{:S(2)}) copy-start(s32[512,2]{0,1:T(2,128)} %param.6) | copy-start | bytes 12292
  4.5 29.1 %collective-permute-start.3 = (bf16[2,144,1024]{2,1,0:T(8,128)(2,1)}, bf16[2,144,1024]{2,1,0:T(8,128)(2,1)S(1)}, u32[]{:S(2)}, u32[]{:S(2)}) collective-permute-start(bf16[2,144,1024]{2,1,0:T(8,128)(2,1)} %get-tuple-element.30), channel_id=1, source_target_pairs={{2,4},{6,8},{10,12},{14,16},{18,20},{22,24},{26,28},{4,2},{8,6},{1... | collective-permute-start | bytes 1769480 | tf_op jit(solution)/shard_map/ppermute | solution.py:504
  10.8 30.7 %collective-permute-start.6 = (bf16[2,128,1024]{2,1,0:T(8,128)(2,1)}, bf16[2,128,1024]{2,1,0:T(8,128)(2,1)}, u32[]{:S(2)}, u32[]{:S(2)}) collective-permute-start(bf16[2,128,1024]{2,1,0:T(8,128)(2,1)} %get-tuple-element.35), channel_id=1, source_target_pairs={{0,2},{4,6},{8,10},{12,14},{16,18},{20,22},{24,26},{28,30},{2,0},{... | collective-permute-start | bytes 1572872 | tf_op jit(solution)/shard_map/ppermute | solution.py:505
  11.2 30.3 %collective-permute-start.7 = (bf16[2,128,1024]{2,1,0:T(8,128)(2,1)}, bf16[2,128,1024]{2,1,0:T(8,128)(2,1)}, u32[]{:S(2)}, u32[]{:S(2)}) collective-permute-start(bf16[2,128,1024]{2,1,0:T(8,128)(2,1)} %get-tuple-element.36), channel_id=1, source_target_pairs={{2,4},{6,8},{10,12},{14,16},{18,20},{22,24},{26,28},{4,2},{8,6},{1... | collective-permute-start | bytes 1572872 | tf_op jit(solution)/shard_map/ppermute | solution.py:504
  17.5 24.0 %copy-start.3 = (bf16[4,128,1024]{2,1,0:T(8,128)(2,1)S(1)}, bf16[4,128,1024]{2,1,0:T(8,128)(2,1)}, u32[]{:S(2)}) copy-start(bf16[4,128,1024]{2,1,0:T(8,128)(2,1)} %get-tuple-element.34.own_ref) | copy-start | bytes 3145732
  17.5 37.1 %collective-permute-start.4 = (bf16[2,128,1024]{2,1,0:T(8,128)(2,1)}, bf16[2,128,1024]{2,1,0:T(8,128)(2,1)S(1)}, u32[]{:S(2)}, u32[]{:S(2)}) collective-permute-start(bf16[2,128,1024]{2,1,0:T(8,128)(2,1)} %get-tuple-element.32), channel_id=1, source_target_pairs={{0,2},{4,6},{8,10},{12,14},{16,18},{20,22},{24,26},{28,30},{2,0},{... | collective-permute-start | bytes 1572872 | tf_op jit(solution)/shard_map/ppermute | solution.py:505
  17.5 40.9 %collective-permute-start.5 = (bf16[2,128,1024]{2,1,0:T(8,128)(2,1)}, bf16[2,128,1024]{2,1,0:T(8,128)(2,1)}, u32[]{:S(2)}, u32[]{:S(2)}) collective-permute-start(bf16[2,128,1024]{2,1,0:T(8,128)(2,1)} %get-tuple-element.33), channel_id=1, source_target_pairs={{2,4},{6,8},{10,12},{14,16},{18,20},{22,24},{26,28},{4,2},{8,6},{1... | collective-permute-start | bytes 1572872 | tf_op jit(solution)/shard_map/ppermute | solution.py:504
  41.5 16.9 %copy-start.2 = (bf16[4,128,1024]{2,1,0:T(8,128)(2,1)S(1)}, bf16[4,128,1024]{2,1,0:T(8,128)(2,1)}, u32[]{:S(2)}) copy-start(bf16[4,128,1024]{2,1,0:T(8,128)(2,1)} %get-tuple-element.31.own_ref) | copy-start | bytes 3145732
  50.1 29.0 %collective-permute-start.9 = (bf16[128,2176]{1,0:T(8,128)(2,1)}, bf16[128,2176]{1,0:T(8,128)(2,1)S(1)}, u32[]{:S(2)}, u32[]{:S(2)}) collective-permute-start(bf16[128,2176]{1,0:T(8,128)(2,1)} %get-tuple-element.45), channel_id=1, source_target_pairs={{0,1},{1,0},{2,3},{3,2},{4,5},{5,4},{6,7},{7,6},{8,9},{9,8},{10,11... | collective-permute-start | bytes 1671176 | tf_op jit(solution)/shard_map/ppermute | solution.py:522
  50.3 28.9 %collective-permute-start.8 = (bf16[128,2176]{1,0:T(8,128)(2,1)}, bf16[128,2176]{1,0:T(8,128)(2,1)S(1)}, u32[]{:S(2)}, u32[]{:S(2)}) collective-permute-start(bf16[128,2176]{1,0:T(8,128)(2,1)} %get-tuple-element.43), channel_id=1, source_target_pairs={{0,1},{1,0},{2,3},{3,2},{4,5},{5,4},{6,7},{7,6},{8,9},{9,8},{10,11... | collective-permute-start | bytes 1671176 | tf_op jit(solution)/shard_map/ppermute | solution.py:522
  54.6 16.8 %copy-start.4 = (bf16[4,128,1024]{2,1,0:T(8,128)(2,1)S(1)}, bf16[4,128,1024]{2,1,0:T(8,128)(2,1)}, u32[]{:S(2)}) copy-start(bf16[4,128,1024]{2,1,0:T(8,128)(2,1)} %get-tuple-element.26.own_ref) | copy-start | bytes 3145732
  54.6 12.3 %collective-permute-start = (bf16[2,128,1024]{2,1,0:T(8,128)(2,1)}, bf16[2,128,1024]{2,1,0:T(8,128)(2,1)S(1)}, u32[]{:S(2)}, u32[]{:S(2)}) collective-permute-start(bf16[2,128,1024]{2,1,0:T(8,128)(2,1)} %get-tuple-element.27), channel_id=1, source_target_pairs={{0,2},{4,6},{8,10},{12,14},{16,18},{20,22},{24,26},{28,30},{2,0},{... | collective-permute-start | bytes 1572872 | tf_op jit(solution)/shard_map/ppermute | solution.py:505
  54.6 16.8 %collective-permute-start.1 = (bf16[2,128,1024]{2,1,0:T(8,128)(2,1)}, bf16[2,128,1024]{2,1,0:T(8,128)(2,1)S(1)}, u32[]{:S(2)}, u32[]{:S(2)}) collective-permute-start(bf16[2,128,1024]{2,1,0:T(8,128)(2,1)} %get-tuple-element.28), channel_id=1, source_target_pairs={{2,4},{6,8},{10,12},{14,16},{18,20},{22,24},{26,28},{4,2},{8,6},{1... | collective-permute-start | bytes 1572872 | tf_op jit(solution)/shard_map/ppermute | solution.py:504
  66.7 14.4 %collective-permute-start.10 = (bf16[128,2176]{1,0:T(8,128)(2,1)S(1)}, bf16[128,2176]{1,0:T(8,128)(2,1)S(1)}, u32[]{:S(2)}, u32[]{:S(2)}) collective-permute-start(bf16[128,2176]{1,0:T(8,128)(2,1)S(1)} %get-tuple-element.47), channel_id=1, source_target_pairs={{0,1},{1,0},{2,3},{3,2},{4,5},{5,4},{6,7},{7,6},{8,9},{9,8},{10,11... | collective-permute-start | bytes 1671176 | tf_op jit(solution)/shard_map/ppermute | solution.py:522
  71.4 12.4 %copy-start = (bf16[1024,1024]{1,0:T(8,128)(2,1)S(1)}, bf16[1024,1024]{1,0:T(8,128)(2,1)}, u32[]{:S(2)}) copy-start(bf16[1024,1024]{1,0:T(8,128)(2,1)} %weight_ref.1) | copy-start | bytes 6291460
  78.9 14.2 %collective-permute-start.11 = (bf16[128,2176]{1,0:T(8,128)(2,1)S(1)}, bf16[128,2176]{1,0:T(8,128)(2,1)S(1)}, u32[]{:S(2)}, u32[]{:S(2)}) collective-permute-start(bf16[128,2176]{1,0:T(8,128)(2,1)S(1)} %get-tuple-element.49), channel_id=1, source_target_pairs={{0,1},{1,0},{2,3},{3,2},{4,5},{5,4},{6,7},{7,6},{8,9},{9,8},{10,11... | collective-permute-start | bytes 1671176 | tf_op jit(solution)/shard_map/ppermute | solution.py:522
  79.2 16.4 %collective-permute-start.12 = (bf16[512,512]{1,0:T(8,128)(2,1)S(1)}, bf16[512,512]{1,0:T(8,128)(2,1)S(1)}, u32[]{:S(2)}, u32[]{:S(2)}) collective-permute-start(bf16[512,512]{1,0:T(8,128)(2,1)S(1)} %pad_maximum_fusion), channel_id=1, source_target_pairs={{2,0},{4,2},{6,4},{8,6},{10,8},{12,10},{14,12},{16,14},{18,16},{20... | collective-permute-start | bytes 1572872 | tf_op jit(solution)/shard_map/ppermute | solution.py:525
  81.2 20.7 %collective-permute-start.13 = (bf16[384,512]{1,0:T(8,128)(2,1)S(1)}, bf16[384,512]{1,0:T(8,128)(2,1)S(1)}, u32[]{:S(2)}, u32[]{:S(2)}) collective-permute-start(bf16[384,512]{1,0:T(8,128)(2,1)S(1)} %pad_maximum_fusion.1), channel_id=1, source_target_pairs={{2,0},{4,2},{6,4},{8,6},{10,8},{12,10},{14,12},{16,14},{18,16},{20... | collective-permute-start | bytes 1179656 | tf_op jit(solution)/shard_map/ppermute | solution.py:525
  93.1 14.9 %collective-permute-start.14 = (bf16[128,512]{1,0:T(8,128)(2,1)S(1)}, bf16[128,512]{1,0:T(8,128)(2,1)S(1)}, u32[]{:S(2)}, u32[]{:S(2)}) collective-permute-start(bf16[128,512]{1,0:T(8,128)(2,1)S(1)} %slice.35), channel_id=1, source_target_pairs={{2,0},{4,2},{6,4},{8,6},{10,8},{12,10},{14,12},{16,14},{18,16},{20... | collective-permute-start | bytes 393224 | tf_op jit(solution)/shard_map/ppermute | solution.py:525

commit v6 on v5

--- a/solution.py
+++ b/solution.py
@@ -15,7 +15,7 @@
 ROWS = 64
 UNIT = 128
 HALO = 2
-PART = 16
+PART = 8
 
 
 def pairs_of(axis, first):
@@ -392,9 +392,11 @@
         for group, column in ((piece_refs, 0), (above_refs, wide)):
             at = 0
             for ref in group:
-                size, width = ref.shape
+                size, width = min(ref.shape[0], held.shape[0] - at), ref.shape[1]
+                if size <= 0:
+                    continue
                 into = held.at[pl.ds(at, size), pl.ds(column, width)]
-                copies.append(pltpu.make_async_copy(ref, into, sems.at[len(copies)]))
+                copies.append(pltpu.make_async_copy(ref.at[pl.ds(0, size)], into, sems.at[len(copies)]))
                 copies[-1].start()
                 at += size
         for copy in copies:
@@ -507,7 +509,8 @@
     coefs = stencil_coefficients(conductivity, *halos[0][1:], depth * lax.axis_size("cells"))
     weight = fold(data_weight, count, per)
     down = [(i + 1, i) for i in range(lax.axis_size("cells") - 1)]
-    stops = sorted({max(per - 2, 0) * count, (per - 1) * count + 1, per * count} - {0})
+    stops = sorted({max(per - 2, 0) * count, (per - 1) * count, (per - 1) * count + 1, per * count} - {0})
+    shared = {(per - 1) * count: (per - 1) * count + 1}
     potentials = None
     pieces, above = [], []
     sums = jnp.zeros((depth * 8, band), jnp.float32)
@@ -520,9 +523,13 @@
         for r in range(1, count):
             pairs = [(i, (i + r) % count) for i in range(count)]
             pieces.append(lax.ppermute(sent[r - 1], "src", pairs))
+    covered = 0
     for stop in stops:
-        lowest = jnp.concatenate([p[:, :band] for p in pieces[done:stop]], axis=0)
-        above.append(lax.ppermute(lowest, "cells", down))
+        if covered < stop:
+            end = shared.get(stop, stop)
+            lowest = jnp.concatenate([p[:, :band] for p in pieces[covered:end]], axis=0)
+            above.append(lax.ppermute(lowest, "cells", down))
+            covered = end
         sums = weigh(
             weight,
             pieces[:stop],

time: 111 us -> 110 us (level)
  the two profiles are of different devices: /device:TPU:21 before, /device:TPU:9 now
where the time goes in v6:
time: 110 us; the launch traced here: 109 us
  Pallas kernels  62.1 us (56%)
  starting transfers between devices  25 us (23%)
  waiting for transfers between devices  21.2 us (19%)
    pallas_call x4, Pallas kernels, sweep(): pl.pallas_call(functools.partial(sweep_kernel, count, band), grid=(size /...  31.9 us
    ppermute x4, waiting for transfers between devices, body(): outer = lax.ppermute(outer, 'cells', pairs_of('cells', 1))  15.3 us
    pallas_call x4, Pallas kernels, weigh(): pl.pallas_call(functools.partial(weigh_kernel, depth, band, len(pieces),...  14.4 us
    ppermute x4, starting transfers between devices, body(): outer = lax.ppermute(outer, 'cells', pairs_of('cells', 1))  13.6 us
    pallas_call x4, Pallas kernels, pack(): pl.pallas_call(functools.partial(pack_kernel, extra), grid=(steps,), in_s...  12.5 us
    ppermute x3, starting transfers between devices, body(): above.append(lax.ppermute(lowest, 'cells', down))  6.32 us
    ppermute x4, waiting for transfers between devices, body(): pieces.append(lax.ppermute(sent[r - 1], 'src', pairs))  5.84 us
    ppermute x4, starting transfers between devices, body(): pieces.append(lax.ppermute(sent[r - 1], 'src', pairs))  4 us
  transfers between devices with their start and end apart: 15, of which 3 were waited for; matrix products, arithmetic and copies ran while one was open for 0% of the time, Pallas kernels for 52%

profile of v6, /device:TPU:9, one launch (start us, length us, event | category | flops | bytes accessed | tf_op | source)
XLA Modules:
  0.0 109.5 jit_solution(7995758263311016576)
XLA Ops:
  0.6 3.2 %pack.5 = (bf16[4,128,1024]{2,1,0:T(8,128)(2,1)}, bf16[2,136,1024]{2,1,0:T(8,128)(2,1)}, bf16[2,136,1024]{2,1,0:T(8,128)(2,1)}) custom-call(bf16[512,4,1024]{2,1,0:T(4,128)(2,1)} %fields_ref.7, f32[4,1024]{1,0:T(4,128)} %sigma_ref.9), custom_call_target="tpu_custom_call" | custom-call | tf_op jit(solution)/shard_map/pack/pallas_call | solution.py:137
  4.5 3.2 %collective-permute-start.3 = (bf16[2,136,1024]{2,1,0:T(8,128)(2,1)}, bf16[2,136,1024]{2,1,0:T(8,128)(2,1)S(1)}, u32[]{:S(2)}, u32[]{:S(2)}) collective-permute-start(bf16[2,136,1024]{2,1,0:T(8,128)(2,1)} %get-tuple-element.30), channel_id=1, source_target_pairs={{2,4},{6,8},{10,12},{14,16},{18,20},{22,24},{26,28},{4,2},{8,6},{1... | collective-permute-start | bytes 1671176 | tf_op jit(solution)/shard_map/ppermute | solution.py:506
  7.7 3.1 %pack.7 = (bf16[4,128,1024]{2,1,0:T(8,128)(2,1)}, bf16[2,128,1024]{2,1,0:T(8,128)(2,1)}, bf16[2,128,1024]{2,1,0:T(8,128)(2,1)}) custom-call(bf16[512,4,1024]{2,1,0:T(4,128)(2,1)} %fields_ref.7, f32[4,1024]{1,0:T(4,128)} %sigma_ref.9), custom_call_target="tpu_custom_call" | custom-call | tf_op jit(solution)/shard_map/pack/pallas_call | solution.py:137
  11.1 3.2 %collective-permute-start.7 = (bf16[2,128,1024]{2,1,0:T(8,128)(2,1)}, bf16[2,128,1024]{2,1,0:T(8,128)(2,1)}, u32[]{:S(2)}, u32[]{:S(2)}) collective-permute-start(bf16[2,128,1024]{2,1,0:T(8,128)(2,1)} %get-tuple-element.36), channel_id=1, source_target_pairs={{2,4},{6,8},{10,12},{14,16},{18,20},{22,24},{26,28},{4,2},{8,6},{1... | collective-permute-start | bytes 1572872 | tf_op jit(solution)/shard_map/ppermute | solution.py:506
  14.3 3.1 %pack.6 = (bf16[4,128,1024]{2,1,0:T(8,128)(2,1)}, bf16[2,128,1024]{2,1,0:T(8,128)(2,1)}, bf16[2,128,1024]{2,1,0:T(8,128)(2,1)}) custom-call(bf16[512,4,1024]{2,1,0:T(4,128)(2,1)} %fields_ref.7, f32[4,1024]{1,0:T(4,128)} %sigma_ref.9), custom_call_target="tpu_custom_call" | custom-call | tf_op jit(solution)/shard_map/pack/pallas_call | solution.py:137
  17.5 3.5 %collective-permute-start.5 = (bf16[2,128,1024]{2,1,0:T(8,128)(2,1)}, bf16[2,128,1024]{2,1,0:T(8,128)(2,1)}, u32[]{:S(2)}, u32[]{:S(2)}) collective-permute-start(bf16[2,128,1024]{2,1,0:T(8,128)(2,1)} %get-tuple-element.33), channel_id=1, source_target_pairs={{2,4},{6,8},{10,12},{14,16},{18,20},{22,24},{26,28},{4,2},{8,6},{1... | collective-permute-start | bytes 1572872 | tf_op jit(solution)/shard_map/ppermute | solution.py:506
  21.0 11.9 %collective-permute-done.3.outer_ref = bf16[2,136,1024]{2,1,0:T(8,128)(2,1)S(1)} collective-permute-done((bf16[2,136,1024]{2,1,0:T(8,128)(2,1)}, bf16[2,136,1024]{2,1,0:T(8,128)(2,1)S(1)}, u32[]{:S(2)}, u32[]{:S(2)}) %collective-permute-start.3) | collective-permute-done | bytes 557088 | tf_op jit(solution)/shard_map/ppermute | solution.py:506
  33.1 7.6 %sweep.4 = (bf16[512,4,1024]{2,1,0:T(4,128)(2,1)}, bf16[128,2176]{1,0:T(8,128)(2,1)S(1)}, bf16[128,2176]{1,0:T(8,128)(2,1)}) custom-call(bf16[4,128,1024]{2,1,0:T(8,128)(2,1)S(1)} %copy-done.1, bf16[2,136,1024]{2,1,0:T(8,128)(2,1)S(1)} %collective-permute-done.2.inner_ref, bf16[2,136,1024]{2,1,0:T(8,128)(2,1)S(1)} %collective-permute-done.3.outer_ref, ...), custom_call_target="tpu_custom_call" | custom-call | flops 31457280 | bytes 4194304 | tf_op jit(solution)/shard_map/sweep/pallas_call | solution.py:314
  40.8 8.5 %sweep.5 = (bf16[512,4,1024]{2,1,0:T(4,128)(2,1)}, bf16[128,2176]{1,0:T(8,128)(2,1)S(1)}, bf16[128,2176]{1,0:T(8,128)(2,1)}) custom-call(bf16[4,128,1024]{2,1,0:T(8,128)(2,1)S(1)} %copy-done.3, bf16[2,128,1024]{2,1,0:T(8,128)(2,1)S(1)} %collective-permute-done.6.inner_ref, ...), custom_call_target="tpu_custom_call", output_to_operand_aliasing={{0}: (5, {})} | custom-call | flops 31457280 | bytes 4194304 | tf_op jit(solution)/shard_map/sweep/pallas_call | solution.py:314
  50.7 3.1 %pack.4 = (bf16[4,128,1024]{2,1,0:T(8,128)(2,1)}, bf16[2,128,1024]{2,1,0:T(8,128)(2,1)}, bf16[2,128,1024]{2,1,0:T(8,128)(2,1)}) custom-call(bf16[512,4,1024]{2,1,0:T(4,128)(2,1)} %fields_ref.7, f32[4,1024]{1,0:T(4,128)} %sigma_ref.9), custom_call_target="tpu_custom_call" | custom-call | tf_op jit(solution)/shard_map/pack/pallas_call | solution.py:137
  53.8 3.7 %collective-permute-start.1 = (bf16[2,128,1024]{2,1,0:T(8,128)(2,1)}, bf16[2,128,1024]{2,1,0:T(8,128)(2,1)S(1)}, u32[]{:S(2)}, u32[]{:S(2)}) collective-permute-start(bf16[2,128,1024]{2,1,0:T(8,128)(2,1)} %get-tuple-element.28), channel_id=1, source_target_pairs={{2,4},{6,8},{10,12},{14,16},{18,20},{22,24},{26,28},{4,2},{8,6},{1... | collective-permute-start | bytes 1572872 | tf_op jit(solution)/shard_map/ppermute | solution.py:506
  57.6 8.3 %sweep.6 = (bf16[512,4,1024]{2,1,0:T(4,128)(2,1)}, bf16[128,2176]{1,0:T(8,128)(2,1)S(1)}, bf16[128,2176]{1,0:T(8,128)(2,1)S(1)}) custom-call(bf16[4,128,1024]{2,1,0:T(8,128)(2,1)S(1)} %copy-done.2, bf16[2,128,1024]{2,1,0:T(8,128)(2,1)S(1)} %collective-permute-done.4.inner_ref, ...), custom_call_target="tpu_custom_call", output_to_operand_aliasing={{0}: (5, {})} | custom-call | flops 31457280 | bytes 4194304 | tf_op jit(solution)/shard_map/sweep/pallas_call | solution.py:314
  65.9 1.3 %collective-permute-start.10 = (bf16[128,2176]{1,0:T(8,128)(2,1)S(1)}, bf16[128,2176]{1,0:T(8,128)(2,1)S(1)}, u32[]{:S(2)}, u32[]{:S(2)}) collective-permute-start(bf16[128,2176]{1,0:T(8,128)(2,1)S(1)} %get-tuple-element.47), channel_id=1, source_target_pairs={{0,1},{1,0},{2,3},{3,2},{4,5},{5,4},{6,7},{7,6},{8,9},{9,8},{10,11... | collective-permute-start | bytes 1671176 | tf_op jit(solution)/shard_map/ppermute | solution.py:525
  67.2 3.4 %collective-permute-done.1.outer_ref = bf16[2,128,1024]{2,1,0:T(8,128)(2,1)S(1)} collective-permute-done((bf16[2,128,1024]{2,1,0:T(8,128)(2,1)}, bf16[2,128,1024]{2,1,0:T(8,128)(2,1)S(1)}, u32[]{:S(2)}, u32[]{:S(2)}) %collective-permute-start.1) | collective-permute-done | bytes 524320 | tf_op jit(solution)/shard_map/ppermute | solution.py:506
  70.6 7.5 %sweep.7 = (bf16[512,4,1024]{2,1,0:T(4,128)(2,1)}, bf16[128,2176]{1,0:T(8,128)(2,1)S(1)}, bf16[128,2176]{1,0:T(8,128)(2,1)S(1)}) custom-call(bf16[4,128,1024]{2,1,0:T(8,128)(2,1)S(1)} %copy-done.4, bf16[2,128,1024]{2,1,0:T(8,128)(2,1)S(1)} %collective-permute-done.inner_ref, ...), custom_call_target="tpu_custom_call", output_to_operand_aliasing={{0}: (5, {})} | custom-call | flops 31457280 | bytes 4194304 | tf_op jit(solution)/shard_map/sweep/pallas_call | solution.py:314
  79.5 1.9 %collective-permute-start.12 = (bf16[512,512]{1,0:T(8,128)(2,1)S(1)}, bf16[512,512]{1,0:T(8,128)(2,1)S(1)}, u32[]{:S(2)}, u32[]{:S(2)}) collective-permute-start(bf16[512,512]{1,0:T(8,128)(2,1)S(1)} %pad_maximum_fusion), channel_id=1, source_target_pairs={{2,0},{4,2},{6,4},{8,6},{10,8},{12,10},{14,12},{16,14},{18,16},{20... | collective-permute-start | bytes 1572872 | tf_op jit(solution)/shard_map/ppermute | solution.py:531
  81.5 1.9 %collective-permute-start.13 = (bf16[384,512]{1,0:T(8,128)(2,1)S(1)}, bf16[384,512]{1,0:T(8,128)(2,1)S(1)}, u32[]{:S(2)}, u32[]{:S(2)}) collective-permute-start(bf16[384,512]{1,0:T(8,128)(2,1)S(1)} %pad_maximum_fusion.1), channel_id=1, source_target_pairs={{2,0},{4,2},{6,4},{8,6},{10,8},{12,10},{14,12},{16,14},{18,16},{20... | collective-permute-start | bytes 1179656 | tf_op jit(solution)/shard_map/ppermute | solution.py:531
  83.4 3.0 %fold.1.weight_ref = bf16[1024,1024]{1,0:T(8,128)(2,1)S(1)} custom-call(bf16[1024,1024]{1,0:T(8,128)(2,1)S(1)} %copy-done), custom_call_target="tpu_custom_call" | custom-call | flops 1048576 | bytes 4194304 | tf_op jit(solution)/shard_map/fold/pallas_call | solution.py:368
  86.5 5.8 %collective-permute-done.11.refs_7_ = bf16[128,2176]{1,0:T(8,128)(2,1)S(1)} collective-permute-done((bf16[128,2176]{1,0:T(8,128)(2,1)S(1)}, bf16[128,2176]{1,0:T(8,128)(2,1)S(1)}, u32[]{:S(2)}, u32[]{:S(2)}) %collective-permute-start.11) | collective-permute-done | bytes 557088 | tf_op jit(solution)/shard_map/ppermute | solution.py:525
  92.3 2.5 %collective-permute-start.14 = (bf16[128,512]{1,0:T(8,128)(2,1)S(1)}, bf16[128,512]{1,0:T(8,128)(2,1)S(1)}, u32[]{:S(2)}, u32[]{:S(2)}) collective-permute-start(bf16[128,512]{1,0:T(8,128)(2,1)S(1)} %slice.35), channel_id=1, source_target_pairs={{2,0},{4,2},{6,4},{8,6},{10,8},{12,10},{14,12},{16,14},{18,16},{20... | collective-permute-start | bytes 393224 | tf_op jit(solution)/shard_map/ppermute | solution.py:531
  94.8 6.3 %weigh.4.refs_8_ = f32[32,512]{1,0:T(8,128)S(1)} custom-call(bf16[1024,1024]{1,0:T(8,128)(2,1)S(1)} %fold.1.weight_ref, bf16[128,2176]{1,0:T(8,128)(2,1)S(1)} %get-tuple-element.42.refs_0_, bf16[128,2176]{1,0:T(8,128)(2,1)S(1)} %collective-permute-done.8.refs_1_, bf16[128,2176]{1,0:T(8,128)(2,1)S(1)} %get-tuple-element.44.refs_2_, ...), custom_call_target="tpu_custom_call" | custom-call | flops 1409286144 | bytes 2752512 | tf_op jit(solution)/shard_map/weigh/pallas_call | solution.py:472
  101.1 4.0 %weigh.5.refs_9_ = f32[32,512]{1,0:T(8,128)S(1)} custom-call(bf16[1024,1024]{1,0:T(8,128)(2,1)S(1)} %fold.1.weight_ref, bf16[128,2176]{1,0:T(8,128)(2,1)S(1)} %get-tuple-element.42.refs_0_, bf16[128,2176]{1,0:T(8,128)(2,1)S(1)} %collective-permute-done.8.refs_1_, bf16[128,2176]{1,0:T(8,128)(2,1)S(1)} %get-tuple-element.44.refs_2_, ...), custom_call_target="tpu_custom_call" | custom-call | flops 1056964608 | bytes 4128768 | tf_op jit(solution)/shard_map/weigh/pallas_call | solution.py:472
  105.1 1.7 %weigh.6.refs_11_ = f32[32,512]{1,0:T(8,128)S(1)} custom-call(bf16[1024,1024]{1,0:T(8,128)(2,1)S(1)} %fold.1.weight_ref, bf16[128,2176]{1,0:T(8,128)(2,1)S(1)} %get-tuple-element.42.refs_0_, bf16[128,2176]{1,0:T(8,128)(2,1)S(1)} %collective-permute-done.8.refs_1_, bf16[128,2176]{1,0:T(8,128)(2,1)S(1)} %get-tuple-element.44.refs_2_, ...), custom_call_target="tpu_custom_call" | custom-call | flops 616562688 | bytes 4816896 | tf_op jit(solution)/shard_map/weigh/pallas_call | solution.py:472
  106.9 2.4 %weigh.7 = f32[4,512]{1,0:T(4,128)} custom-call(bf16[1024,1024]{1,0:T(8,128)(2,1)S(1)} %fold.1.weight_ref, bf16[128,2176]{1,0:T(8,128)(2,1)S(1)} %get-tuple-element.42.refs_0_, bf16[128,2176]{1,0:T(8,128)(2,1)S(1)} %collective-permute-done.8.refs_1_, bf16[128,2176]{1,0:T(8,128)(2,1)S(1)} %get-tuple-element.44.refs_2_, ...), custom_call_target="tpu_custom_call" | custom-call | flops 704643072 | bytes 5505024 | tf_op jit(solution)/shard_map/weigh/pallas_call | solution.py:472
  (45 shorter events, 4.2 us)
Async XLA Ops:
  3.8 13.6 %collective-permute-start.2 = (bf16[2,136,1024]{2,1,0:T(8,128)(2,1)}, bf16[2,136,1024]{2,1,0:T(8,128)(2,1)S(1)}, u32[]{:S(2)}, u32[]{:S(2)}) collective-permute-start(bf16[2,136,1024]{2,1,0:T(8,128)(2,1)} %get-tuple-element.29), channel_id=1, source_target_pairs={{0,2},{4,6},{8,10},{12,14},{16,18},{20,22},{24,26},{28,30},{2,0},{... | collective-permute-start | bytes 1671176 | tf_op jit(solution)/shard_map/ppermute | solution.py:507
  4.5 28.4 %copy-start.5 = (f32[4,1024]{1,0:T(4,128)S(1)}, f32[4,1024]{1,0:T(4,128)}, u32[]{:S(2)}) copy-start(f32[4,1024]{1,0:T(4,128)} %sigma_ref.9) | copy-start | bytes 49156
  4.5 28.6 %copy-start.1 = (bf16[4,128,1024]{2,1,0:T(8,128)(2,1)S(1)}, bf16[4,128,1024]{2,1,0:T(8,128)(2,1)}, u32[]{:S(2)}) copy-start(bf16[4,128,1024]{2,1,0:T(8,128)(2,1)} %get-tuple-element.37.own_ref) | copy-start | bytes 3145732
  4.5 28.6 %copy-start.6 = (s32[512,2]{0,1:T(2,128)S(1)}, s32[512,2]{0,1:T(2,128)}, u32[]{:S(2)}) copy-start(s32[512,2]{0,1:T(2,128)} %param.6) | copy-start | bytes 12292
  4.5 28.4 %collective-permute-start.3 = (bf16[2,136,1024]{2,1,0:T(8,128)(2,1)}, bf16[2,136,1024]{2,1,0:T(8,128)(2,1)S(1)}, u32[]{:S(2)}, u32[]{:S(2)}) collective-permute-start(bf16[2,136,1024]{2,1,0:T(8,128)(2,1)} %get-tuple-element.30), channel_id=1, source_target_pairs={{2,4},{6,8},{10,12},{14,16},{18,20},{22,24},{26,28},{4,2},{8,6},{1... | collective-permute-start | bytes 1671176 | tf_op jit(solution)/shard_map/ppermute | solution.py:506
  10.7 30.0 %collective-permute-start.6 = (bf16[2,128,1024]{2,1,0:T(8,128)(2,1)}, bf16[2,128,1024]{2,1,0:T(8,128)(2,1)S(1)}, u32[]{:S(2)}, u32[]{:S(2)}) collective-permute-start(bf16[2,128,1024]{2,1,0:T(8,128)(2,1)} %get-tuple-element.35), channel_id=1, source_target_pairs={{0,2},{4,6},{8,10},{12,14},{16,18},{20,22},{24,26},{28,30},{2,0},{... | collective-permute-start | bytes 1572872 | tf_op jit(solution)/shard_map/ppermute | solution.py:507
  11.1 29.7 %collective-permute-start.7 = (bf16[2,128,1024]{2,1,0:T(8,128)(2,1)}, bf16[2,128,1024]{2,1,0:T(8,128)(2,1)}, u32[]{:S(2)}, u32[]{:S(2)}) collective-permute-start(bf16[2,128,1024]{2,1,0:T(8,128)(2,1)} %get-tuple-element.36), channel_id=1, source_target_pairs={{2,4},{6,8},{10,12},{14,16},{18,20},{22,24},{26,28},{4,2},{8,6},{1... | collective-permute-start | bytes 1572872 | tf_op jit(solution)/shard_map/ppermute | solution.py:506
  17.4 23.3 %copy-start.3 = (bf16[4,128,1024]{2,1,0:T(8,128)(2,1)S(1)}, bf16[4,128,1024]{2,1,0:T(8,128)(2,1)}, u32[]{:S(2)}) copy-start(bf16[4,128,1024]{2,1,0:T(8,128)(2,1)} %get-tuple-element.34.own_ref) | copy-start | bytes 3145732
  17.4 36.4 %collective-permute-start.4 = (bf16[2,128,1024]{2,1,0:T(8,128)(2,1)}, bf16[2,128,1024]{2,1,0:T(8,128)(2,1)S(1)}, u32[]{:S(2)}, u32[]{:S(2)}) collective-permute-start(bf16[2,128,1024]{2,1,0:T(8,128)(2,1)} %get-tuple-element.32), channel_id=1, source_target_pairs={{0,2},{4,6},{8,10},{12,14},{16,18},{20,22},{24,26},{28,30},{2,0},{... | collective-permute-start | bytes 1572872 | tf_op jit(solution)/shard_map/ppermute | solution.py:507
  17.5 40.1 %collective-permute-start.5 = (bf16[2,128,1024]{2,1,0:T(8,128)(2,1)}, bf16[2,128,1024]{2,1,0:T(8,128)(2,1)}, u32[]{:S(2)}, u32[]{:S(2)}) collective-permute-start(bf16[2,128,1024]{2,1,0:T(8,128)(2,1)} %get-tuple-element.33), channel_id=1, source_target_pairs={{2,4},{6,8},{10,12},{14,16},{18,20},{22,24},{26,28},{4,2},{8,6},{1... | collective-permute-start | bytes 1572872 | tf_op jit(solution)/shard_map/ppermute | solution.py:506
  40.8 16.8 %copy-start.2 = (bf16[4,128,1024]{2,1,0:T(8,128)(2,1)S(1)}, bf16[4,128,1024]{2,1,0:T(8,128)(2,1)}, u32[]{:S(2)}) copy-start(bf16[4,128,1024]{2,1,0:T(8,128)(2,1)} %get-tuple-element.31.own_ref) | copy-start | bytes 3145732
  49.3 30.1 %collective-permute-start.9 = (bf16[128,2176]{1,0:T(8,128)(2,1)}, bf16[128,2176]{1,0:T(8,128)(2,1)S(1)}, u32[]{:S(2)}, u32[]{:S(2)}) collective-permute-start(bf16[128,2176]{1,0:T(8,128)(2,1)} %get-tuple-element.45), channel_id=1, source_target_pairs={{0,1},{1,0},{2,3},{3,2},{4,5},{5,4},{6,7},{7,6},{8,9},{9,8},{10,11... | collective-permute-start | bytes 1671176 | tf_op jit(solution)/shard_map/ppermute | solution.py:525
  50.5 28.9 %collective-permute-start.8 = (bf16[128,2176]{1,0:T(8,128)(2,1)}, bf16[128,2176]{1,0:T(8,128)(2,1)S(1)}, u32[]{:S(2)}, u32[]{:S(2)}) collective-permute-start(bf16[128,2176]{1,0:T(8,128)(2,1)} %get-tuple-element.43), channel_id=1, source_target_pairs={{0,1},{1,0},{2,3},{3,2},{4,5},{5,4},{6,7},{7,6},{8,9},{9,8},{10,11... | collective-permute-start | bytes 1671176 | tf_op jit(solution)/shard_map/ppermute | solution.py:525
  53.8 16.8 %copy-start.4 = (bf16[4,128,1024]{2,1,0:T(8,128)(2,1)S(1)}, bf16[4,128,1024]{2,1,0:T(8,128)(2,1)}, u32[]{:S(2)}) copy-start(bf16[4,128,1024]{2,1,0:T(8,128)(2,1)} %get-tuple-element.26.own_ref) | copy-start | bytes 3145732
  53.8 13.4 %collective-permute-start = (bf16[2,128,1024]{2,1,0:T(8,128)(2,1)}, bf16[2,128,1024]{2,1,0:T(8,128)(2,1)S(1)}, u32[]{:S(2)}, u32[]{:S(2)}) collective-permute-start(bf16[2,128,1024]{2,1,0:T(8,128)(2,1)} %get-tuple-element.27), channel_id=1, source_target_pairs={{0,2},{4,6},{8,10},{12,14},{16,18},{20,22},{24,26},{28,30},{2,0},{... | collective-permute-start | bytes 1572872 | tf_op jit(solution)/shard_map/ppermute | solution.py:507
  53.8 16.8 %collective-permute-start.1 = (bf16[2,128,1024]{2,1,0:T(8,128)(2,1)}, bf16[2,128,1024]{2,1,0:T(8,128)(2,1)S(1)}, u32[]{:S(2)}, u32[]{:S(2)}) collective-permute-start(bf16[2,128,1024]{2,1,0:T(8,128)(2,1)} %get-tuple-element.28), channel_id=1, source_target_pairs={{2,4},{6,8},{10,12},{14,16},{18,20},{22,24},{26,28},{4,2},{8,6},{1... | collective-permute-start | bytes 1572872 | tf_op jit(solution)/shard_map/ppermute | solution.py:506
  65.9 15.5 %collective-permute-start.10 = (bf16[128,2176]{1,0:T(8,128)(2,1)S(1)}, bf16[128,2176]{1,0:T(8,128)(2,1)S(1)}, u32[]{:S(2)}, u32[]{:S(2)}) collective-permute-start(bf16[128,2176]{1,0:T(8,128)(2,1)S(1)} %get-tuple-element.47), channel_id=1, source_target_pairs={{0,1},{1,0},{2,3},{3,2},{4,5},{5,4},{6,7},{7,6},{8,9},{9,8},{10,11... | collective-permute-start | bytes 1671176 | tf_op jit(solution)/shard_map/ppermute | solution.py:525
  70.6 12.8 %copy-start = (bf16[1024,1024]{1,0:T(8,128)(2,1)S(1)}, bf16[1024,1024]{1,0:T(8,128)(2,1)}, u32[]{:S(2)}) copy-start(bf16[1024,1024]{1,0:T(8,128)(2,1)} %weight_ref.1) | copy-start | bytes 6291460
  78.1 14.2 %collective-permute-start.11 = (bf16[128,2176]{1,0:T(8,128)(2,1)S(1)}, bf16[128,2176]{1,0:T(8,128)(2,1)S(1)}, u32[]{:S(2)}, u32[]{:S(2)}) collective-permute-start(bf16[128,2176]{1,0:T(8,128)(2,1)S(1)} %get-tuple-element.49), channel_id=1, source_target_pairs={{0,1},{1,0},{2,3},{3,2},{4,5},{5,4},{6,7},{7,6},{8,9},{9,8},{10,11... | collective-permute-start | bytes 1671176 | tf_op jit(solution)/shard_map/ppermute | solution.py:525
  79.5 15.3 %collective-permute-start.12 = (bf16[512,512]{1,0:T(8,128)(2,1)S(1)}, bf16[512,512]{1,0:T(8,128)(2,1)S(1)}, u32[]{:S(2)}, u32[]{:S(2)}) collective-permute-start(bf16[512,512]{1,0:T(8,128)(2,1)S(1)} %pad_maximum_fusion), channel_id=1, source_target_pairs={{2,0},{4,2},{6,4},{8,6},{10,8},{12,10},{14,12},{16,14},{18,16},{20... | collective-permute-start | bytes 1572872 | tf_op jit(solution)/shard_map/ppermute | solution.py:531
  81.5 19.6 %collective-permute-start.13 = (bf16[384,512]{1,0:T(8,128)(2,1)S(1)}, bf16[384,512]{1,0:T(8,128)(2,1)S(1)}, u32[]{:S(2)}, u32[]{:S(2)}) collective-permute-start(bf16[384,512]{1,0:T(8,128)(2,1)S(1)} %pad_maximum_fusion.1), channel_id=1, source_target_pairs={{2,0},{4,2},{6,4},{8,6},{10,8},{12,10},{14,12},{16,14},{18,16},{20... | collective-permute-start | bytes 1179656 | tf_op jit(solution)/shard_map/ppermute | solution.py:531
  92.3 14.6 %collective-permute-start.14 = (bf16[128,512]{1,0:T(8,128)(2,1)S(1)}, bf16[128,512]{1,0:T(8,128)(2,1)S(1)}, u32[]{:S(2)}, u32[]{:S(2)}) collective-permute-start(bf16[128,512]{1,0:T(8,128)(2,1)S(1)} %slice.35), channel_id=1, source_target_pairs={{2,0},{4,2},{6,4},{8,6},{10,8},{12,10},{14,12},{16,14},{18,16},{20... | collective-permute-start | bytes 393224 | tf_op jit(solution)/shard_map/ppermute | solution.py:531
